TPU v7x, 32 devices: a whole 2x2x4 slice. The times are simulated.
32 devices in a mesh: view: 4 (over y, x), tile: 8 (over z, core).
Axes of the slice: x: 2, y: 2, z: 4, core: 2. Of those that a mesh axis runs over, the one named last changes fastest.
Arguments:
- object_band: float32 [8, 2, 512, 128], P('view', None, 'tile'), may hold values from -6 to 6
- dual_band: float32 [8, 2, 512, 128], P('view', None, 'tile'), may hold values from -6 to 6
- probe_field: float32 [2, 128, 128], replicated, may hold values from -6 to 6
- positions: int32 [8, 256], P('view', 'tile'), may hold values from 0 to 63
- live_counts: int32 [8, 8], P('view', 'tile'), may hold values from 1 to 32, 85 in all within a row
- photon_counts: int32 [8, 256, 128, 128], P('view', 'tile'), may hold values from 0 to 1023
- footprints: int32 [8, 8], P('view', 'tile'), may hold values from 0 to 6
- weights: bfloat16 [8, 128, 65536], P('view', None, 'tile'), may hold values from -0.046875 to 0.046875
- volume: float32 [2, 512, 128, 128], P(None, 'tile'), may hold values from -6 to 6
Outputs:
- object_new: float32 [8, 2, 512, 128], P('view', None, 'tile')
- dual_new: float32 [8, 2, 512, 128], P('view', None, 'tile')
- volume_new: float32 [2, 512, 128, 128], P(None, 'tile')
Inputs may be any that keep to these rules, and one draw needn't show every extreme that they name: `positions`: offset of a slot's scan position from the first column of the tile that owns the slot. `live_counts`: the first that many of a tile's 32 slots are live; each view has exactly 85 live slots, and in each view some tile has all 32 live. `footprints`: first of the 2 consecutive detector tiles that a volume tile's shadow covers in a view.
All inputs are finite; a program needn't handle non-finite values. No bound on the sum of `live_counts` on one device may be relied on, other than what follows from the above.
Results may differ from a plain program's by a relative error of at most 0.006.
Values may be sent and summed in bfloat16 or wider, within the bound.
No kernel may reach another device: no remote copies, remote signals or barrier semaphores. Data moves between devices by JAX's collectives and lax.ppermute only.
A program may use at most 128 MiB of HBM per device.

v0:
```python
import jax
import jax.numpy as jnp
from jax import lax
from jax.sharding import PartitionSpec as P

rho_weight = 0.5
step_size = 0.5
prior_weight = 0.5
floor_term = 0.25


def passed_along(value, axis, steps):
    count = lax.axis_size(axis)
    initial, last = (max(0, -steps), min(count, count - steps))
    return lax.ppermute(value, axis, [(source, source + steps) for source in range(initial, last)])


def extended(array, sides, width):
    for axis, dim in sides:
        devices, length = (lax.axis_size(axis), array.shape[dim])
        up = [(i, (i + 1) % devices) for i in range(devices - 1)]
        down = [(j, i) for i, j in up]
        last = lax.slice_in_dim(array, length - width, length, axis=dim)
        initial = lax.slice_in_dim(array, 0, width, axis=dim)
        before = lax.ppermute(last, axis, up)
        after = lax.ppermute(initial, axis, down)
        array = jnp.concatenate([before, array, after], axis=dim)
    return array


def tables(order_n):
    counter = jnp.arange(order_n, dtype=jnp.int32)
    phase_index = counter[:, None] * counter[None, :] % order_n
    angles = phase_index.astype(jnp.float32) * (2.0 * jnp.pi / order_n)
    scaling = 1.0 / jnp.sqrt(jnp.float32(order_n))
    return (jnp.cos(angles) * scaling, -jnp.sin(angles) * scaling)


def block_minus(parts):
    upper_half = jnp.concatenate([parts[0], -parts[1]], axis=1)
    lower_half = jnp.concatenate([parts[1], parts[0]], axis=1)
    return jnp.concatenate([upper_half, lower_half], axis=0).astype(jnp.bfloat16)


def block_plus(parts):
    upper_half = jnp.concatenate([parts[0], parts[1]], axis=1)
    lower_half = jnp.concatenate([-parts[1], parts[0]], axis=1)
    return jnp.concatenate([upper_half, lower_half], axis=0).astype(jnp.bfloat16)


def markov(padded):
    centre = padded[:, 1:-1, 1:-1, 1:-1]
    summed = jnp.zeros_like(centre)
    neighbours = (
        padded[:, 2:, 1:-1, 1:-1],
        padded[:, :-2, 1:-1, 1:-1],
        padded[:, 1:-1, 2:, 1:-1],
        padded[:, 1:-1, :-2, 1:-1],
        padded[:, 1:-1, 1:-1, 2:],
        padded[:, 1:-1, 1:-1, :-2],
    )
    for neighbour in neighbours:
        difference = centre - neighbour
        summed = summed + difference / jnp.sqrt(1.0 + difference * difference)
    return summed


def batch_update(windows, probe_field, counts_grid, dft_blocks):
    left_a, right_b, right_a, left_b = dft_blocks
    probe_re = probe_field[0]
    probe_im = probe_field[1]
    obj_re = windows[:, 0]
    obj_im = windows[:, 1]
    exit_wave = jnp.stack(
        [probe_re * obj_re - probe_im * obj_im, probe_re * obj_im + probe_im * obj_re], axis=1
    ).astype(jnp.bfloat16)
    num_slots = exit_wave.shape[0]
    num_cols = exit_wave.shape[2]
    num_rows = exit_wave.shape[3]
    columns_done = jnp.einsum(
        "ab,sbh->sah",
        left_a,
        exit_wave.reshape(num_slots, 2 * num_cols, num_rows),
        preferred_element_type=jnp.float32,
    ).astype(jnp.bfloat16)
    columns_done = (
        columns_done.reshape(num_slots, 2, num_cols, num_rows)
        .transpose(0, 2, 1, 3)
        .reshape(num_slots, num_cols, 2 * num_rows)
    )
    spectrum = jnp.einsum("sph,hq->spq", columns_done, right_b, preferred_element_type=jnp.float32)
    amplitude = jnp.sqrt(counts_grid.astype(jnp.float32)) / 16.0
    spec_re = spectrum[:, :, :num_rows]
    spec_im = spectrum[:, :, num_rows:]
    factor = amplitude / jnp.sqrt(spec_re * spec_re + spec_im * spec_im + floor_term)
    replaced = (spectrum * jnp.concatenate([factor, factor], axis=2)).astype(jnp.bfloat16)
    inverse_rows = jnp.einsum(
        "spq,qh->sph", replaced, right_a, preferred_element_type=jnp.float32
    ).astype(jnp.bfloat16)
    inverse_rows = (
        inverse_rows.reshape(num_slots, num_cols, 2, num_rows)
        .transpose(0, 2, 1, 3)
        .reshape(num_slots, 2 * num_cols, num_rows)
    )
    new_wave = jnp.einsum(
        "ab,sbh->sah", left_b, inverse_rows, preferred_element_type=jnp.float32
    ).reshape(num_slots, 2, num_cols, num_rows)
    difference = new_wave - exit_wave.astype(jnp.float32)
    diff_re = difference[:, 0]
    diff_im = difference[:, 1]
    power = jnp.broadcast_to(probe_re * probe_re + probe_im * probe_im, diff_re.shape)
    return jnp.stack(
        [probe_re * diff_re + probe_im * diff_im, probe_re * diff_im - probe_im * diff_re, power],
        axis=2,
    )


def place_windows(shadows, footprints, tile_cols, band_cols):
    placed = []
    for view_index in range(shadows.shape[0]):
        blank = jnp.zeros((shadows.shape[1], band_cols, shadows.shape[3]), jnp.float32)
        first_col = footprints[view_index, 0] * tile_cols
        placed.append(lax.dynamic_update_slice_in_dim(blank, shadows[view_index], first_col, 1))
    return jnp.stack(placed)


def cut_windows(full_band, footprints, tile_cols, foot_cols):
    pieces = []
    for view_index in range(full_band.shape[0]):
        first_col = footprints[view_index, 0] * tile_cols
        pieces.append(lax.dynamic_slice_in_dim(full_band[view_index], first_col, foot_cols, 1))
    return jnp.stack(pieces)


def per_device(
    object_band,
    dual_band,
    probe_field,
    positions,
    live_counts,
    photon_counts,
    footprints,
    weights,
    volume,
):
    views_here = object_band.shape[0]
    tile_cols = object_band.shape[2]
    band_rows = object_band.shape[3]
    patch_cols = probe_field.shape[1]
    slots_here = positions.shape[1]
    band_cols = tile_cols * lax.axis_size("tile")
    foot_cols = weights.shape[1]
    voxels_here = weights.shape[2]
    depth_rows = volume.shape[2]
    dft_blocks = (
        block_minus(tables(patch_cols)),
        block_plus(tables(band_rows)),
        block_minus(tables(band_rows)),
        block_plus(tables(patch_cols)),
    )
    volume_low = volume.astype(jnp.bfloat16).reshape(2, voxels_here, band_rows)
    shadows = jnp.einsum("acx,kxh->akch", weights, volume_low, preferred_element_type=jnp.float32)
    placed = place_windows(shadows, footprints, tile_cols, band_cols)
    projection = lax.psum_scatter(placed, "tile", scatter_dimension=2, tiled=True)
    ahead_one = passed_along(object_band, "tile", -1)
    ahead_two = passed_along(object_band, "tile", -2)
    reach = jnp.concatenate([object_band, ahead_one, ahead_two], axis=2)
    slot_rank = jnp.arange(slots_here, dtype=jnp.int32)
    patch_rank = jnp.arange(patch_cols, dtype=jnp.int32)
    reach_rank = jnp.arange(3 * tile_cols, dtype=jnp.int32)
    updates = []
    for view_index in range(views_here):
        view_reach = reach[view_index]
        offsets = positions[view_index]
        windows = jax.vmap(
            lambda offset_col: lax.dynamic_slice_in_dim(view_reach, offset_col, patch_cols, 1)
        )(offsets)
        contrib = batch_update(windows, probe_field, photon_counts[view_index], dft_blocks)
        is_live = (slot_rank < live_counts[view_index, 0]).astype(jnp.float32)
        target_col = offsets[:, None] + patch_rank[None, :]
        placement = (target_col[:, :, None] == reach_rank[None, None, :]).astype(
            jnp.float32
        ) * is_live[:, None, None]
        placement = placement.reshape(slots_here * patch_cols, 3 * tile_cols)
        flat = contrib.reshape(slots_here * patch_cols, 3 * band_rows)
        gathered_cols = jnp.dot(
            placement.T, flat, precision=lax.Precision.HIGHEST, preferred_element_type=jnp.float32
        )
        updates.append(gathered_cols.reshape(3 * tile_cols, 3, band_rows).transpose(1, 0, 2))
    local_updates = jnp.stack(updates)
    own_part = local_updates[:, :, :tile_cols]
    from_one = passed_along(
        local_updates[:, :, tile_cols : 2 * tile_cols].astype(jnp.bfloat16), "tile", 1
    ).astype(jnp.float32)
    from_two = passed_along(
        local_updates[:, :, 2 * tile_cols :].astype(jnp.bfloat16), "tile", 2
    ).astype(jnp.float32)
    summed_update = own_part + from_one + from_two
    object_new = (
        object_band
        + summed_update[:, 0:2] / (1.0 + summed_update[:, 2:3])
        - rho_weight * (object_band - projection - dual_band)
    )
    dual_new = dual_band + projection - object_new
    residual = (projection - object_new + dual_band).astype(jnp.bfloat16)
    residual_full = lax.all_gather(residual, "tile", axis=2, tiled=True)
    residual_windows = cut_windows(residual_full, footprints, tile_cols, foot_cols)
    grad_part = jnp.einsum(
        "acx,akch->kxh", weights, residual_windows, preferred_element_type=jnp.float32
    ).reshape(2, tile_cols, depth_rows, band_rows)
    gradient = lax.psum(grad_part, "view")
    half_step = volume - step_size * gradient
    padded = extended(half_step, (("tile", 1),), 1)
    padded = jnp.pad(padded, ((0, 0), (0, 0), (1, 1), (1, 1)))
    volume_new = half_step - step_size * prior_weight * markov(padded)
    return (object_new, dual_new, volume_new)


def solution(mesh):
    return jax.shard_map(
        per_device,
        mesh=mesh,
        in_specs=(
            P("view", None, "tile", None),
            P("view", None, "tile", None),
            P(),
            P("view", "tile"),
            P("view", "tile"),
            P("view", "tile", None, None),
            P("view", "tile"),
            P("view", None, "tile"),
            P(None, "tile", None, None),
        ),
        out_specs=(
            P("view", None, "tile", None),
            P("view", None, "tile", None),
            P(None, "tile", None, None),
        ),
        check_vma=False,
    )
```

profile of v0, /device:TPU:1, one launch (start us, length us, event | category | flops | bytes accessed | tf_op | source)
XLA Modules:
  0.0 534.7 jit_solution(6786026787238977698)
XLA Ops:
  7.2 1.0 fusion.98
  8.3 1.9 collective-permute-start
  10.2 1.3 collective-permute-start.1
  11.5 1.3 fusion.100
  14.1 6.4 %convert_element_type.129 = bf16[2,64,128,128]{3,2,1,0:T(8,128)(2,1)} convert(f32[2,64,128,128]{3,2,1,0:T(8,128)} %param.17) | non-fusion elementwise | flops 2097152 | bytes 12582912 | tf_op jit(solution)/shard_map/convert_element_type | solution.py:161
  20.5 4.7 fusion.47
  25.4 1.1 pad_maximum_fusion.4
  27.4 0.6 compare_convert_fusion
  28.0 0.7 compare_convert_fusion.1
  29.6 6.9 %gather_fusion.1 = f32[32,2,128,128]{3,1,2,0:T(2,128)} fusion(f32[2,192,128]{2,0,1:T(2,128)S(1)} %get-tuple-element.23, s32[32]{0:T(128)S(1)} %get-tuple-element.36), kind=kCustom, calls=%fused_computation.1 | custom fusion | bytes 8388992 | tf_op jit(solution)/shard_map/vmap()/gather | solution.py:176
  36.5 9.9 %fusion.94 = (f32[32,1,128,128]{3,1,2,0:T(1,128)}, f32[32,1,128,128]{3,1,2,0:T(1,128)}) fusion(f32[32,2,128,128]{3,1,2,0:T(2,128)} %gather_fusion.1), kind=kLoop, calls=%fused_computation.162 | loop fusion | bytes 8388608 | tf_op jit(solution)/shard_map/slice | solution.py:73
  46.4 7.3 %gather_fusion = f32[32,2,128,128]{3,1,2,0:T(2,128)} fusion(f32[2,192,128]{2,0,1:T(2,128)S(1)} %get-tuple-element.24, s32[32]{0:T(128)S(1)} %get-tuple-element.37), kind=kCustom, calls=%fused_computation | custom fusion | bytes 8388992 | tf_op jit(solution)/shard_map/vmap()/gather | solution.py:176
  53.7 7.8 %fusion.95 = (f32[32,1,128,128]{3,1,2,0:T(1,128)S(1)}, f32[32,1,128,128]{3,1,2,0:T(1,128)S(1)}) fusion(f32[32,2,128,128]{3,1,2,0:T(2,128)} %gather_fusion), kind=kLoop, calls=%fused_computation.163 | loop fusion | bytes 8388608 | tf_op jit(solution)/shard_map/slice | solution.py:73
  61.5 1.4 fusion.28
  64.1 1.1 multiply_subtract_fusion.3
  65.7 2.1 convert_bitcast_fusion
  67.8 4.0 reshape.292
  71.7 8.0 %copy.103 = bf16[32,128,2,128]{3,2,1,0:T(2,128)(2,1)} copy(bf16[32,128,2,128]{1,2,3,0:T(2,128)(2,1)} %bitcast.198) | data formatting | bytes 4194304 | tf_op jit(solution)/shard_map/transpose | solution.py:88
  79.7 4.4 reshape.293
  84.1 4.4 fusion.83
  88.7 2.1 convert_bitcast_fusion.1
  90.8 4.0 reshape.286
  94.8 8.0 %copy.94 = bf16[32,128,2,128]{3,2,1,0:T(2,128)(2,1)} copy(bf16[32,128,2,128]{1,2,3,0:T(2,128)(2,1)} %bitcast.199) | data formatting | bytes 4194304 | tf_op jit(solution)/shard_map/transpose | solution.py:88
  102.8 4.4 reshape.287
  107.2 2.4 fusion.86
  110.0 3.9 fusion.23
  113.8 2.1 fusion.29
  115.9 2.0 fusion.32
  118.0 4.0 reshape.294
  121.9 8.0 %copy.104 = bf16[32,2,128,128]{2,1,3,0:T(2,128)(2,1)} copy(bf16[32,2,128,128]{3,1,2,0:T(2,128)(2,1)} %bitcast.200) | data formatting | bytes 4194304 | tf_op jit(solution)/shard_map/transpose | solution.py:102
  129.9 4.4 reshape.295
  134.4 4.0 reshape.288
  138.3 8.0 %copy.95 = bf16[32,2,128,128]{2,1,3,0:T(2,128)(2,1)} copy(bf16[32,2,128,128]{3,1,2,0:T(2,128)(2,1)} %bitcast.201) | data formatting | bytes 4194304 | tf_op jit(solution)/shard_map/transpose | solution.py:102
  146.4 4.4 reshape.289
  150.7 4.3 convolution_bitcast_fusion.2
  155.1 5.7 %copy.96 = f32[32,256,128]{2,1,0:T(8,128)} copy(f32[32,256,128]{1,2,0:T(8,128)} %convolution_bitcast_fusion.2) | data formatting | bytes 8388608 | tf_op jit(solution)/shard_map/ab,sbh->sah/transpose | solution.py:105
  160.8 5.5 %convert_subtract_fusion = f32[32,2,128,128]{3,2,1,0:T(8,128)} fusion(f32[32,2,128,128]{3,2,1,0:T(8,128)} %bitcast.195, bf16[32,1,128,128]{3,2,1,0:T(8,128)(2,1)} %fusion.28, bf16[32,1,128,128]{3,2,1,0:T(8,128)(2,1)S(1)} %get-tuple-element.29), kind=kLoop, calls=%fused_computation.36 | loop fusion | flops 3145728 | bytes 10485760 | tf_op jit(solution)/shard_map/sub | solution.py:108
  166.3 2.8 convolution_bitcast_fusion.1
  169.1 5.7 %copy.105 = f32[32,256,128]{2,1,0:T(8,128)} copy(f32[32,256,128]{1,2,0:T(8,128)} %convolution_bitcast_fusion.1) | data formatting | bytes 8388608 | tf_op jit(solution)/shard_map/ab,sbh->sah/transpose | solution.py:105
  174.7 2.9 copy_subtract_fusion
  178.2 1.9 multiply_add_fusion
  180.3 5.4 %pad_maximum_fusion = (f32[32,128,3,128]{3,1,0,2:T(8,128)}, f32[32,128,3,128]{3,1,0,2:T(8,128)}) fusion(f32[32,128,1,128]{3,1,0,2:T(8,128)S(1)} %stack_broadcast_in_dim.4, f32[32,128,1,128]{3,1,0,2:T(8,128)S(1)} %get-tuple-element.8, f32[32,128,1,128]{3,1,0,2:T(8,128)S(1)} %get-tuple-element.7, f32[32,128,1,128]{3,1,0,2:T(8,128)S(1)} %get-tuple-element.27, ...), kind=kLoop, calls=%fused_computation.12 | loop fusion | flops 6291456 | bytes 23068672 | tf_op jit(solution)/shard_map/stack | solution.py:112
  185.7 6.7 %copy.107 = f32[32,128,3,128]{1,0,3,2:T(8,128)} copy(f32[32,128,3,128]{3,1,0,2:T(8,128)} %get-tuple-element.19) | data formatting | bytes 12582912 | tf_op jit(solution)/shard_map/stack | solution.py:112
  192.4 11.4 %copy.132 = f32[48,8,32,128]{3,1,2,0:T(8,128)} copy(f32[48,8,32,128]{3,2,1,0:T(8,128)} %bitcast.189) | data formatting | bytes 12582912
  203.8 7.1 %copy.98 = f32[32,128,3,128]{1,0,3,2:T(8,128)} copy(f32[32,128,3,128]{3,1,0,2:T(8,128)} %get-tuple-element.20) | data formatting | bytes 12582912 | tf_op jit(solution)/shard_map/stack | solution.py:112
  210.9 8.9 %copy.133 = f32[48,8,32,128]{3,1,2,0:T(8,128)S(1)} copy(f32[48,8,32,128]{3,2,1,0:T(8,128)} %bitcast.190) | data formatting | bytes 12582912
  219.9 6.6 %fusion.44 = f32[1,3,192,128]{3,2,1,0:T(8,128)S(1)} fusion(f32[3,128,4096]{2,1,0:T(8,128)S(1)} %bitcast.187, f32[4096]{0:T(1024)S(1)} %broadcast_bitcast_fusion, s32[4096]{0:T(1024)S(1)} %get-tuple-element.44), kind=kOutput, calls=%fused_computation.85 | convolution fusion | flops 3625451520 | bytes 6619136 | tf_op jit(solution)/shard_map/dot_general | solution.py:186
  226.5 6.5 %fusion.41 = f32[1,3,192,128]{3,2,1,0:T(8,128)S(1)} fusion(f32[3,128,4096]{2,1,0:T(8,128)S(1)} %bitcast.188, f32[4096]{0:T(1024)S(1)} %broadcast_bitcast_fusion.1, s32[4096]{0:T(1024)S(1)} %get-tuple-element.45), kind=kOutput, calls=%fused_computation.84 | convolution fusion | flops 3625451520 | bytes 6619136 | tf_op jit(solution)/shard_map/dot_general | solution.py:186
  233.1 5.2 collective-permute-start.2
  238.3 3.7 collective-permute-start.3
  242.0 1.9 collective-permute-done.3
  244.0 1.0 add_convert_fusion
  245.0 15.8 %all_gather.3 = bf16[2,2,512,128]{3,2,1,0:T(8,128)(2,1)S(1)} all-gather(bf16[2,2,64,128]{3,2,1,0:T(8,128)(2,1)S(1)} %get-tuple-element.3), channel_id=1, replica_groups=mesh['view'=4,'tile'=8] {'tile'}, dimensions={2}, use_global_device_ids=true | all-gather | bytes 589824 | tf_op jit(solution)/shard_map/all_gather | solution.py:206
  260.8 6.9 %convolution_bitcast_fusion = f32[2,8192,128]{1,2,0:T(8,128)} fusion(bf16[2,128,8192]{2,1,0:T(8,128)(2,1)} %param.16, bf16[1,2,128,128]{3,2,1,0:T(8,128)(2,1)S(1)} %constant_dynamic-slice_fusion, bf16[1,2,128,128]{3,2,1,0:T(8,128)(2,1)S(1)} %constant_dynamic-slice_fusion.1), kind=kOutput, calls=%fused_computation.11 | convolution fusion | flops 1073807360 | bytes 12713984 | tf_op jit(solution)/shard_map/acx,akch->kxh/dot_general | solution.py:208
  267.7 8.9 %copy.119 = f32[2,8192,128]{2,1,0:T(8,128)} copy(f32[2,8192,128]{1,2,0:T(8,128)} %convolution_bitcast_fusion) | data formatting | bytes 16777216 | tf_op jit(solution)/shard_map/reshape | solution.py:210
  276.6 172.5 %all-reduce.3.cloned.1.call-done = f32[2,64,128,128]{3,2,1,0:T(8,128)} async-done(((f32[2,64,128,128]{3,2,1,0:T(8,128)}), f32[2,64,128,128]{3,2,1,0:T(8,128)}) %all-reduce.3.cloned.1.call-update) | async-done | bytes 8388624 | tf_op jit(solution)/shard_map/psum | solution.py:211
  449.0 11.9 %multiply_subtract_fusion.1 = f32[2,64,128,128]{3,2,1,0:T(8,128)} fusion(f32[2,64,128,128]{3,2,1,0:T(8,128)} %param.17, f32[2,64,128,128]{3,2,1,0:T(8,128)} %all-reduce.3.cloned.1.call-done), kind=kLoop, calls=%fused_computation.23 | loop fusion | flops 4194304 | bytes 25165824 | tf_op jit(solution)/shard_map/sub | solution.py:212
  461.0 1.0 fusion.93
  462.0 3.8 collective-permute-start.5
  465.8 1.9 collective-permute-start.4
  467.7 0.7 add_subtract_fusion
  468.4 3.7 collective-permute-done.4
  472.1 15.3 %select_maximum_fusion = f32[2,66,130,130]{3,2,1,0:T(8,128)} fusion(f32[2,1,128,128]{3,2,1,0:T(8,128)S(1)} %collective-permute-done.4, f32[2,64,128,128]{3,2,1,0:T(8,128)} %multiply_subtract_fusion.1, f32[2,1,128,128]{3,2,1,0:T(8,128)S(1)} %collective-permute-done.5), kind=kLoop, calls=%fused_computation.6 | loop fusion | flops 33462000 | bytes 17573952 | tf_op jit(solution)/shard_map/concatenate | solution.py:27
  487.4 40.2 %multiply_subtract_fusion = f32[2,64,128,128]{3,2,1,0:T(8,128)} fusion(f32[2,64,128,128]{3,2,1,0:T(8,128)} %multiply_subtract_fusion.1, f32[2,66,130,130]{3,2,1,0:T(8,128)} %select_maximum_fusion, f32[2,1,128,128]{3,2,1,0:T(8,128)S(1)} %collective-permute-done.5, f32[2,1,128,128]{3,2,1,0:T(8,128)S(1)} %collective-permute-done.4), kind=kLoop, calls=%fused_computation.22 | loop fusion | flops 69206016 | bytes 50593792 | tf_op jit(solution)/shard_map/sub | solution.py:215
  (68 shorter events, 5.1 us)
Async XLA Ops:
  7.2 236.8 %reduce-scatter.2.cloned.1.call-start = ((), (), s32[]{:S(2)}) async-start(), calls=%async_computation.1 | async-start | bytes 1179648 | tf_op jit(solution)/shard_map/reduce_scatter | solution.py:164
  8.3 21.2 %collective-permute-start = (f32[2,2,64,128]{3,1,2,0:T(2,128)S(1)}, f32[2,2,64,128]{3,1,2,0:T(2,128)S(1)}, u32[]{:S(2)}, u32[]{:S(2)}) collective-permute-start(f32[2,2,64,128]{3,1,2,0:T(2,128)S(1)} %get-tuple-element.32), channel_id=1, source_target_pairs={{1,0},{2,1},{3,2},{4,3},{5,4},{6,5},{7,6},{9,8},{10,9},{11,10},{12... | collective-permute-start | bytes 393224 | tf_op jit(solution)/shard_map/ppermute | solution.py:15
  10.2 19.3 %collective-permute-start.1 = (f32[2,2,64,128]{3,1,2,0:T(2,128)S(1)}, f32[2,2,64,128]{3,1,2,0:T(2,128)S(1)}, u32[]{:S(2)}, u32[]{:S(2)}) collective-permute-start(f32[2,2,64,128]{3,1,2,0:T(2,128)S(1)} %get-tuple-element.32), channel_id=1, source_target_pairs={{2,0},{3,1},{4,2},{5,3},{6,4},{7,5},{10,8},{11,9},{12,10},{13,11},... | collective-permute-start | bytes 393224 | tf_op jit(solution)/shard_map/ppermute | solution.py:15
  25.2 1.5 copy-start.11
  25.2 1.5 copy-start.6
  25.2 1.6 copy-start.12
  26.5 422.5 %all-reduce.3.cloned.1.call-start = ((), (), s32[]{:S(2)}) async-start(), calls=%async_computation.2 | async-start | bytes 16777216 | tf_op jit(solution)/shard_map/psum | solution.py:211
  61.5 2.0 copy-start.4
  61.5 2.6 copy-start.5
  84.1 4.4 copy-start.2
  107.2 2.8 copy-start
  160.8 5.5 %copy-start.3 = (bf16[32,256,128]{1,2,0:T(8,128)(2,1)S(1)}, bf16[32,256,128]{1,2,0:T(8,128)(2,1)}, u32[]{:S(2)}) copy-start(bf16[32,256,128]{1,2,0:T(8,128)(2,1)} %reshape.295) | copy-start | bytes 6291460
  174.7 3.4 copy-start.1
  203.8 16.0 %slice-start = ((s8[6291456]{0:T(1024)(128)(4,1)}), s8[2097152]{0:T(1024)(128)(4,1)S(1)}, s32[]{:S(2)}) async-start(s8[6291456]{0:T(1024)(128)(4,1)} %bitcast.185), calls=%async_computation.3 | async-start | bytes 4194304
  210.9 8.9 %slice-start.1 = ((s8[6291456]{0:T(1024)(128)(4,1)}), s8[4194304]{0:T(1024)(128)(4,1)S(1)}, s32[]{:S(2)}) async-start(s8[6291456]{0:T(1024)(128)(4,1)} %bitcast.185), calls=%async_computation.4 | async-start | bytes 8388608
  226.5 17.5 %copy-start.7 = (f32[2,2,64,128]{3,2,1,0:T(8,128)S(1)}, f32[2,2,64,128]{3,2,1,0:T(8,128)}, u32[]{:S(2)}) copy-start(f32[2,2,64,128]{3,2,1,0:T(8,128)} %param.9) | copy-start | bytes 393220
  226.5 17.5 %copy-start.8 = (f32[2,2,64,128]{3,2,1,0:T(8,128)S(1)}, f32[2,2,64,128]{3,2,1,0:T(8,128)}, u32[]{:S(2)}) copy-start(f32[2,2,64,128]{3,2,1,0:T(8,128)} %param.10) | copy-start | bytes 393220
  233.1 8.9 %collective-permute-start.2 = (bf16[2,3,64,128]{3,2,1,0:T(8,128)(2,1)S(1)}, bf16[2,3,64,128]{3,2,1,0:T(8,128)(2,1)S(1)}, u32[]{:S(2)}, u32[]{:S(2)}) collective-permute-start(bf16[2,3,64,128]{3,2,1,0:T(8,128)(2,1)S(1)} %get-tuple-element.25), channel_id=1, source_target_pairs={{0,1},{1,2},{2,3},{3,4},{4,5},{5,6},{6,7},{8,9},{9,10},{10,11},{11... | collective-permute-start | bytes 294920 | tf_op jit(solution)/shard_map/ppermute | solution.py:15
  238.3 5.6 %collective-permute-start.3 = (bf16[2,3,64,128]{3,2,1,0:T(8,128)(2,1)S(1)}, bf16[2,3,64,128]{3,2,1,0:T(8,128)(2,1)S(1)}, u32[]{:S(2)}, u32[]{:S(2)}) collective-permute-start(bf16[2,3,64,128]{3,2,1,0:T(8,128)(2,1)S(1)} %get-tuple-element.26), channel_id=1, source_target_pairs={{0,2},{1,3},{2,4},{3,5},{4,6},{5,7},{8,10},{9,11},{10,12},{11,13},... | collective-permute-start | bytes 294920 | tf_op jit(solution)/shard_map/ppermute | solution.py:15
  244.9 222.8 %copy-start.10 = (f32[2,2,64,128]{3,2,1,0:T(8,128)}, f32[2,2,64,128]{3,2,1,0:T(8,128)S(1)}, u32[]{:S(2)}) copy-start(f32[2,2,64,128]{3,2,1,0:T(8,128)S(1)} %get-tuple-element.4) | copy-start | bytes 393220
  276.5 191.2 %copy-start.9 = (f32[2,2,64,128]{3,2,1,0:T(8,128)S(1)}, f32[2,2,64,128]{3,2,1,0:T(8,128)}, u32[]{:S(2)}) copy-start(f32[2,2,64,128]{3,2,1,0:T(8,128)} %reduce-scatter.2.cloned.1.call-done) | copy-start | bytes 393220
  462.0 6.5 %collective-permute-start.5 = (f32[2,1,128,128]{3,2,1,0:T(8,128)S(1)}, f32[2,1,128,128]{3,2,1,0:T(8,128)S(1)}, u32[]{:S(2)}, u32[]{:S(2)}) collective-permute-start(f32[2,1,128,128]{3,2,1,0:T(8,128)S(1)} %get-tuple-element.5), channel_id=1, source_target_pairs={{0,1},{1,2},{2,3},{3,4},{4,5},{5,6},{6,7},{8,9},{9,10},{10,11},{11... | collective-permute-start | bytes 393224 | tf_op jit(solution)/shard_map/ppermute | solution.py:25
  465.8 6.3 %collective-permute-start.4 = (f32[2,1,128,128]{3,2,1,0:T(8,128)S(1)}, f32[2,1,128,128]{3,2,1,0:T(8,128)S(1)}, u32[]{:S(2)}, u32[]{:S(2)}) collective-permute-start(f32[2,1,128,128]{3,2,1,0:T(8,128)S(1)} %get-tuple-element.6), channel_id=1, source_target_pairs={{1,0},{2,1},{3,2},{4,3},{5,4},{6,5},{7,6},{9,8},{10,9},{11,10},{12... | collective-permute-start | bytes 393224 | tf_op jit(solution)/shard_map/ppermute | solution.py:26
Sparse Core Ops, SparseCore 0:
  26.6 32.3 reduce-scatter.1
  276.7 172.3 all-reduce.2
where the time goes:
time: 540 us; the launch traced here: 535 us
  waiting for transfers between devices  178 us (33%)
  local copies, waits for them, and re-layouts  159 us (29%)
  other arithmetic  101 us (19%)
  matrix products  46.9 us (9%)
  starting transfers between devices  18.1 us (3%)
  between operations  16.1 us (3%)
  blocking collectives  15.8 us (3%)
    psum x1, waiting for transfers between devices, per_device(): gradient = lax.psum(grad_part, 'view')  172 us
    sub x1, other arithmetic, per_device(): volume_new = half_step - step_size * prior_weight * markov(padded)  40.2 us
    unnamed x34, local copies, waits for them, and re-layouts  23.5 us
    slice x2, local copies, waits for them, and re-layouts, batch_update(): obj_im = windows[:, 1]  17.8 us
    transpose x2, local copies, waits for them, and re-layouts, batch_update(): columns_done = columns_done.reshape(num_slots, 2, num_cols, num_rows).tra...  16 us
    transpose x2, local copies, waits for them, and re-layouts, batch_update(): inverse_rows = inverse_rows.reshape(num_slots, num_cols, 2, num_rows).tra...  16 us
    all_gather x1, blocking collectives, per_device(): residual_full = lax.all_gather(residual, 'tile', axis=2, tiled=True)  15.8 us
    concatenate x1, other arithmetic, extended(): array = jnp.concatenate([before, array, after], axis=dim)  15.3 us
  transfers between devices with their start and end apart: 8, of which 3 were waited for; matrix products, arithmetic and copies ran while one was open for 41% of the time, Pallas kernels for 0%

commit v1 on v0

v1 whole, which is shorter than its diff:
```python
import functools
import numpy as np
import jax
import jax.numpy as jnp
from jax import lax
from jax.experimental import pallas as pl
from jax.experimental.pallas import tpu as pltpu
from jax.sharding import PartitionSpec as P

rho_weight = 0.5
step_size = 0.5
prior_weight = 0.5
floor_term = 0.25

F32 = jnp.float32
BF16 = jnp.bfloat16
VMEM = pltpu.VMEM
SMEM = pltpu.SMEM


def passed_along(value, axis, steps):
    count = lax.axis_size(axis)
    initial, last = (max(0, -steps), min(count, count - steps))
    return lax.ppermute(value, axis, [(source, source + steps) for source in range(initial, last)])


def swapped(value, axis, mask):
    count = lax.axis_size(axis)
    return lax.ppermute(value, axis, [(i, i ^ mask) for i in range(count)])


def masks_of(count):
    return [1 << b for b in range(count.bit_length() - 1)]


def packed_rank(value, masks):
    rank = jnp.zeros_like(value)
    for place, mask in enumerate(masks):
        rank = rank + jnp.where((value & mask) != 0, 1 << place, 0)
    return rank


def dft_block(order_n, inverse):
    counter = np.arange(order_n)
    angles = (counter[:, None] * counter[None, :] % order_n) * (2.0 * np.pi / order_n)
    re = np.cos(angles) / np.sqrt(order_n)
    im = -np.sin(angles) / np.sqrt(order_n)
    im = -im if inverse else im
    return jnp.asarray(np.block([[re, -im], [im, re]]).astype(np.float32)).astype(BF16)


def project_kernel(spots, weights_ref, volume_ref, placed_ref, total):
    step = pl.program_id(0)
    views, cols, span = weights_ref.shape
    rows = volume_ref.shape[3]

    @pl.when(step == 0)
    def _():
        total[...] = jnp.zeros_like(total)

    low = jnp.concatenate(
        [volume_ref[0].reshape(span, rows), volume_ref[1].reshape(span, rows)], axis=1
    ).astype(BF16)
    total[...] += jnp.dot(
        weights_ref[...].reshape(views * cols, span), low, preferred_element_type=F32
    )

    @pl.when(step == pl.num_programs(0) - 1)
    def _():
        placed_ref[...] = jnp.zeros_like(placed_ref)
        width = placed_ref.shape[3]
        for v in range(views):
            for part in range(cols // width):
                spot = spots[v, part]
                first = v * cols + part * width
                for k in range(2):
                    placed_ref[spot, v, k] = total[
                        first : first + width, k * rows : (k + 1) * rows
                    ].astype(BF16)


def project(spots, weights, volume, tiles, tile_cols):
    views, cols, voxels = weights.shape
    _, vcols, depth, rows = volume.shape
    chunk = max(1, vcols // 8)
    span = chunk * depth
    return pl.pallas_call(
        project_kernel,
        out_shape=jax.ShapeDtypeStruct((tiles, views, 2, tile_cols, rows), BF16),
        grid_spec=pltpu.PrefetchScalarGridSpec(
            num_scalar_prefetch=1,
            grid=(vcols // chunk,),
            in_specs=[
                pl.BlockSpec((views, cols, span), lambda i, s: (0, 0, i)),
                pl.BlockSpec((2, chunk, depth, rows), lambda i, s: (0, i, 0, 0)),
            ],
            out_specs=pl.BlockSpec((tiles, views, 2, tile_cols, rows), lambda i, s: (0,) * 5),
            scratch_shapes=[VMEM((views * cols, 2 * rows), F32)],
        ),
        cost_estimate=pl.CostEstimate(
            flops=4 * views * cols * voxels * rows,
            transcendentals=0,
            bytes_accessed=weights.size * 2 + volume.size * 4,
        ),
        name="project",
    )(spots, weights, volume)


GROUP = 4


def patch_kernel(
    positions,
    live,
    own_ref,
    one_ref,
    two_ref,
    probe_ref,
    forward_ref,
    inverse_ref,
    counts_ref,
    near_ref,
    ahead_ref,
    reach,
    total,
    buffer,
    sems,
):
    views, _, width, rows = own_ref.shape
    cols = probe_ref.shape[1]
    span = 3 * width
    for part, ref in enumerate((own_ref, one_ref, two_ref)):
        reach[:, :, part * width : (part + 1) * width, :] = ref[...]
    total[...] = jnp.zeros_like(total)
    starts = [0]
    for v in range(views):
        starts.append(starts[-1] + lax.div(live[v] + (GROUP - 1), GROUP))

    def located(step):
        view, first = 0, 0
        for v in range(1, views):
            after = (step >= starts[v]).astype(jnp.int32)
            view = view + after
            first = jnp.where(after == 1, starts[v], first)
        return view, (step - first) * GROUP

    def fetch(step, slot):
        view, first = located(step)
        return pltpu.make_async_copy(
            counts_ref.at[view, pl.ds(first, GROUP)], buffer.at[slot], sems.at[slot]
        )

    fetch(0, 0).start()

    def body(step, carry):
        slot = step & 1
        view, first = located(step)
        pltpu.make_async_copy(
            counts_ref.at[view, pl.ds(first, GROUP)], buffer.at[slot], sems.at[slot]
        ).wait()

        @pl.when(step + 1 < starts[views])
        def _():
            fetch(step + 1, 1 - slot).start()

        probe_re = probe_ref[0]
        probe_im = probe_ref[1]
        spots = []
        exits = []
        for g in range(GROUP):
            offset = positions[view, first + g]
            spots.append(jnp.where(first + g < live[view], offset, span))
            obj_re = reach[view, 0, pl.ds(offset, cols), :]
            obj_im = reach[view, 1, pl.ds(offset, cols), :]
            wave_re = (probe_re * obj_re - probe_im * obj_im).astype(BF16)
            wave_im = (probe_re * obj_im + probe_im * obj_re).astype(BF16)
            exits.append(jnp.concatenate([wave_re, wave_im], axis=0))
        waves = jnp.concatenate(exits, axis=1)
        done = jnp.dot(forward_ref[...], waves, preferred_element_type=F32).astype(BF16)
        done = jnp.concatenate(
            [
                jnp.concatenate(
                    [
                        done[:cols, g * rows : (g + 1) * rows],
                        done[cols:, g * rows : (g + 1) * rows],
                    ],
                    axis=1,
                )
                for g in range(GROUP)
            ],
            axis=0,
        )
        spectrum = jnp.dot(done, inverse_ref[...], preferred_element_type=F32)
        spec_re = spectrum[:, :rows]
        spec_im = spectrum[:, rows:]
        counts = buffer[slot].reshape(GROUP * cols, rows).astype(F32)
        square = spec_re * spec_re + spec_im * spec_im + floor_term
        factor = (counts * (1.0 / 16.0)) * lax.rsqrt(jnp.maximum(counts * square, 1e-6))
        replaced = jnp.concatenate(
            [(spec_re * factor).astype(BF16), (spec_im * factor).astype(BF16)], axis=1
        )
        back = jnp.dot(replaced, forward_ref[...], preferred_element_type=F32).astype(BF16)
        back = jnp.concatenate(
            [
                jnp.concatenate(
                    [
                        back[g * cols : (g + 1) * cols, :rows],
                        back[g * cols : (g + 1) * cols, rows:],
                    ],
                    axis=0,
                )
                for g in range(GROUP)
            ],
            axis=1,
        )
        wave = jnp.dot(inverse_ref[...], back, preferred_element_type=F32)
        power = probe_re * probe_re + probe_im * probe_im
        for g in range(GROUP):
            diff = wave[:, g * rows : (g + 1) * rows] - exits[g].astype(F32)
            diff_re = diff[:cols]
            diff_im = diff[cols:]
            place = pl.ds(spots[g], cols)
            total[view, 0, place, :] += probe_re * diff_re + probe_im * diff_im
            total[view, 1, place, :] += probe_re * diff_im - probe_im * diff_re
            total[view, 2, place, :] += power
        return carry

    lax.fori_loop(0, starts[views], body, 0)
    near_ref[...] = total[:, :, :width, :]
    for part in range(2):
        ahead_ref[part] = total[:, :, (part + 1) * width : (part + 2) * width, :].astype(BF16)


def patches(positions, live, own, one, two, probe, forward, inverse, counts):
    views, _, width, rows = own.shape
    cols = probe.shape[1]
    slots = counts.shape[1]
    vmem = pl.BlockSpec(memory_space=VMEM)
    smem = pl.BlockSpec(memory_space=SMEM)
    return pl.pallas_call(
        patch_kernel,
        out_shape=(
            jax.ShapeDtypeStruct((views, 3, width, rows), F32),
            jax.ShapeDtypeStruct((2, views, 3, width, rows), BF16),
        ),
        in_specs=[smem, smem] + [vmem] * 6 + [pl.BlockSpec(memory_space=pl.ANY)],
        out_specs=(vmem, vmem),
        scratch_shapes=[
            VMEM((views, 2, 3 * width, rows), F32),
            VMEM((views, 3, 3 * width + cols, rows), F32),
            VMEM((2, GROUP, cols, rows), jnp.int32),
            pltpu.SemaphoreType.DMA((2,)),
        ],
        cost_estimate=pl.CostEstimate(
            flops=views * slots * 16 * cols * cols * rows,
            transcendentals=0,
            bytes_accessed=counts.size * 4,
        ),
        name="patches",
    )(positions, live, own, one, two, probe, forward, inverse, counts)


def cut_kernel(spots, *refs):
    pieces, windows_ref, held = refs[:-2], refs[-2], refs[-1]
    first = 0
    for ref in pieces:
        held[first : first + ref.shape[0]] = ref[...]
        first += ref.shape[0]
    views, planes, cols, rows = windows_ref.shape
    width = held.shape[3]
    for v in range(views):
        for part in range(cols // width):
            for k in range(planes):
                windows_ref[v, k, part * width : (part + 1) * width] = held[spots[v, part], v, k]


def cut(spots, pieces, cols):
    blocks = sum(piece.shape[0] for piece in pieces)
    _, views, planes, width, rows = pieces[0].shape
    vmem = pl.BlockSpec(memory_space=VMEM)
    return pl.pallas_call(
        cut_kernel,
        out_shape=jax.ShapeDtypeStruct((views, planes, cols, rows), BF16),
        in_specs=[pl.BlockSpec(memory_space=SMEM)] + [vmem] * len(pieces),
        out_specs=vmem,
        scratch_shapes=[VMEM((blocks, views, planes, width, rows), BF16)],
        name="cut",
    )(spots, *pieces)


def half_kernel(groups, mine, *refs):
    weight_refs = refs[:groups]
    window_refs = refs[groups : 2 * groups]
    volume_ref, half_ref, low_ref, high_ref = refs[2 * groups :]
    step = pl.program_id(0)
    _, chunk, depth, rows = half_ref.shape
    gradient = None
    for weights, windows in zip(weight_refs, window_refs):
        for v in range(weights.shape[0]):
            both = jnp.concatenate([windows[v, 0], windows[v, 1]], axis=1)
            product = lax.dot_general(
                weights[v], both, (((0,), (0,)), ((), ())), preferred_element_type=F32
            )
            gradient = product if gradient is None else gradient + product
    for k in range(2):
        plane = gradient[:, k * rows : (k + 1) * rows].reshape(chunk, depth, rows)
        half_ref[k] = volume_ref[k] - step_size * plane

    @pl.when(step == 0)
    def _():
        low_ref[...] = half_ref[:, :1]

    @pl.when(step == pl.num_programs(0) - 1)
    def _():
        high_ref[...] = half_ref[:, chunk - 1 :]


def half_step_of(mine, weights, pieces, windows, volume):
    groups = len(windows)
    views, cols, voxels = weights.shape
    _, vcols, depth, rows = volume.shape
    share = vcols // groups
    chunk = min(4, share)
    span = chunk * depth
    steps = share // chunk
    edge = pl.BlockSpec((2, 1, depth, rows), lambda i, m: (0, 0, 0, 0))
    whole = pl.BlockSpec(windows[0].shape, lambda i, m: (0, 0, 0, 0))
    piece = pl.BlockSpec((views, cols, span), lambda i, m: (0, 0, i))
    return pl.pallas_call(
        functools.partial(half_kernel, groups),
        out_shape=(
            jax.ShapeDtypeStruct((2, share, depth, rows), F32),
            jax.ShapeDtypeStruct((2, 1, depth, rows), F32),
            jax.ShapeDtypeStruct((2, 1, depth, rows), F32),
        ),
        grid_spec=pltpu.PrefetchScalarGridSpec(
            num_scalar_prefetch=1,
            grid=(steps,),
            in_specs=[pl.BlockSpec((views, cols, span), lambda i, m: (0, 0, m[0] * steps + i))]
            + [piece] * (groups - 1)
            + [whole] * groups
            + [pl.BlockSpec((2, chunk, depth, rows), lambda i, m: (0, m[0] * steps + i, 0, 0))],
            out_specs=(
                pl.BlockSpec((2, chunk, depth, rows), lambda i, m: (0, i, 0, 0)),
                edge,
                edge,
            ),
        ),
        name="half_step",
    )(mine, weights, *pieces, *windows, volume)


def bent(d):
    return d * lax.rsqrt(1.0 + d * d)


def prior_kernel(mine, half_ref, before_ref, after_ref, out_ref, first_ref, second_ref, link):
    step = pl.program_id(0)
    last = pl.num_programs(0) - 1
    depth, rows = half_ref.shape[2:]
    lane = lax.broadcasted_iota(jnp.int32, (depth, rows), 1)
    level = lax.broadcasted_iota(jnp.int32, (depth, rows), 0)
    for k, low_ref in ((0, first_ref), (1, second_ref)):
        here = half_ref[k, step]

        @pl.when(step == 0)
        def _():
            link[k] = bent(before_ref[k, 0] - here)

        following = half_ref[k, jnp.minimum(step + 1, last)]
        following = jnp.where(step == last, after_ref[k, 0], following)
        ahead = bent(here - following)
        prior = ahead - link[k]
        link[k] = ahead
        beyond = jnp.where(lane == rows - 1, 0.0, pltpu.roll(here, rows - 1, 1))
        pair = bent(here - beyond)
        alone = bent(here)
        prior = prior + pair - jnp.where(lane == 0, -alone, pltpu.roll(pair, 1, 1))
        beyond = jnp.where(level == depth - 1, 0.0, pltpu.roll(here, depth - 1, 0))
        pair = bent(here - beyond)
        prior = prior + pair - jnp.where(level == 0, -alone, pltpu.roll(pair, 1, 0))
        fresh = here - step_size * prior_weight * prior
        out_ref[k, 0] = fresh
        low_ref[...] = fresh.astype(BF16)


def prior_step(mine, half, before, after, vcols):
    _, share, depth, rows = half.shape
    edge = pl.BlockSpec((2, 1, depth, rows), lambda i, m: (0, 0, 0, 0))
    low = pl.BlockSpec((depth, rows), lambda i, m: (i, 0))
    return pl.pallas_call(
        prior_kernel,
        out_shape=(
            jax.ShapeDtypeStruct((2, vcols, depth, rows), F32),
            jax.ShapeDtypeStruct((share * depth, rows), BF16),
            jax.ShapeDtypeStruct((share * depth, rows), BF16),
        ),
        grid_spec=pltpu.PrefetchScalarGridSpec(
            num_scalar_prefetch=1,
            grid=(share,),
            in_specs=[
                pl.BlockSpec((2, share, depth, rows), lambda i, m: (0, 0, 0, 0)),
                edge,
                edge,
            ],
            out_specs=(
                pl.BlockSpec((2, 1, depth, rows), lambda i, m: (0, m[0] * share + i, 0, 0)),
                low,
                low,
            ),
            scratch_shapes=[VMEM((2, depth, rows), F32)],
        ),
        name="prior",
    )(mine, half, before, after)


def place_kernel(where, piece_ref, whole_ref, out_ref):
    out_ref[...] = piece_ref[...].reshape(out_ref.shape).astype(F32)


def place(where, piece, whole, plane, groups):
    _, vcols, depth, rows = whole.shape
    share = vcols // groups
    chunk = max(1, share // 2)
    steps = share // chunk
    return pl.pallas_call(
        place_kernel,
        out_shape=jax.ShapeDtypeStruct(whole.shape, F32),
        grid_spec=pltpu.PrefetchScalarGridSpec(
            num_scalar_prefetch=1,
            grid=(steps,),
            in_specs=[
                pl.BlockSpec((chunk * depth, rows), lambda i, w: (i, 0)),
                pl.BlockSpec(memory_space=pl.ANY),
            ],
            out_specs=pl.BlockSpec(
                (1, chunk, depth, rows), lambda i, w: (plane, w[0] * steps + i, 0, 0)
            ),
        ),
        input_output_aliases={2: 0},
        name="place",
    )(where, piece, whole)


def per_device(
    object_band,
    dual_band,
    probe_field,
    positions,
    live_counts,
    photon_counts,
    footprints,
    weights,
    volume,
):
    tiles, groups = lax.axis_size("tile"), lax.axis_size("view")
    tile, group = lax.axis_index("tile"), lax.axis_index("view")
    tile_cols = object_band.shape[2]
    foot_cols = weights.shape[1]
    vcols = volume.shape[1]
    share_voxels = weights.shape[2] // groups
    tile_masks = masks_of(tiles)
    forward = dft_block(probe_field.shape[1], False)
    inverse = dft_block(probe_field.shape[1], True)
    mine = group.astype(jnp.int32).reshape(1)
    blocks = footprints + jnp.arange(foot_cols // tile_cols, dtype=jnp.int32)[None, :]
    relative = blocks ^ tile.astype(jnp.int32)

    ahead_one = passed_along(object_band, "tile", -1)
    ahead_two = passed_along(object_band, "tile", -2)
    weight_pieces = [
        swapped(
            lax.dynamic_slice_in_dim(weights, (group ^ j) * share_voxels, share_voxels, 2),
            "view",
            j,
        )
        for j in range(1, groups)
    ]

    placed = project(packed_rank(relative, tile_masks[::-1]), weights, volume, tiles, tile_cols)
    held = placed
    for mask in tile_masks:
        half = held.shape[0] // 2
        arrived = swapped(held[half:], "tile", mask)
        held = held[:half].astype(F32) + arrived.astype(F32)
        held = held.astype(BF16) if half > 1 else held
    projection = held[0]

    near, ahead = patches(
        positions,
        live_counts[:, 0],
        object_band,
        ahead_one,
        ahead_two,
        probe_field,
        forward,
        inverse,
        photon_counts,
    )
    from_one = passed_along(ahead[0], "tile", 1).astype(F32)
    from_two = passed_along(ahead[1], "tile", 2).astype(F32)
    summed = near + from_one + from_two
    object_new = (
        object_band
        + summed[:, 0:2] / (1.0 + summed[:, 2:3])
        - rho_weight * (object_band - projection - dual_band)
    )
    dual_new = dual_band + projection - object_new
    residual = (projection - object_new + dual_band).astype(BF16)

    pieces = [residual[None]]
    for mask in tile_masks[::-1]:
        gathered = pieces[0] if len(pieces) == 1 else jnp.concatenate(pieces, axis=0)
        pieces.append(swapped(gathered, "tile", mask))
    windows = cut(packed_rank(relative, tile_masks[::-1]), pieces, foot_cols)
    all_windows = [windows] + [swapped(windows, "view", j) for j in range(1, groups)]

    half, low_edge, high_edge = half_step_of(mine, weights, weight_pieces, all_windows, volume)
    order = [g * tiles + t for t in range(tiles) for g in range(groups)]
    up = list(zip(order[:-1], order[1:]))
    before = lax.ppermute(high_edge, ("view", "tile"), up)
    after = lax.ppermute(low_edge, ("view", "tile"), [(b, a) for a, b in up])
    volume_new, *shares = prior_step(mine, half, before, after, vcols)
    view_masks = masks_of(groups)
    for plane, masks in ((0, view_masks), (1, view_masks[::-1])):
        held = {0: shares[plane]}
        for mask in masks:
            held.update({j ^ mask: swapped(value, "view", mask) for j, value in held.items()})
        for j, value in held.items():
            if j:
                volume_new = place(mine ^ j, value, volume_new, plane, groups)
    return (object_new, dual_new, volume_new)


def solution(mesh):
    return jax.shard_map(
        per_device,
        mesh=mesh,
        in_specs=(
            P("view", None, "tile", None),
            P("view", None, "tile", None),
            P(),
            P("view", "tile"),
            P("view", "tile"),
            P("view", "tile", None, None),
            P("view", "tile"),
            P("view", None, "tile"),
            P(None, "tile", None, None),
        ),
        out_specs=(
            P("view", None, "tile", None),
            P("view", None, "tile", None),
            P(None, "tile", None, None),
        ),
        check_vma=False,
    )
```

time: 540 us -> 164 us (0.30)
  local copies, waits for them, and re-layouts: 159 us -> 12.3 us
  waiting for transfers between devices: 178 us -> 47.3 us
  other arithmetic: 101 us -> 4.11 us
  Pallas kernels: 0 us -> 47.3 us
  matrix products: 46.9 us -> 0 us
  starting transfers between devices: 18.1 us -> 50.1 us
  blocking collectives: 15.8 us -> 0 us
  between operations: 16.1 us -> 0.92 us
    psum x1 -> x0, waiting for transfers between devices: 172 us -> none  [per_device(): gradient = lax.psum(grad_part, 'view')]
    sub x5 -> x0, other arithmetic: 61.8 us -> none  [the longest x1 40.2 us: per_device(): volume_new = half_step - step_size * prior_weight * markov(padded)]
    pallas_call x0 -> x11, Pallas kernels: none -> 47.3 us  [the longest x6 11.7 us: place(): pl.pallas_call(place_kernel, out_shape=jax.ShapeDtypeStruct(whole.shape,...]
    dot_general x12 -> x0, matrix products: 46.9 us -> none  [the longest x2 13.1 us: per_device(): jnp.dot(placement.T, flat, precision=lax.Precision.HIGHEST, preferred_ele...]
    ppermute x2 -> x20, waiting for transfers between devices: 3.66 us -> 47.1 us  [the longest x18 44.2 us: swapped(): return lax.ppermute(value, axis, [(i, i ^ mask) for i in range(count)])]
    transpose x6 -> x0, local copies, waits for them, and re-layouts: 43.4 us -> none  [the longest x2 16 us: batch_update(): columns_done = columns_done.reshape(num_slots, 2, num_cols, num_rows).tra...]
    reshape x9 -> x0, local copies, waits for them, and re-layouts: 42.3 us -> none  [the longest x1 8.85 us: per_device(): grad_part = jnp.einsum('acx,akch->kxh', weights, residual_windows, prefer...]
    ppermute x2 -> x20, starting transfers between devices: 5.76 us -> 35.5 us  [the longest x18 29 us: swapped(): return lax.ppermute(value, axis, [(i, i ^ mask) for i in range(count)])]
  transfers between devices with their start and end apart: 8 -> 24, of which waited for: 3 -> 14; matrix products, arithmetic and copies ran while one was open for 41% -> 6% of each run, Pallas kernels for 0% -> 18%
where the time goes in v1:
time: 164 us; the launch traced here: 162 us
  starting transfers between devices  50.1 us (31%)
  Pallas kernels  47.3 us (29%)
  waiting for transfers between devices  47.3 us (29%)
  local copies, waits for them, and re-layouts  12.3 us (8%)
  other arithmetic  4.11 us (3%)
    ppermute x18, waiting for transfers between devices, swapped(): return lax.ppermute(value, axis, [(i, i ^ mask) for i in range(count)])  44.2 us
    ppermute x18, starting transfers between devices, swapped(): return lax.ppermute(value, axis, [(i, i ^ mask) for i in range(count)])  29 us
    ppermute x4, starting transfers between devices, passed_along(): lax.ppermute(value, axis, [(source, source + steps) for source in range(i...  14.7 us
    pallas_call x6, Pallas kernels, place(): pl.pallas_call(place_kernel, out_shape=jax.ShapeDtypeStruct(whole.shape,...  11.7 us
    pallas_call x1, Pallas kernels, prior_step(): pl.pallas_call(prior_kernel, out_shape=(jax.ShapeDtypeStruct((2, vcols, d...  10.1 us
    pallas_call x1, Pallas kernels, project(): pl.pallas_call(project_kernel, out_shape=jax.ShapeDtypeStruct((tiles, vie...  9.19 us
    pallas_call x1, Pallas kernels, patches(): pl.pallas_call(patch_kernel, out_shape=(jax.ShapeDtypeStruct((views, 3, w...  8.03 us
    unnamed x46, local copies, waits for them, and re-layouts  6.59 us
  transfers between devices with their start and end apart: 24, of which 14 were waited for; matrix products, arithmetic and copies ran while one was open for 6% of the time, Pallas kernels for 18%

profile of v1, /device:TPU:1, one launch (start us, length us, event | category | flops | bytes accessed | tf_op | source)
XLA Modules:
  0.0 162.0 jit_solution(1074885771565361990)
XLA Ops:
  0.6 1.9 %collective-permute-start = (f32[2,2,64,128]{3,2,1,0:T(8,128)}, f32[2,2,64,128]{3,2,1,0:T(8,128)S(1)}, u32[]{:S(2)}, u32[]{:S(2)}) collective-permute-start(f32[2,2,64,128]{3,2,1,0:T(8,128)} %own_ref.1), channel_id=1, source_target_pairs={{1,0},{2,1},{3,2},{4,3},{5,4},{6,5},{7,6},{9,8},{10,9},{11,10},{12... | collective-permute-start | bytes 393224 | tf_op jit(solution)/shard_map/ppermute | solution.py:24
  2.6 1.3 collective-permute-start.1
  3.9 1.3 fusion.10.spots
  5.2 9.2 %project.1 = bf16[8,2,2,64,128]{4,3,2,1,0:T(8,128)(2,1)} custom-call(s32[2,2]{1,0:T(2,128)} %fusion.10.spots, bf16[2,128,8192]{2,1,0:T(8,128)(2,1)} %refs_0_.1, f32[2,64,128,128]{3,2,1,0:T(8,128)} %refs_8_.1), custom_call_target="tpu_custom_call" | custom-call | flops 1073741824 | bytes 12582912 | tf_op jit(solution)/shard_map/project/pallas_call | solution.py:87
  14.4 1.0 slice.43
  15.4 0.1 collective-permute-start.4
  15.6 3.7 %constant_dynamic-slice_fusion = (bf16[2,128,2048]{2,1,0:T(8,128)(2,1)}, bf16[2,128,2048]{2,1,0:T(8,128)(2,1)}, bf16[2,128,2048]{2,1,0:T(8,128)(2,1)}) fusion(bf16[2,128,8192]{2,1,0:T(8,128)(2,1)} %refs_0_.1, s32[]{:T(128)S(6)} %select_n.27, s32[]{:T(128)S(6)} %select_n.26, s32[]{:T(128)S(6)} %select_n.25), kind=kLoop, calls=%fused_computation.27 | loop fusion | bytes 6291468 | tf_op jit(solution)/shard_map/dynamic_slice | solution.py:473
  19.3 2.7 %collective-permute-start.7 = (bf16[2,128,2048]{2,1,0:T(8,128)(2,1)}, bf16[2,128,2048]{2,1,0:T(8,128)(2,1)S(1)}, u32[]{:S(2)}, u32[]{:S(2)}) collective-permute-start(bf16[2,128,2048]{2,1,0:T(8,128)(2,1)} %get-tuple-element.23), channel_id=1, source_target_pairs={{0,8},{8,0},{16,24},{24,16},{1,9},{9,1},{17,25},{25,17},{2,10},{10... | collective-permute-start | bytes 3145736 | tf_op jit(solution)/shard_map/ppermute | solution.py:29
  21.9 1.2 collective-permute-start.8
  23.2 0.0 collective-permute-start.9
  23.2 0.6 copy-done.22
  23.8 8.0 %patches.1 = (f32[2,3,64,128]{3,2,1,0:T(8,128)}, bf16[2,2,3,64,128]{4,3,2,1,0:T(8,128)(2,1)}) custom-call(s32[2,32]{1,0:T(2,128)} %positions.1, s32[2]{0:T(128)} %bitcast.31, f32[2,2,64,128]{3,2,1,0:T(8,128)} %own_ref.1, f32[2,2,64,128]{3,2,1,0:T(8,128)} %copy-done.22, f32[2,2,64,128]{3,2,1,0:T(8,128)} %collective-permute-done.1.two_ref, ...), custom_call_target="tpu_custom_call" | custom-call | flops 2147483648 | bytes 4194304 | tf_op jit(solution)/shard_map/patches/pallas_call | solution.py:240
  31.9 1.0 slice_bitcast_fusion.1
  32.8 10.2 %collective-permute-start.2 = (bf16[2,3,64,128]{3,2,1,0:T(8,128)(2,1)S(1)}, bf16[2,3,64,128]{3,2,1,0:T(8,128)(2,1)S(1)}, u32[]{:S(2)}, u32[]{:S(2)}) collective-permute-start(bf16[2,3,64,128]{3,2,1,0:T(8,128)(2,1)S(1)} %get-tuple-element.24), channel_id=1, source_target_pairs={{0,1},{1,2},{2,3},{3,4},{4,5},{5,6},{6,7},{8,9},{9,10},{10,11},{11... | collective-permute-start | bytes 294920 | tf_op jit(solution)/shard_map/ppermute | solution.py:24
  43.0 1.3 collective-permute-start.3
  44.3 0.1 add_convert_fusion
  44.4 0.2 collective-permute-done.2
  44.6 4.3 %collective-permute-start.5 = (bf16[2,2,2,64,128]{4,3,2,1,0:T(8,128)(2,1)S(1)}, bf16[2,2,2,64,128]{4,3,2,1,0:T(8,128)(2,1)S(1)}, u32[]{:S(2)}, u32[]{:S(2)}) collective-permute-start(bf16[2,2,2,64,128]{4,3,2,1,0:T(8,128)(2,1)S(1)} %slice.45), channel_id=1, source_target_pairs={{0,2},{1,3},{2,0},{3,1},{4,6},{5,7},{6,4},{7,5},{8,10},{9,11},{10,... | collective-permute-start | bytes 393224 | tf_op jit(solution)/shard_map/ppermute | solution.py:29
  48.9 1.0 convert_add_fusion
  49.9 2.2 %collective-permute-done.5 = bf16[2,2,2,64,128]{4,3,2,1,0:T(8,128)(2,1)S(1)} collective-permute-done((bf16[2,2,2,64,128]{4,3,2,1,0:T(8,128)(2,1)S(1)}, bf16[2,2,2,64,128]{4,3,2,1,0:T(8,128)(2,1)S(1)}, u32[]{:S(2)}, u32[]{:S(2)}) %collective-permute-start.5) | collective-permute-done | bytes 131104 | tf_op jit(solution)/shard_map/ppermute | solution.py:29
  52.2 1.3 collective-permute-start.6
  53.5 3.2 %collective-permute-done.6 = bf16[1,2,2,64,128]{4,3,2,1,0:T(8,128)(2,1)S(1)} collective-permute-done((bf16[1,2,2,64,128]{4,3,2,1,0:T(8,128)(2,1)S(1)}, bf16[1,2,2,64,128]{4,3,2,1,0:T(8,128)(2,1)S(1)}, u32[]{:S(2)}, u32[]{:S(2)}) %collective-permute-start.6) | collective-permute-done | bytes 65568 | tf_op jit(solution)/shard_map/ppermute | solution.py:29
  56.6 0.1 fusion.7
  56.7 1.3 collective-permute-start.10
  58.0 3.2 %collective-permute-done.10.refs_1_ = bf16[1,2,2,64,128]{4,3,2,1,0:T(8,128)(2,1)S(1)} collective-permute-done((bf16[1,2,2,64,128]{4,3,2,1,0:T(8,128)(2,1)S(1)}, bf16[1,2,2,64,128]{4,3,2,1,0:T(8,128)(2,1)S(1)}, u32[]{:S(2)}, u32[]{:S(2)}) %collective-permute-start.10) | collective-permute-done | bytes 65568 | tf_op jit(solution)/shard_map/ppermute | solution.py:29
  61.2 1.2 collective-permute-start.11
  62.5 3.0 %collective-permute-done.11.refs_2_ = bf16[2,2,2,64,128]{4,3,2,1,0:T(8,128)(2,1)S(1)} collective-permute-done((bf16[2,2,2,64,128]{4,3,2,1,0:T(8,128)(2,1)S(1)}, bf16[2,2,2,64,128]{4,3,2,1,0:T(8,128)(2,1)S(1)}, u32[]{:S(2)}, u32[]{:S(2)}) %collective-permute-start.11) | collective-permute-done | bytes 131104 | tf_op jit(solution)/shard_map/ppermute | solution.py:29
  65.6 3.6 %collective-permute-start.12 = (bf16[4,2,2,64,128]{4,3,2,1,0:T(8,128)(2,1)S(1)}, bf16[4,2,2,64,128]{4,3,2,1,0:T(8,128)(2,1)S(1)}, u32[]{:S(2)}, u32[]{:S(2)}) collective-permute-start(bf16[4,2,2,64,128]{4,3,2,1,0:T(8,128)(2,1)S(1)} %pad_maximum_fusion), channel_id=1, source_target_pairs={{0,1},{1,0},{2,3},{3,2},{4,5},{5,4},{6,7},{7,6},{8,9},{9,8},{10,11... | collective-permute-start | bytes 786440 | tf_op jit(solution)/shard_map/ppermute | solution.py:29
  69.1 1.2 collective-permute-done.12.refs_3_
  70.3 0.7 copy-done.14
  71.0 1.8 %cut.1.refs_4_ = bf16[2,2,128,128]{3,2,1,0:T(8,128)(2,1)} custom-call(s32[2,2]{1,0:T(2,128)} %fusion.10.spots, bf16[1,2,2,64,128]{4,3,2,1,0:T(8,128)(2,1)} %copy-done.3, bf16[1,2,2,64,128]{4,3,2,1,0:T(8,128)(2,1)} %copy-done.4, bf16[2,2,2,64,128]{4,3,2,1,0:T(8,128)(2,1)} %copy-done.11, bf16[4,2,2,64,128]{4,3,2,1,0:T(8,128)(2,1)} %copy-done.14), custom_call_target="tpu_custom_call" | custom-call | tf_op jit(solution)/shard_map/cut/pallas_call | solution.py:281
  72.8 0.1 collective-permute-start.14
  72.9 4.8 %collective-permute-done.13.refs_5_ = bf16[2,2,128,128]{3,2,1,0:T(8,128)(2,1)S(1)} collective-permute-done((bf16[2,2,128,128]{3,2,1,0:T(8,128)(2,1)}, bf16[2,2,128,128]{3,2,1,0:T(8,128)(2,1)S(1)}, u32[]{:S(2)}, u32[]{:S(2)}) %collective-permute-start.13) | collective-permute-done | bytes 131104 | tf_op jit(solution)/shard_map/ppermute | solution.py:29
  77.7 4.9 %collective-permute-done.15.refs_7_ = bf16[2,2,128,128]{3,2,1,0:T(8,128)(2,1)S(1)} collective-permute-done((bf16[2,2,128,128]{3,2,1,0:T(8,128)(2,1)}, bf16[2,2,128,128]{3,2,1,0:T(8,128)(2,1)S(1)}, u32[]{:S(2)}, u32[]{:S(2)}) %collective-permute-start.15) | collective-permute-done | bytes 131104 | tf_op jit(solution)/shard_map/ppermute | solution.py:29
  82.7 0.6 copy-done.18
  83.3 0.4 copy-done.1
  83.6 0.4 copy-done.2
  84.0 6.4 %half_step.1 = (f32[2,16,128,128]{3,2,1,0:T(8,128)}, f32[2,1,128,128]{3,2,1,0:T(8,128)}, f32[2,1,128,128]{3,2,1,0:T(8,128)}) custom-call(s32[1]{0:T(128)} %bitcast.6.mine, bf16[2,128,8192]{2,1,0:T(8,128)(2,1)} %refs_0_.1, bf16[2,128,2048]{2,1,0:T(8,128)(2,1)} %copy-done.1, bf16[2,128,2048]{2,1,0:T(8,128)(2,1)} %copy-done.2, ...), custom_call_target="tpu_custom_call" | custom-call | tf_op jit(solution)/shard_map/half_step/pallas_call | solution.py:329
  90.4 2.2 %collective-permute-start.16 = (f32[2,1,128,128]{3,2,1,0:T(8,128)}, f32[2,1,128,128]{3,2,1,0:T(8,128)S(1)}, u32[]{:S(2)}, u32[]{:S(2)}) collective-permute-start(f32[2,1,128,128]{3,2,1,0:T(8,128)} %get-tuple-element.14), channel_id=1, source_target_pairs={{0,8},{8,16},{16,24},{24,1},{1,9},{9,17},{17,25},{25,2},{2,10},{10... | collective-permute-start | bytes 393224 | tf_op jit(solution)/shard_map/ppermute | solution.py:521
  92.6 4.3 %collective-permute-start.17 = (f32[2,1,128,128]{3,2,1,0:T(8,128)}, f32[2,1,128,128]{3,2,1,0:T(8,128)S(1)}, u32[]{:S(2)}, u32[]{:S(2)}) collective-permute-start(f32[2,1,128,128]{3,2,1,0:T(8,128)} %get-tuple-element.15), channel_id=1, source_target_pairs={{8,0},{16,8},{24,16},{1,24},{9,1},{17,9},{25,17},{2,25},{10,2},{18... | collective-permute-start | bytes 393224 | tf_op jit(solution)/shard_map/ppermute | solution.py:522
  96.9 0.9 collective-permute-done.16.before_ref
  97.8 2.0 %collective-permute-done.17.after_ref = f32[2,1,128,128]{3,2,1,0:T(8,128)S(1)} collective-permute-done((f32[2,1,128,128]{3,2,1,0:T(8,128)}, f32[2,1,128,128]{3,2,1,0:T(8,128)S(1)}, u32[]{:S(2)}, u32[]{:S(2)}) %collective-permute-start.17) | collective-permute-done | bytes 131104 | tf_op jit(solution)/shard_map/ppermute | solution.py:522
  99.8 0.7 copy-done.20
  100.5 10.1 %prior.1 = (f32[2,64,128,128]{3,2,1,0:T(8,128)}, bf16[2048,128]{1,0:T(8,128)(2,1)}, bf16[2048,128]{1,0:T(8,128)(2,1)}) custom-call(s32[1]{0:T(128)} %bitcast.6.mine, f32[2,16,128,128]{3,2,1,0:T(8,128)} %get-tuple-element.13.half_ref, f32[2,1,128,128]{3,2,1,0:T(8,128)} %copy-done.19, f32[2,1,128,128]{3,2,1,0:T(8,128)} %copy-done.20), custom_call_target="tpu_custom_call" | custom-call | tf_op jit(solution)/shard_map/prior/pallas_call | solution.py:391
  110.7 0.6 collective-permute-start.21
  111.2 6.3 %collective-permute-start.18 = (bf16[2048,128]{1,0:T(8,128)(2,1)}, bf16[2048,128]{1,0:T(8,128)(2,1)S(1)}, u32[]{:S(2)}, u32[]{:S(2)}) collective-permute-start(bf16[2048,128]{1,0:T(8,128)(2,1)} %get-tuple-element.16), channel_id=1, source_target_pairs={{0,16},{8,24},{16,0},{24,8},{1,17},{9,25},{17,1},{25,9},{2,18},{10... | collective-permute-start | bytes 1572872 | tf_op jit(solution)/shard_map/ppermute | solution.py:29
  117.6 4.4 %collective-permute-done.21.piece_ref = bf16[2048,128]{1,0:T(8,128)(2,1)S(1)} collective-permute-done((bf16[2048,128]{1,0:T(8,128)(2,1)}, bf16[2048,128]{1,0:T(8,128)(2,1)S(1)}, u32[]{:S(2)}, u32[]{:S(2)}) %collective-permute-start.21) | collective-permute-done | bytes 524320 | tf_op jit(solution)/shard_map/ppermute | solution.py:29
  122.0 5.6 %collective-permute-start.22 = (bf16[2048,128]{1,0:T(8,128)(2,1)S(1)}, bf16[2048,128]{1,0:T(8,128)(2,1)S(1)}, u32[]{:S(2)}, u32[]{:S(2)}) collective-permute-start(bf16[2048,128]{1,0:T(8,128)(2,1)S(1)} %collective-permute-done.21.piece_ref), channel_id=1, source_target_pairs={{0,16},{8,24},{16,0},{24,8},{1,17},{9,25},{17,1},{25,9},{2,18},{10... | collective-permute-start | bytes 1572872 | tf_op jit(solution)/shard_map/ppermute | solution.py:29
  127.6 0.6 collective-permute-start.20
  128.2 2.0 %collective-permute-done.18.piece_ref = bf16[2048,128]{1,0:T(8,128)(2,1)S(1)} collective-permute-done((bf16[2048,128]{1,0:T(8,128)(2,1)}, bf16[2048,128]{1,0:T(8,128)(2,1)S(1)}, u32[]{:S(2)}, u32[]{:S(2)}) %collective-permute-start.18) | collective-permute-done | bytes 524320 | tf_op jit(solution)/shard_map/ppermute | solution.py:29
  130.2 0.1 collective-permute-start.19
  130.3 1.6 fusion.4
  131.9 2.0 %place.6.whole_ref = f32[2,64,128,128]{3,2,1,0:T(8,128)} custom-call(s32[1]{0:T(128)S(6)} %xor.33.where, bf16[2048,128]{1,0:T(8,128)(2,1)} %copy-done.6, f32[2,64,128,128]{3,2,1,0:T(8,128)} %get-tuple-element.18.whole_ref), custom_call_target="tpu_custom_call", output_to_operand_aliasing={{}: (2, {})} | custom-call | tf_op jit(solution)/shard_map/place/pallas_call | solution.py:426
  133.9 7.6 %collective-permute-done.23.piece_ref = bf16[2048,128]{1,0:T(8,128)(2,1)S(1)} collective-permute-done((bf16[2048,128]{1,0:T(8,128)(2,1)}, bf16[2048,128]{1,0:T(8,128)(2,1)S(1)}, u32[]{:S(2)}, u32[]{:S(2)}) %collective-permute-start.23) | collective-permute-done | bytes 524320 | tf_op jit(solution)/shard_map/ppermute | solution.py:29
  141.5 0.8 copy-done.9
  142.3 2.0 %place.7.whole_ref = f32[2,64,128,128]{3,2,1,0:T(8,128)} custom-call(s32[1]{0:T(128)S(6)} %xor.34.where, bf16[2048,128]{1,0:T(8,128)(2,1)} %copy-done.9, f32[2,64,128,128]{3,2,1,0:T(8,128)} %place.6.whole_ref), custom_call_target="tpu_custom_call", output_to_operand_aliasing={{}: (2, {})} | custom-call | tf_op jit(solution)/shard_map/place/pallas_call | solution.py:426
  144.2 7.6 %collective-permute-done.22.piece_ref = bf16[2048,128]{1,0:T(8,128)(2,1)S(1)} collective-permute-done((bf16[2048,128]{1,0:T(8,128)(2,1)S(1)}, bf16[2048,128]{1,0:T(8,128)(2,1)S(1)}, u32[]{:S(2)}, u32[]{:S(2)}) %collective-permute-start.22) | collective-permute-done | bytes 524320 | tf_op jit(solution)/shard_map/ppermute | solution.py:29
  151.8 0.8 copy-done.10
  152.6 2.0 %place.8.whole_ref = f32[2,64,128,128]{3,2,1,0:T(8,128)} custom-call(s32[1]{0:T(128)S(6)} %xor.29.where, bf16[2048,128]{1,0:T(8,128)(2,1)} %copy-done.10, f32[2,64,128,128]{3,2,1,0:T(8,128)} %place.7.whole_ref), custom_call_target="tpu_custom_call", output_to_operand_aliasing={{}: (2, {})} | custom-call | tf_op jit(solution)/shard_map/place/pallas_call | solution.py:426
  154.6 2.0 %place.9.whole_ref = f32[2,64,128,128]{3,2,1,0:T(8,128)} custom-call(s32[1]{0:T(128)S(6)} %xor.34.where, bf16[2048,128]{1,0:T(8,128)(2,1)} %copy-done.5, f32[2,64,128,128]{3,2,1,0:T(8,128)} %place.8.whole_ref), custom_call_target="tpu_custom_call", output_to_operand_aliasing={{}: (2, {})} | custom-call | tf_op jit(solution)/shard_map/place/pallas_call | solution.py:426
  156.5 0.8 copy-done.8
  157.3 2.0 %place.10.whole_ref = f32[2,64,128,128]{3,2,1,0:T(8,128)} custom-call(s32[1]{0:T(128)S(6)} %xor.33.where, bf16[2048,128]{1,0:T(8,128)(2,1)} %copy-done.8, f32[2,64,128,128]{3,2,1,0:T(8,128)} %place.9.whole_ref), custom_call_target="tpu_custom_call", output_to_operand_aliasing={{}: (2, {})} | custom-call | tf_op jit(solution)/shard_map/place/pallas_call | solution.py:426
  159.3 0.8 copy-done.7
  160.1 2.0 %place.11 = f32[2,64,128,128]{3,2,1,0:T(8,128)} custom-call(s32[1]{0:T(128)S(6)} %xor.29.where, bf16[2048,128]{1,0:T(8,128)(2,1)} %copy-done.7, f32[2,64,128,128]{3,2,1,0:T(8,128)} %place.10.whole_ref), custom_call_target="tpu_custom_call", output_to_operand_aliasing={{}: (2, {})} | custom-call | tf_op jit(solution)/shard_map/place/pallas_call | solution.py:426
  (55 shorter events, 0.2 us)
Async XLA Ops:
  0.6 22.6 %collective-permute-start = (f32[2,2,64,128]{3,2,1,0:T(8,128)}, f32[2,2,64,128]{3,2,1,0:T(8,128)S(1)}, u32[]{:S(2)}, u32[]{:S(2)}) collective-permute-start(f32[2,2,64,128]{3,2,1,0:T(8,128)} %own_ref.1), channel_id=1, source_target_pairs={{1,0},{2,1},{3,2},{4,3},{5,4},{6,5},{7,6},{9,8},{10,9},{11,10},{12... | collective-permute-start | bytes 393224 | tf_op jit(solution)/shard_map/ppermute | solution.py:24
  2.6 20.7 %collective-permute-start.1 = (f32[2,2,64,128]{3,2,1,0:T(8,128)}, f32[2,2,64,128]{3,2,1,0:T(8,128)}, u32[]{:S(2)}, u32[]{:S(2)}) collective-permute-start(f32[2,2,64,128]{3,2,1,0:T(8,128)} %own_ref.1), channel_id=1, source_target_pairs={{2,0},{3,1},{4,2},{5,3},{6,4},{7,5},{10,8},{11,9},{12,10},{13,11},... | collective-permute-start | bytes 393224 | tf_op jit(solution)/shard_map/ppermute | solution.py:24
  14.4 29.9 %copy-start = (bf16[8,2,2,64,128]{4,3,2,1,0:T(8,128)(2,1)S(1)}, bf16[8,2,2,64,128]{4,3,2,1,0:T(8,128)(2,1)}, u32[]{:S(2)}) copy-start(bf16[8,2,2,64,128]{4,3,2,1,0:T(8,128)(2,1)} %project.1) | copy-start | bytes 1572868
  15.4 27.6 %collective-permute-start.4 = (bf16[4,2,2,64,128]{4,3,2,1,0:T(8,128)(2,1)S(1)}, bf16[4,2,2,64,128]{4,3,2,1,0:T(8,128)(2,1)S(1)}, u32[]{:S(2)}, u32[]{:S(2)}) collective-permute-start(bf16[4,2,2,64,128]{4,3,2,1,0:T(8,128)(2,1)S(1)} %slice.43), channel_id=1, source_target_pairs={{0,1},{1,0},{2,3},{3,2},{4,5},{5,4},{6,7},{7,6},{8,9},{9,8},{10,11... | collective-permute-start | bytes 786440 | tf_op jit(solution)/shard_map/ppermute | solution.py:29
  15.5 41.1 %copy-start.12 = (f32[2,2,64,128]{3,2,1,0:T(8,128)S(1)}, f32[2,2,64,128]{3,2,1,0:T(8,128)}, u32[]{:S(2)}) copy-start(f32[2,2,64,128]{3,2,1,0:T(8,128)} %param.12) | copy-start | bytes 393220
  15.5 41.1 %copy-start.21 = (f32[2,2,64,128]{3,2,1,0:T(8,128)S(1)}, f32[2,2,64,128]{3,2,1,0:T(8,128)}, u32[]{:S(2)}) copy-start(f32[2,2,64,128]{3,2,1,0:T(8,128)} %own_ref.1) | copy-start | bytes 393220
  19.3 63.4 %collective-permute-start.7 = (bf16[2,128,2048]{2,1,0:T(8,128)(2,1)}, bf16[2,128,2048]{2,1,0:T(8,128)(2,1)S(1)}, u32[]{:S(2)}, u32[]{:S(2)}) collective-permute-start(bf16[2,128,2048]{2,1,0:T(8,128)(2,1)} %get-tuple-element.23), channel_id=1, source_target_pairs={{0,8},{8,0},{16,24},{24,16},{1,9},{9,1},{17,25},{25,17},{2,10},{10... | collective-permute-start | bytes 3145736 | tf_op jit(solution)/shard_map/ppermute | solution.py:29
  21.9 60.7 %collective-permute-start.8 = (bf16[2,128,2048]{2,1,0:T(8,128)(2,1)}, bf16[2,128,2048]{2,1,0:T(8,128)(2,1)S(1)}, u32[]{:S(2)}, u32[]{:S(2)}) collective-permute-start(bf16[2,128,2048]{2,1,0:T(8,128)(2,1)} %get-tuple-element.22), channel_id=1, source_target_pairs={{0,16},{8,24},{16,0},{24,8},{1,17},{9,25},{17,1},{25,9},{2,18},{10... | collective-permute-start | bytes 3145736 | tf_op jit(solution)/shard_map/ppermute | solution.py:29
  23.2 0.7 copy-start.22
  23.2 59.5 %collective-permute-start.9 = (bf16[2,128,2048]{2,1,0:T(8,128)(2,1)}, bf16[2,128,2048]{2,1,0:T(8,128)(2,1)}, u32[]{:S(2)}, u32[]{:S(2)}) collective-permute-start(bf16[2,128,2048]{2,1,0:T(8,128)(2,1)} %get-tuple-element.21), channel_id=1, source_target_pairs={{0,24},{8,16},{16,8},{24,0},{1,25},{9,17},{17,9},{25,1},{2,26},{10... | collective-permute-start | bytes 3145736 | tf_op jit(solution)/shard_map/ppermute | solution.py:29
  32.8 11.8 %collective-permute-start.2 = (bf16[2,3,64,128]{3,2,1,0:T(8,128)(2,1)S(1)}, bf16[2,3,64,128]{3,2,1,0:T(8,128)(2,1)S(1)}, u32[]{:S(2)}, u32[]{:S(2)}) collective-permute-start(bf16[2,3,64,128]{3,2,1,0:T(8,128)(2,1)S(1)} %get-tuple-element.24), channel_id=1, source_target_pairs={{0,1},{1,2},{2,3},{3,4},{4,5},{5,6},{6,7},{8,9},{9,10},{10,11},{11... | collective-permute-start | bytes 294920 | tf_op jit(solution)/shard_map/ppermute | solution.py:24
  43.0 5.9 %collective-permute-start.3 = (bf16[2,3,64,128]{3,2,1,0:T(8,128)(2,1)S(1)}, bf16[2,3,64,128]{3,2,1,0:T(8,128)(2,1)S(1)}, u32[]{:S(2)}, u32[]{:S(2)}) collective-permute-start(bf16[2,3,64,128]{3,2,1,0:T(8,128)(2,1)S(1)} %get-tuple-element.25), channel_id=1, source_target_pairs={{0,2},{1,3},{2,4},{3,5},{4,6},{5,7},{8,10},{9,11},{10,12},{11,13},... | collective-permute-start | bytes 294920 | tf_op jit(solution)/shard_map/ppermute | solution.py:24
  44.6 7.5 %collective-permute-start.5 = (bf16[2,2,2,64,128]{4,3,2,1,0:T(8,128)(2,1)S(1)}, bf16[2,2,2,64,128]{4,3,2,1,0:T(8,128)(2,1)S(1)}, u32[]{:S(2)}, u32[]{:S(2)}) collective-permute-start(bf16[2,2,2,64,128]{4,3,2,1,0:T(8,128)(2,1)S(1)} %slice.45), channel_id=1, source_target_pairs={{0,2},{1,3},{2,0},{3,1},{4,6},{5,7},{6,4},{7,5},{8,10},{9,11},{10,... | collective-permute-start | bytes 393224 | tf_op jit(solution)/shard_map/ppermute | solution.py:29
  52.2 4.5 %collective-permute-start.6 = (bf16[1,2,2,64,128]{4,3,2,1,0:T(8,128)(2,1)S(1)}, bf16[1,2,2,64,128]{4,3,2,1,0:T(8,128)(2,1)S(1)}, u32[]{:S(2)}, u32[]{:S(2)}) collective-permute-start(bf16[1,2,2,64,128]{4,3,2,1,0:T(8,128)(2,1)S(1)} %slice.47), channel_id=1, source_target_pairs={{0,4},{1,5},{2,6},{3,7},{4,0},{5,1},{6,2},{7,3},{8,12},{9,13},{10,... | collective-permute-start | bytes 196616 | tf_op jit(solution)/shard_map/ppermute | solution.py:29
  56.6 5.8 %copy-start.15 = (bf16[1,2,2,64,128]{4,3,2,1,0:T(8,128)(2,1)}, bf16[1,2,2,64,128]{4,3,2,1,0:T(8,128)(2,1)S(1)}, u32[]{:S(2)}) copy-start(bf16[1,2,2,64,128]{4,3,2,1,0:T(8,128)(2,1)S(1)} %collective-permute-done.6) | copy-start | bytes 196612
  56.7 13.6 %copy-start.3 = (bf16[1,2,2,64,128]{4,3,2,1,0:T(8,128)(2,1)}, bf16[1,2,2,64,128]{4,3,2,1,0:T(8,128)(2,1)S(1)}, u32[]{:S(2)}) copy-start(bf16[1,2,2,64,128]{4,3,2,1,0:T(8,128)(2,1)S(1)} %get-tuple-element.19.refs_0_) | copy-start | bytes 196612
  56.7 73.6 %copy-start.13 = (f32[2,2,64,128]{3,2,1,0:T(8,128)}, f32[2,2,64,128]{3,2,1,0:T(8,128)S(1)}, u32[]{:S(2)}) copy-start(f32[2,2,64,128]{3,2,1,0:T(8,128)S(1)} %get-tuple-element.20) | copy-start | bytes 393220
  56.7 4.5 %collective-permute-start.10 = (bf16[1,2,2,64,128]{4,3,2,1,0:T(8,128)(2,1)S(1)}, bf16[1,2,2,64,128]{4,3,2,1,0:T(8,128)(2,1)S(1)}, u32[]{:S(2)}, u32[]{:S(2)}) collective-permute-start(bf16[1,2,2,64,128]{4,3,2,1,0:T(8,128)(2,1)S(1)} %get-tuple-element.19.refs_0_), channel_id=1, source_target_pairs={{0,4},{1,5},{2,6},{3,7},{4,0},{5,1},{6,2},{7,3},{8,12},{9,13},{10,... | collective-permute-start | bytes 196616 | tf_op jit(solution)/shard_map/ppermute | solution.py:29
  61.2 9.1 %copy-start.4 = (bf16[1,2,2,64,128]{4,3,2,1,0:T(8,128)(2,1)}, bf16[1,2,2,64,128]{4,3,2,1,0:T(8,128)(2,1)S(1)}, u32[]{:S(2)}) copy-start(bf16[1,2,2,64,128]{4,3,2,1,0:T(8,128)(2,1)S(1)} %collective-permute-done.10.refs_1_) | copy-start | bytes 196612
  61.2 4.3 %collective-permute-start.11 = (bf16[2,2,2,64,128]{4,3,2,1,0:T(8,128)(2,1)S(1)}, bf16[2,2,2,64,128]{4,3,2,1,0:T(8,128)(2,1)S(1)}, u32[]{:S(2)}, u32[]{:S(2)}) collective-permute-start(bf16[2,2,2,64,128]{4,3,2,1,0:T(8,128)(2,1)S(1)} %pad_maximum_fusion.1), channel_id=1, source_target_pairs={{0,2},{1,3},{2,0},{3,1},{4,6},{5,7},{6,4},{7,5},{8,10},{9,11},{10,... | collective-permute-start | bytes 393224 | tf_op jit(solution)/shard_map/ppermute | solution.py:29
  65.5 4.8 %copy-start.11 = (bf16[2,2,2,64,128]{4,3,2,1,0:T(8,128)(2,1)}, bf16[2,2,2,64,128]{4,3,2,1,0:T(8,128)(2,1)S(1)}, u32[]{:S(2)}) copy-start(bf16[2,2,2,64,128]{4,3,2,1,0:T(8,128)(2,1)S(1)} %collective-permute-done.11.refs_2_) | copy-start | bytes 393220
  65.6 4.7 %collective-permute-start.12 = (bf16[4,2,2,64,128]{4,3,2,1,0:T(8,128)(2,1)S(1)}, bf16[4,2,2,64,128]{4,3,2,1,0:T(8,128)(2,1)S(1)}, u32[]{:S(2)}, u32[]{:S(2)}) collective-permute-start(bf16[4,2,2,64,128]{4,3,2,1,0:T(8,128)(2,1)S(1)} %pad_maximum_fusion), channel_id=1, source_target_pairs={{0,1},{1,0},{2,3},{3,2},{4,5},{5,4},{6,7},{7,6},{8,9},{9,8},{10,11... | collective-permute-start | bytes 786440 | tf_op jit(solution)/shard_map/ppermute | solution.py:29
  70.3 0.7 copy-start.14
  72.8 4.9 %collective-permute-start.13 = (bf16[2,2,128,128]{3,2,1,0:T(8,128)(2,1)}, bf16[2,2,128,128]{3,2,1,0:T(8,128)(2,1)S(1)}, u32[]{:S(2)}, u32[]{:S(2)}) collective-permute-start(bf16[2,2,128,128]{3,2,1,0:T(8,128)(2,1)} %cut.1.refs_4_), channel_id=1, source_target_pairs={{0,8},{8,0},{16,24},{24,16},{1,9},{9,1},{17,25},{25,17},{2,10},{10... | collective-permute-start | bytes 393224 | tf_op jit(solution)/shard_map/ppermute | solution.py:29
  72.8 4.9 %collective-permute-start.14 = (bf16[2,2,128,128]{3,2,1,0:T(8,128)(2,1)}, bf16[2,2,128,128]{3,2,1,0:T(8,128)(2,1)S(1)}, u32[]{:S(2)}, u32[]{:S(2)}) collective-permute-start(bf16[2,2,128,128]{3,2,1,0:T(8,128)(2,1)} %cut.1.refs_4_), channel_id=1, source_target_pairs={{0,16},{8,24},{16,0},{24,8},{1,17},{9,25},{17,1},{25,9},{2,18},{10... | collective-permute-start | bytes 393224 | tf_op jit(solution)/shard_map/ppermute | solution.py:29
  77.7 5.0 %copy-start.16 = (bf16[2,2,128,128]{3,2,1,0:T(8,128)(2,1)}, bf16[2,2,128,128]{3,2,1,0:T(8,128)(2,1)S(1)}, u32[]{:S(2)}) copy-start(bf16[2,2,128,128]{3,2,1,0:T(8,128)(2,1)S(1)} %collective-permute-done.13.refs_5_) | copy-start | bytes 393220
  77.7 4.9 %collective-permute-start.15 = (bf16[2,2,128,128]{3,2,1,0:T(8,128)(2,1)}, bf16[2,2,128,128]{3,2,1,0:T(8,128)(2,1)S(1)}, u32[]{:S(2)}, u32[]{:S(2)}) collective-permute-start(bf16[2,2,128,128]{3,2,1,0:T(8,128)(2,1)} %cut.1.refs_4_), channel_id=1, source_target_pairs={{0,24},{8,16},{16,8},{24,0},{1,25},{9,17},{17,9},{25,1},{2,26},{10... | collective-permute-start | bytes 393224 | tf_op jit(solution)/shard_map/ppermute | solution.py:29
  77.7 5.0 %copy-start.17 = (bf16[2,2,128,128]{3,2,1,0:T(8,128)(2,1)}, bf16[2,2,128,128]{3,2,1,0:T(8,128)(2,1)S(1)}, u32[]{:S(2)}) copy-start(bf16[2,2,128,128]{3,2,1,0:T(8,128)(2,1)S(1)} %collective-permute-done.14.refs_6_) | copy-start | bytes 393220
  82.6 0.7 copy-start.18
  82.6 1.0 copy-start.1
  82.6 1.4 copy-start.2
  90.4 7.4 %collective-permute-start.16 = (f32[2,1,128,128]{3,2,1,0:T(8,128)}, f32[2,1,128,128]{3,2,1,0:T(8,128)S(1)}, u32[]{:S(2)}, u32[]{:S(2)}) collective-permute-start(f32[2,1,128,128]{3,2,1,0:T(8,128)} %get-tuple-element.14), channel_id=1, source_target_pairs={{0,8},{8,16},{16,24},{24,1},{1,9},{9,17},{17,25},{25,2},{2,10},{10... | collective-permute-start | bytes 393224 | tf_op jit(solution)/shard_map/ppermute | solution.py:521
  92.6 7.2 %collective-permute-start.17 = (f32[2,1,128,128]{3,2,1,0:T(8,128)}, f32[2,1,128,128]{3,2,1,0:T(8,128)S(1)}, u32[]{:S(2)}, u32[]{:S(2)}) collective-permute-start(f32[2,1,128,128]{3,2,1,0:T(8,128)} %get-tuple-element.15), channel_id=1, source_target_pairs={{8,0},{16,8},{24,16},{1,24},{9,1},{17,9},{25,17},{2,25},{10,2},{18... | collective-permute-start | bytes 393224 | tf_op jit(solution)/shard_map/ppermute | solution.py:522
  97.8 2.0 %copy-start.19 = (f32[2,1,128,128]{3,2,1,0:T(8,128)}, f32[2,1,128,128]{3,2,1,0:T(8,128)S(1)}, u32[]{:S(2)}) copy-start(f32[2,1,128,128]{3,2,1,0:T(8,128)S(1)} %collective-permute-done.16.before_ref) | copy-start | bytes 393220
  99.8 0.7 copy-start.20
  110.7 11.4 %collective-permute-start.21 = (bf16[2048,128]{1,0:T(8,128)(2,1)}, bf16[2048,128]{1,0:T(8,128)(2,1)S(1)}, u32[]{:S(2)}, u32[]{:S(2)}) collective-permute-start(bf16[2048,128]{1,0:T(8,128)(2,1)} %get-tuple-element.17), channel_id=1, source_target_pairs={{0,8},{8,0},{16,24},{24,16},{1,9},{9,1},{17,25},{25,17},{2,10},{10... | collective-permute-start | bytes 1572872 | tf_op jit(solution)/shard_map/ppermute | solution.py:29
  111.2 19.0 %collective-permute-start.18 = (bf16[2048,128]{1,0:T(8,128)(2,1)}, bf16[2048,128]{1,0:T(8,128)(2,1)S(1)}, u32[]{:S(2)}, u32[]{:S(2)}) collective-permute-start(bf16[2048,128]{1,0:T(8,128)(2,1)} %get-tuple-element.16), channel_id=1, source_target_pairs={{0,16},{8,24},{16,0},{24,8},{1,17},{9,25},{17,1},{25,9},{2,18},{10... | collective-permute-start | bytes 1572872 | tf_op jit(solution)/shard_map/ppermute | solution.py:29
  117.6 23.9 %collective-permute-start.23 = (bf16[2048,128]{1,0:T(8,128)(2,1)}, bf16[2048,128]{1,0:T(8,128)(2,1)S(1)}, u32[]{:S(2)}, u32[]{:S(2)}) collective-permute-start(bf16[2048,128]{1,0:T(8,128)(2,1)} %get-tuple-element.17), channel_id=1, source_target_pairs={{0,16},{8,24},{16,0},{24,8},{1,17},{9,25},{17,1},{25,9},{2,18},{10... | collective-permute-start | bytes 1572872 | tf_op jit(solution)/shard_map/ppermute | solution.py:29
  122.0 9.9 %copy-start.6 = (bf16[2048,128]{1,0:T(8,128)(2,1)}, bf16[2048,128]{1,0:T(8,128)(2,1)S(1)}, u32[]{:S(2)}) copy-start(bf16[2048,128]{1,0:T(8,128)(2,1)S(1)} %collective-permute-done.21.piece_ref) | copy-start | bytes 1572868
  122.0 29.8 %collective-permute-start.22 = (bf16[2048,128]{1,0:T(8,128)(2,1)S(1)}, bf16[2048,128]{1,0:T(8,128)(2,1)S(1)}, u32[]{:S(2)}, u32[]{:S(2)}) collective-permute-start(bf16[2048,128]{1,0:T(8,128)(2,1)S(1)} %collective-permute-done.21.piece_ref), channel_id=1, source_target_pairs={{0,16},{8,24},{16,0},{24,8},{1,17},{9,25},{17,1},{25,9},{2,18},{10... | collective-permute-start | bytes 1572872 | tf_op jit(solution)/shard_map/ppermute | solution.py:29
  127.6 28.9 %collective-permute-start.20 = (bf16[2048,128]{1,0:T(8,128)(2,1)}, bf16[2048,128]{1,0:T(8,128)(2,1)S(1)}, u32[]{:S(2)}, u32[]{:S(2)}) collective-permute-start(bf16[2048,128]{1,0:T(8,128)(2,1)} %get-tuple-element.16), channel_id=1, source_target_pairs={{0,8},{8,0},{16,24},{24,16},{1,9},{9,1},{17,25},{25,17},{2,10},{10... | collective-permute-start | bytes 1572872 | tf_op jit(solution)/shard_map/ppermute | solution.py:29
  130.2 3.6 %copy-start.5 = (bf16[2048,128]{1,0:T(8,128)(2,1)}, bf16[2048,128]{1,0:T(8,128)(2,1)S(1)}, u32[]{:S(2)}) copy-start(bf16[2048,128]{1,0:T(8,128)(2,1)S(1)} %collective-permute-done.18.piece_ref) | copy-start | bytes 1572868
  130.2 29.0 %collective-permute-start.19 = (bf16[2048,128]{1,0:T(8,128)(2,1)S(1)}, bf16[2048,128]{1,0:T(8,128)(2,1)S(1)}, u32[]{:S(2)}, u32[]{:S(2)}) collective-permute-start(bf16[2048,128]{1,0:T(8,128)(2,1)S(1)} %collective-permute-done.18.piece_ref), channel_id=1, source_target_pairs={{0,8},{8,0},{16,24},{24,16},{1,9},{9,1},{17,25},{25,17},{2,10},{10... | collective-permute-start | bytes 1572872 | tf_op jit(solution)/shard_map/ppermute | solution.py:29
  141.5 0.8 copy-start.9
  151.8 0.8 copy-start.10
  156.5 0.8 copy-start.8
  159.3 0.8 copy-start.7

commit v2 on v1

v2 whole, which is shorter than its diff:
```python
import functools
import numpy as np
import jax
import jax.numpy as jnp
from jax import lax
from jax.experimental import pallas as pl
from jax.experimental.pallas import tpu as pltpu
from jax.sharding import PartitionSpec as P


rho_weight = 0.5
step_size = 0.5
prior_weight = 0.5
floor_term = 0.25


F32 = jnp.float32
BF16 = jnp.bfloat16
VMEM = pltpu.VMEM
SMEM = pltpu.SMEM


def passed_along(value, axis, steps):
    count = lax.axis_size(axis)
    initial, last = (max(0, -steps), min(count, count - steps))
    return lax.ppermute(value, axis, [(source, source + steps) for source in range(initial, last)])


def near(*arrays):
    return tuple(pltpu.with_memory_space_constraint(array, VMEM) for array in arrays)


def limit(mebibytes):
    return pltpu.CompilerParams(vmem_limit_bytes=mebibytes << 20)


def swapped(value, axis, mask):
    count = lax.axis_size(axis)
    return lax.ppermute(value, axis, [(i, i ^ mask) for i in range(count)])


def masks_of(count):
    return [1 << b for b in range(count.bit_length() - 1)]


def dft_block(order_n, inverse):
    counter = np.arange(order_n)
    angles = (counter[:, None] * counter[None, :] % order_n) * (2.0 * np.pi / order_n)
    re = np.cos(angles) / np.sqrt(order_n)
    im = -np.sin(angles) / np.sqrt(order_n)
    im = -im if inverse else im
    return jnp.asarray(np.block([[re, -im], [im, re]]).astype(np.float32)).astype(BF16)


def deal_kernel(weights_ref, *refs):
    *shares, sems = refs
    group = lax.axis_index("view")
    copies = []
    for j, ref in list(enumerate(shares))[1:] + [(0, shares[0])]:
        size = ref.shape[2]
        first = pl.multiple_of((group ^ j) * size, size)
        copies.append(
            pltpu.make_async_copy(weights_ref.at[:, :, pl.ds(first, size)], ref, sems.at[j])
        )
        copies[-1].start()
    for copy in copies:
        copy.wait()


def deal(weights, groups):
    views, cols, voxels = weights.shape
    vmem = pl.BlockSpec(memory_space=VMEM)
    return pl.pallas_call(
        deal_kernel,
        out_shape=(VMEM((views, cols, voxels // groups), BF16),) * groups,
        in_specs=[pl.BlockSpec(memory_space=pl.ANY)],
        out_specs=(vmem,) * groups,
        scratch_shapes=[pltpu.SemaphoreType.DMA((groups,))],
        compiler_params=limit(8),
        name="deal",
    )(pltpu.with_memory_space_constraint(weights, pltpu.HBM))


def ranks(footprints, views, parts, tiles):
    tile = lax.axis_index("tile")
    found = []
    for v in range(views):
        row = []
        for part in range(parts):
            other = (footprints[v] + part) ^ tile
            row.append((other >> 1) + (other & 1) * (tiles // 2))
        found.append(row)
    return found


def project_kernel(footprints, volume_ref, *refs):
    *shares, keep_ref, send_ref, part_ref = refs
    views, cols, size = shares[0].shape
    _, count, _, rows = part_ref.shape
    half, _, _, width, _ = keep_ref.shape
    group = lax.axis_index("view")
    keep_ref[...] = jnp.zeros_like(keep_ref)
    send_ref[...] = jnp.zeros_like(send_ref)
    part_ref[...] = volume_ref[:, pl.ds(group * count, count)]
    total = jnp.zeros((views * cols, 2 * rows), F32)
    for j, ref in enumerate(shares):
        first = (group ^ j) * count
        low = jnp.concatenate(
            [volume_ref[k, pl.ds(first, count)].reshape(size, rows).astype(BF16) for k in range(2)],
            axis=1,
        )
        total = total + jnp.dot(
            ref[...].reshape(views * cols, size), low, preferred_element_type=F32
        )
    spots = ranks(footprints, views, cols // width, 2 * half)
    for v in range(views):
        for part in range(cols // width):
            first = v * cols + part * width
            spot = spots[v][part]
            for ref, wanted, index in (
                (keep_ref, spot < half, spot),
                (send_ref, spot >= half, spot - half),
            ):

                @pl.when(wanted)
                def _():
                    for k in range(2):
                        ref[index, v, k] = total[
                            first : first + width, k * rows : (k + 1) * rows
                        ].astype(BF16)


def project(footprints, shares, volume, tiles, tile_cols):
    groups = len(shares)
    views, _, _ = shares[0].shape
    _, vcols, depth, rows = volume.shape
    vmem = pl.BlockSpec(memory_space=VMEM)
    placed = VMEM((tiles // 2, views, 2, tile_cols, rows), BF16)
    return pl.pallas_call(
        project_kernel,
        out_shape=(placed, placed, VMEM((2, vcols // groups, depth, rows), F32)),
        in_specs=[pl.BlockSpec(memory_space=SMEM)] + [vmem] * (groups + 1),
        out_specs=(vmem,) * 3,
        compiler_params=limit(16),
        name="project",
    )(footprints, *near(volume, *shares))


def fold_kernel(keep_ref, arrived_ref, *refs):
    for n, ref in enumerate(refs):
        ref[...] = (keep_ref[n].astype(F32) + arrived_ref[n].astype(F32)).astype(ref.dtype)


def fold(keep, arrived):
    vmem = pl.BlockSpec(memory_space=VMEM)
    return pl.pallas_call(
        fold_kernel,
        out_shape=tuple(VMEM(keep.shape[1:], BF16 if n else F32) for n in range(keep.shape[0])),
        in_specs=[vmem] * 2,
        out_specs=(vmem,) * keep.shape[0],
        compiler_params=limit(8),
        name="fold",
    )(*near(keep, arrived))


GROUP = 4


def patch_kernel(
    positions,
    live,
    own_ref,
    one_ref,
    two_ref,
    probe_ref,
    forward_ref,
    inverse_ref,
    counts_ref,
    token_ref,
    near_ref,
    ahead_one_ref,
    ahead_two_ref,
    reach,
    total,
    buffer,
    sems,
):
    views, _, width, rows = own_ref.shape
    cols = probe_ref.shape[1]
    span = 3 * width
    for part, ref in enumerate((own_ref, one_ref, two_ref)):
        reach[:, :, part * width : (part + 1) * width, :] = ref[...]
    total[...] = jnp.zeros_like(total)
    starts = [0]
    for v in range(views):
        starts.append(starts[-1] + lax.div(live[v] + (GROUP - 1), GROUP))

    def located(step):
        view, first = 0, 0
        for v in range(1, views):
            after = (step >= starts[v]).astype(jnp.int32)
            view = view + after
            first = jnp.where(after == 1, starts[v], first)
        return view, (step - first) * GROUP

    def fetch(step, slot):
        view, first = located(step)
        return pltpu.make_async_copy(
            counts_ref.at[view, pl.ds(first, GROUP)], buffer.at[slot], sems.at[slot]
        )

    fetch(0, 0).start()

    def body(step, carry):
        slot = step & 1
        view, first = located(step)
        pltpu.make_async_copy(
            counts_ref.at[view, pl.ds(first, GROUP)], buffer.at[slot], sems.at[slot]
        ).wait()

        @pl.when(step + 1 < starts[views])
        def _():
            fetch(step + 1, 1 - slot).start()

        probe_re = probe_ref[0]
        probe_im = probe_ref[1]
        spots = []
        exits = []
        for g in range(GROUP):
            offset = positions[view, first + g]
            spots.append(jnp.where(first + g < live[view], offset, span))
            obj_re = reach[view, 0, pl.ds(offset, cols), :]
            obj_im = reach[view, 1, pl.ds(offset, cols), :]
            wave_re = (probe_re * obj_re - probe_im * obj_im).astype(BF16)
            wave_im = (probe_re * obj_im + probe_im * obj_re).astype(BF16)
            exits.append(jnp.concatenate([wave_re, wave_im], axis=0))
        waves = jnp.concatenate(exits, axis=1)
        done = jnp.dot(forward_ref[...], waves, preferred_element_type=F32).astype(BF16)
        done = jnp.concatenate(
            [
                jnp.concatenate(
                    [
                        done[:cols, g * rows : (g + 1) * rows],
                        done[cols:, g * rows : (g + 1) * rows],
                    ],
                    axis=1,
                )
                for g in range(GROUP)
            ],
            axis=0,
        )
        spectrum = jnp.dot(done, inverse_ref[...], preferred_element_type=F32)
        spec_re = spectrum[:, :rows]
        spec_im = spectrum[:, rows:]
        counts = buffer[slot].reshape(GROUP * cols, rows).astype(F32)
        square = spec_re * spec_re + spec_im * spec_im + floor_term
        factor = (counts * (1.0 / 16.0)) * lax.rsqrt(jnp.maximum(counts * square, 1e-6))
        replaced = jnp.concatenate(
            [(spec_re * factor).astype(BF16), (spec_im * factor).astype(BF16)], axis=1
        )
        back = jnp.dot(replaced, forward_ref[...], preferred_element_type=F32).astype(BF16)
        back = jnp.concatenate(
            [
                jnp.concatenate(
                    [
                        back[g * cols : (g + 1) * cols, :rows],
                        back[g * cols : (g + 1) * cols, rows:],
                    ],
                    axis=0,
                )
                for g in range(GROUP)
            ],
            axis=1,
        )
        wave = jnp.dot(inverse_ref[...], back, preferred_element_type=F32)
        power = probe_re * probe_re + probe_im * probe_im
        for g in range(GROUP):
            diff = wave[:, g * rows : (g + 1) * rows] - exits[g].astype(F32)
            diff_re = diff[:cols]
            diff_im = diff[cols:]
            place = pl.ds(spots[g], cols)
            total[view, 0, place, :] += probe_re * diff_re + probe_im * diff_im
            total[view, 1, place, :] += probe_re * diff_im - probe_im * diff_re
            total[view, 2, place, :] += power
        return carry

    lax.fori_loop(0, starts[views], body, 0)
    near_ref[...] = total[:, :, :width, :]
    for part, ref in ((1, ahead_one_ref), (2, ahead_two_ref)):
        ref[...] = total[:, :, part * width : (part + 1) * width, :].astype(BF16)


def patches(positions, live, own, one, two, probe, forward, inverse, counts, token):
    views, _, width, rows = own.shape
    cols = probe.shape[1]
    slots = counts.shape[1]
    vmem = pl.BlockSpec(memory_space=VMEM)
    smem = pl.BlockSpec(memory_space=SMEM)
    return pl.pallas_call(
        patch_kernel,
        out_shape=(
            VMEM((views, 3, width, rows), F32),
            VMEM((views, 3, width, rows), BF16),
            VMEM((views, 3, width, rows), BF16),
        ),
        in_specs=[smem, smem] + [vmem] * 6 + [pl.BlockSpec(memory_space=pl.ANY)] * 2,
        out_specs=(vmem, vmem, vmem),
        scratch_shapes=[
            VMEM((views, 2, 3 * width, rows), F32),
            VMEM((views, 3, 3 * width + cols, rows), F32),
            VMEM((2, GROUP, cols, rows), jnp.int32),
            pltpu.SemaphoreType.DMA((2,)),
        ],
        compiler_params=limit(20),
        cost_estimate=pl.CostEstimate(
            flops=views * slots * 16 * cols * cols * rows,
            transcendentals=0,
            bytes_accessed=counts.size * 4,
        ),
        name="patches",
    )(positions, live, own, *near(one, two), probe, forward, inverse, counts, *near(token))


def cut_kernel(tiles, footprints, *refs):
    pieces, windows_ref = refs[:-1], refs[-1]
    views, _, cols, _ = windows_ref.shape
    width = pieces[0].shape[3]
    spots = ranks(footprints, views, cols // width, tiles)
    for v in range(views):
        for part in range(cols // width):
            first = 0
            for ref in pieces:
                inside = spots[v][part] - first

                @pl.when((inside >= 0) & (inside < ref.shape[0]))
                def _():
                    windows_ref[v, :, part * width : (part + 1) * width] = ref[inside, v]

                first += ref.shape[0]


def cut(footprints, pieces, cols, tiles):
    _, views, planes, _, rows = pieces[0].shape
    vmem = pl.BlockSpec(memory_space=VMEM)
    return pl.pallas_call(
        functools.partial(cut_kernel, tiles),
        out_shape=VMEM((views, planes, cols, rows), BF16),
        in_specs=[pl.BlockSpec(memory_space=SMEM)] + [vmem] * len(pieces),
        out_specs=vmem,
        compiler_params=limit(8),
        name="cut",
    )(footprints, *near(*pieces))


def bent(d):
    return d * lax.rsqrt(1.0 + d * d)


def settled(here, behind, ahead):
    depth, rows = here.shape
    lane = lax.broadcasted_iota(jnp.int32, (depth, rows), 1)
    level = lax.broadcasted_iota(jnp.int32, (depth, rows), 0)
    prior = ahead - behind
    beyond = jnp.where(lane == rows - 1, 0.0, pltpu.roll(here, rows - 1, 1))
    pair = bent(here - beyond)
    prior = prior + pair - jnp.where(lane == 0, -bent(here), pltpu.roll(pair, 1, 1))
    beyond = jnp.where(level == depth - 1, 0.0, pltpu.roll(here, depth - 1, 0))
    pair = bent(here - beyond)
    prior = prior + pair - jnp.where(level == 0, -bent(here[:1]), pltpu.roll(pair, 1, 0))
    return here - step_size * prior_weight * prior


def run_of_columns(half_ref, k, first, count, final, store):
    before = half_ref[k, first - 1]
    here = half_ref[k, first]

    def body(i, carry):
        behind, here = carry
        following = half_ref[k, first + i + 1]
        ahead = bent(here - following)
        store(i, settled(here, behind, ahead))
        return ahead, following

    inner = count if final is None else count - 1
    behind, here = lax.fori_loop(0, inner, body, (bent(before - here), here), unroll=2)
    if final is not None:
        store(count - 1, settled(here, behind, bent(here - final)))


def gradient_kernel(groups, pieces, *refs):
    weight_refs = refs[:groups]
    window_refs = refs[groups : 2 * groups]
    volume_ref, half_ref, low_ref, high_ref = refs[2 * groups :]
    _, share, depth, rows = half_ref.shape
    views, cols, _ = weight_refs[0].shape
    chunk = share // pieces
    span = chunk * depth
    windows = [
        jnp.concatenate(
            [jnp.concatenate([ref[v, 0], ref[v, 1]], axis=1) for v in range(views)], axis=0
        )
        for ref in window_refs
    ]
    for i in range(pieces):
        gradient = None
        for g in range(groups):
            product = lax.dot_general(
                weight_refs[g][:, :, i * span : (i + 1) * span].reshape(views * cols, span),
                windows[g],
                (((0,), (0,)), ((), ())),
                preferred_element_type=F32,
            )
            gradient = product if gradient is None else gradient + product
        for k in range(2):
            plane = gradient[:, k * rows : (k + 1) * rows].reshape(chunk, depth, rows)
            held = slice(i * chunk, (i + 1) * chunk)
            half_ref[k, held] = volume_ref[k, held] - step_size * plane
    low_ref[...] = half_ref[:, :1].astype(BF16)
    high_ref[...] = half_ref[:, share - 1 :].astype(BF16)


def half_step_of(weights, windows, volume):
    groups = len(windows)
    _, share, depth, rows = volume.shape
    vmem = pl.BlockSpec(memory_space=VMEM)
    edge = VMEM((2, 1, depth, rows), BF16)
    return pl.pallas_call(
        functools.partial(gradient_kernel, groups, min(4, share)),
        out_shape=(VMEM((2, share, depth, rows), F32), edge, edge),
        in_specs=[vmem] * (2 * groups + 1),
        out_specs=(vmem, vmem, vmem),
        compiler_params=limit(20),
        name="half_step",
    )(*near(*weights, *windows, volume))


def first_kernel(half_ref, part_ref, whole_ref, fresh, sems):
    group = lax.axis_index("view")
    share = half_ref.shape[1]
    puts = []
    for k in range(2):

        def store(i, column):
            fresh[k, i] = column
            part_ref[k, i] = column.astype(BF16)

        run_of_columns(half_ref, k, 1, share // 2, None, store)
        puts.append(
            pltpu.make_async_copy(
                fresh.at[k],
                whole_ref.at[k, pl.ds(group * share + 1, share // 2)],
                sems.at[k],
            )
        )
        puts[-1].start()
    for put in puts:
        put.wait()


def first_part(half, vcols):
    _, share, depth, rows = half.shape
    hbm = pl.BlockSpec(memory_space=pl.ANY)
    vmem = pl.BlockSpec(memory_space=VMEM)
    return pl.pallas_call(
        first_kernel,
        out_shape=(
            VMEM((2, share // 2, depth, rows), BF16),
            jax.ShapeDtypeStruct((2, vcols, depth, rows), F32),
        ),
        in_specs=[vmem],
        out_specs=(vmem, hbm),
        scratch_shapes=[
            VMEM((2, share // 2, depth, rows), F32),
            pltpu.SemaphoreType.DMA((2,)),
        ],
        compiler_params=limit(16),
        name="first_part",
    )(*near(half))


def second_kernel(half_ref, before_ref, after_ref, _, part_ref, whole_ref, fresh, sems):
    group = lax.axis_index("view")
    share = half_ref.shape[1]
    middle = share // 2
    puts = []
    for k in range(2):

        def store(i, column):
            fresh[k, i + 1] = column
            part_ref[k, i + 1] = column.astype(BF16)

        here = half_ref[k, 0]
        column = settled(here, bent(before_ref[k, 0].astype(F32) - here), bent(here - half_ref[k, 1]))
        store(-1, column)
        run_of_columns(half_ref, k, middle + 1, middle - 1, after_ref[k, 0].astype(F32), store)
        for place, (source, target, count) in enumerate(
            ((0, 0, 1), (1, middle + 1, middle - 1))
        ):
            puts.append(
                pltpu.make_async_copy(
                    fresh.at[k, pl.ds(source, count)],
                    whole_ref.at[k, pl.ds(group * share + target, count)],
                    sems.at[k, place],
                )
            )
            puts[-1].start()
    for put in puts:
        put.wait()


def second_part(half, before, after, whole):
    _, share, depth, rows = half.shape
    hbm = pl.BlockSpec(memory_space=pl.ANY)
    vmem = pl.BlockSpec(memory_space=VMEM)
    return pl.pallas_call(
        second_kernel,
        out_shape=(
            VMEM((2, share // 2, depth, rows), BF16),
            jax.ShapeDtypeStruct(whole.shape, F32),
        ),
        in_specs=[vmem, vmem, vmem, hbm],
        out_specs=(vmem, hbm),
        scratch_shapes=[
            VMEM((2, share // 2, depth, rows), F32),
            pltpu.SemaphoreType.DMA((2, 2)),
        ],
        input_output_aliases={3: 1},
        compiler_params=limit(16),
        name="second_part",
    )(*near(half, before, after), whole)


def place_kernel(kinds, groups, *refs):
    parts = refs[: len(kinds)]
    _, whole_ref, fresh, sems = refs[len(kinds) :]
    group = lax.axis_index("view")
    share = whole_ref.shape[1] // groups
    middle = share // 2
    puts = []
    for n, ((second, j), ref) in enumerate(zip(kinds, parts)):
        first = (group ^ j) * share
        runs = ((0, 0, 1), (1, middle + 1, middle - 1)) if second else ((0, 1, middle),)
        for place, (source, target, count) in enumerate(runs):
            for k in range(2):
                fresh[n, k, source : source + count] = ref[k, source : source + count].astype(F32)
                puts.append(
                    pltpu.make_async_copy(
                        fresh.at[n, k, pl.ds(source, count)],
                        whole_ref.at[k, pl.ds(first + target, count)],
                        sems.at[n, k, place],
                    )
                )
                puts[-1].start()
    for put in puts:
        put.wait()


def place(kinds, parts, whole, groups):
    hbm = pl.BlockSpec(memory_space=pl.ANY)
    vmem = pl.BlockSpec(memory_space=VMEM)
    return pl.pallas_call(
        functools.partial(place_kernel, kinds, groups),
        out_shape=jax.ShapeDtypeStruct(whole.shape, F32),
        in_specs=[vmem] * len(parts) + [hbm],
        out_specs=hbm,
        scratch_shapes=[
            VMEM((len(parts),) + parts[0].shape, F32),
            pltpu.SemaphoreType.DMA((len(parts), 2, 2)),
        ],
        input_output_aliases={len(parts): 0},
        compiler_params=limit(16),
        name="place",
    )(*near(*parts), whole)


def per_device(
    object_band,
    dual_band,
    probe_field,
    positions,
    live_counts,
    photon_counts,
    footprints,
    weights,
    volume,
):
    tiles, groups = lax.axis_size("tile"), lax.axis_size("view")
    tile_cols = object_band.shape[2]
    foot_cols = weights.shape[1]
    footprints = footprints[:, 0]
    forward = dft_block(probe_field.shape[1], False)
    inverse = dft_block(probe_field.shape[1], True)

    dealt = deal(weights, groups)
    weight_pieces = [dealt[0]]
    for j in range(1, groups):
        weight_pieces.append(swapped(dealt[j], "view", j))
    keep, send, volume_own = project(footprints, dealt, volume, tiles, tile_cols)
    ahead_one = passed_along(object_band, "tile", -1)
    ahead_two = passed_along(object_band, "tile", -2)
    arrived = swapped(send, "tile", 1)
    projection, *rest = fold(keep, arrived)
    token = rest[-1]
    for n, block in enumerate(rest):
        projection = projection + swapped(block, "tile", 2 * (n + 1)).astype(F32)

    own_update, spill_one, spill_two = patches(
        positions,
        live_counts[:, 0],
        object_band,
        ahead_one,
        ahead_two,
        probe_field,
        forward,
        inverse,
        photon_counts,
        token,
    )
    from_one = passed_along(spill_one, "tile", 1)
    from_two = passed_along(spill_two, "tile", 2)
    summed = own_update + from_one.astype(F32) + from_two.astype(F32)
    object_new = (
        object_band
        + summed[:, 0:2] / (1.0 + summed[:, 2:3])
        - rho_weight * (object_band - projection - dual_band)
    )
    dual_new = dual_band + projection - object_new
    residual = (projection - object_new + dual_band).astype(BF16)

    pieces = [residual]
    for n in range(1, tiles // 2):
        pieces.append(swapped(residual, "tile", 2 * n))
    others = swapped(jnp.stack(pieces), "tile", 1)
    windows = cut(footprints, [piece[None] for piece in pieces] + [others], foot_cols, tiles)
    all_windows = [windows]
    for j in range(1, groups):
        all_windows.append(swapped(windows, "view", j))

    half, low_edge, high_edge = half_step_of(weight_pieces, all_windows, volume_own)
    view_masks = masks_of(groups)
    order = [g * tiles + t for t in range(tiles) for g in range(groups)]
    up = list(zip(order[:-1], order[1:]))
    before = lax.ppermute(high_edge, ("view", "tile"), up)
    after = lax.ppermute(low_edge, ("view", "tile"), [(b, a) for a, b in up])
    part, volume_new = first_part(half, volume.shape[1])
    other, volume_new = second_part(half, before, after, volume_new)
    held = {(False, 0): part, (True, 0): other}
    for masks in zip(view_masks, view_masks[::-1]):
        arrived = {}
        for kind, mask in zip((False, True), masks):
            for (second, j), value in held.items():
                if second == kind:
                    arrived[kind, j ^ mask] = swapped(value, "view", mask)
        held.update(arrived)
    waiting = [key for key in held if key[1]]
    near_keys = [key for key in waiting if key[1] in view_masks]
    rounds = [[key for key in near_keys if not key[0]], [key for key in near_keys if key[0]]]
    far_keys = [key for key in waiting if key not in near_keys]
    rounds += [far_keys[n : n + 2] for n in range(0, len(far_keys), 2)]
    for keys in rounds:
        if keys:
            volume_new = place(keys, [held[key] for key in keys], volume_new, groups)
    return (object_new, dual_new, volume_new)


def solution(mesh):
    return jax.shard_map(
        per_device,
        mesh=mesh,
        in_specs=(
            P("view", None, "tile", None),
            P("view", None, "tile", None),
            P(),
            P("view", "tile"),
            P("view", "tile"),
            P("view", "tile", None, None),
            P("view", "tile"),
            P("view", None, "tile"),
            P(None, "tile", None, None),
        ),
        out_specs=(
            P("view", None, "tile", None),
            P("view", None, "tile", None),
            P(None, "tile", None, None),
        ),
        check_vma=False,
    )
```

time: 164 us -> 145 us (0.88)
  the two profiles are of different devices: /device:TPU:1 before, /device:TPU:0 now
where the time goes in v2:
time: 145 us
  waiting for transfers between devices  62 us (43%)
  starting transfers between devices  53.5 us (37%)
  Pallas kernels  23.7 us (16%)
  local copies, waits for them, and re-layouts  4.08 us (3%)
    ppermute x20, waiting for transfers between devices, swapped(): return lax.ppermute(value, axis, [(i, i ^ mask) for i in range(count)])  56 us
    ppermute x20, starting transfers between devices, swapped(): return lax.ppermute(value, axis, [(i, i ^ mask) for i in range(count)])  31.8 us
    ppermute x4, starting transfers between devices, passed_along(): lax.ppermute(value, axis, [(source, source + steps) for source in range(i...  16.5 us
    pallas_call x1, Pallas kernels, patches(): pl.pallas_call(patch_kernel, out_shape=(VMEM((views, 3, width, rows), F32...  7.96 us
    ppermute x4, waiting for transfers between devices, passed_along(): lax.ppermute(value, axis, [(source, source + steps) for source in range(i...  5.96 us
    pallas_call x3, Pallas kernels, place(): pl.pallas_call(functools.partial(place_kernel, kinds, groups), out_shape=...  4.21 us
    unnamed x24, local copies, waits for them, and re-layouts  4.08 us
    ppermute x1, starting transfers between devices, per_device(): before = lax.ppermute(high_edge, ('view', 'tile'), up)  3.93 us
  transfers between devices with their start and end apart: 26, of which 14 were waited for; matrix products, arithmetic and copies ran while one was open for 1% of the time, Pallas kernels for 6%

profile of v2, /device:TPU:0, one launch (start us, length us, event | category | flops | bytes accessed | tf_op | source)
XLA Modules:
  0.0 145.2 jit_solution(16710431067954825480)
XLA Ops:
  0.6 0.0 copy-start.8
  0.6 0.0 copy-start.9
  0.7 2.3 %deal.1 = (bf16[2,128,2048]{2,1,0:T(8,128)(2,1)S(1)}, bf16[2,128,2048]{2,1,0:T(8,128)(2,1)S(1)}, bf16[2,128,2048]{2,1,0:T(8,128)(2,1)S(1)}, bf16[2,128,2048]{2,1,0:T(8,128)(2,1)S(1)}) custom-call(bf16[2,128,8192]{2,1,0:T(8,128)(2,1)} %weights_ref.1), custom_call_target="tpu_custom_call" | custom-call | tf_op jit(solution)/shard_map/deal/pallas_call | solution.py:73
  3.0 0.0 copy-start
  3.0 3.4 %copy-done = f32[2,64,128,128]{3,2,1,0:T(8,128)S(1)} copy-done((f32[2,64,128,128]{3,2,1,0:T(8,128)S(1)}, f32[2,64,128,128]{3,2,1,0:T(8,128)}, u32[]{:S(2)}) %copy-start) | copy-done | bytes 8388632
  6.4 0.7 copy-done.2
  7.0 2.0 %project.1 = (bf16[4,2,2,64,128]{4,3,2,1,0:T(8,128)(2,1)S(1)}, bf16[4,2,2,64,128]{4,3,2,1,0:T(8,128)(2,1)S(1)}, f32[2,16,128,128]{3,2,1,0:T(8,128)S(1)}) custom-call(s32[2]{0:T(128)S(1)} %bitcast.16, f32[2,64,128,128]{3,2,1,0:T(8,128)S(1)} %copy-done, bf16[2,128,2048]{2,1,0:T(8,128)(2,1)S(1)} %get-tuple-element.24.refs_0_, ...), custom_call_target="tpu_custom_call" | custom-call | tf_op jit(solution)/shard_map/project/pallas_call | solution.py:139
  9.0 0.0 copy-start.3
  9.1 0.6 collective-permute-start.2
  9.6 1.3 collective-permute-start.1
  10.9 1.3 collective-permute-start
  12.2 0.0 collective-permute-done.2.arrived_ref
  12.2 0.1 fold.1
  12.3 6.0 %collective-permute-done.1.two_ref = f32[2,2,64,128]{3,2,1,0:T(8,128)S(1)} collective-permute-done((f32[2,2,64,128]{3,2,1,0:T(8,128)S(1)}, f32[2,2,64,128]{3,2,1,0:T(8,128)S(1)}, u32[]{:S(2)}, u32[]{:S(2)}) %collective-permute-start.1) | collective-permute-done | bytes 131104 | tf_op jit(solution)/shard_map/ppermute | solution.py:26
  18.2 0.0 collective-permute-done.one_ref
  18.3 8.0 %patches.1 = (f32[2,3,64,128]{3,2,1,0:T(8,128)S(1)}, bf16[2,3,64,128]{3,2,1,0:T(8,128)(2,1)S(1)}, bf16[2,3,64,128]{3,2,1,0:T(8,128)(2,1)S(1)}) custom-call(s32[2,32]{1,0:T(2,128)S(1)} %copy-done.6, s32[2]{0:T(128)S(1)} %bitcast.18, f32[2,2,64,128]{3,2,1,0:T(8,128)S(1)} %copy-done.1, f32[2,2,64,128]{3,2,1,0:T(8,128)S(1)} %collective-permute-done.one_ref, ...), custom_call_target="tpu_custom_call" | custom-call | flops 2147483648 | bytes 4194304 | tf_op jit(solution)/shard_map/patches/pallas_call | solution.py:299
  26.3 2.2 %collective-permute-start.3 = (bf16[2,3,64,128]{3,2,1,0:T(8,128)(2,1)S(1)}, bf16[2,3,64,128]{3,2,1,0:T(8,128)(2,1)S(1)}, u32[]{:S(2)}, u32[]{:S(2)}) collective-permute-start(bf16[2,3,64,128]{3,2,1,0:T(8,128)(2,1)S(1)} %get-tuple-element.32), channel_id=1, source_target_pairs={{0,1},{1,2},{2,3},{3,4},{4,5},{5,6},{6,7},{8,9},{9,10},{10,11},{11... | collective-permute-start | bytes 294920 | tf_op jit(solution)/shard_map/ppermute | solution.py:26
  28.5 11.8 %collective-permute-start.4 = (bf16[2,3,64,128]{3,2,1,0:T(8,128)(2,1)S(1)}, bf16[2,3,64,128]{3,2,1,0:T(8,128)(2,1)S(1)}, u32[]{:S(2)}, u32[]{:S(2)}) collective-permute-start(bf16[2,3,64,128]{3,2,1,0:T(8,128)(2,1)S(1)} %get-tuple-element.33), channel_id=1, source_target_pairs={{0,2},{1,3},{2,4},{3,5},{4,6},{5,7},{8,10},{9,11},{10,12},{11,13},... | collective-permute-start | bytes 294920 | tf_op jit(solution)/shard_map/ppermute | solution.py:26
  40.2 0.1 collective-permute-start.8
  40.3 0.1 collective-permute-start.9
  40.4 3.4 %collective-permute-start.10 = (bf16[2,128,2048]{2,1,0:T(8,128)(2,1)S(1)}, bf16[2,128,2048]{2,1,0:T(8,128)(2,1)S(1)}, u32[]{:S(2)}, u32[]{:S(2)}) collective-permute-start(bf16[2,128,2048]{2,1,0:T(8,128)(2,1)S(1)} %get-tuple-element.27.refs_3_), channel_id=1, source_target_pairs={{0,24},{8,16},{16,8},{24,0},{1,25},{9,17},{17,9},{25,1},{2,26},{10... | collective-permute-start | bytes 3145736 | tf_op jit(solution)/shard_map/ppermute | solution.py:39
  43.8 0.0 collective-permute-done.3
  43.8 0.0 collective-permute-start.7
  43.8 0.0 collective-permute-done.4
  43.8 1.1 collective-permute-start.5
  45.0 3.6 %collective-permute-done.5 = bf16[2,2,64,128]{3,2,1,0:T(8,128)(2,1)S(1)} collective-permute-done((bf16[2,2,64,128]{3,2,1,0:T(8,128)(2,1)S(1)}, bf16[2,2,64,128]{3,2,1,0:T(8,128)(2,1)S(1)}, u32[]{:S(2)}, u32[]{:S(2)}) %collective-permute-start.5) | collective-permute-done | bytes 65568 | tf_op jit(solution)/shard_map/ppermute | solution.py:39
  48.6 2.5 %collective-permute-start.6 = (bf16[2,2,64,128]{3,2,1,0:T(8,128)(2,1)S(1)}, bf16[2,2,64,128]{3,2,1,0:T(8,128)(2,1)S(1)}, u32[]{:S(2)}, u32[]{:S(2)}) collective-permute-start(bf16[2,2,64,128]{3,2,1,0:T(8,128)(2,1)S(1)} %get-tuple-element.36), channel_id=1, source_target_pairs={{0,4},{1,5},{2,6},{3,7},{4,0},{5,1},{6,2},{7,3},{8,12},{9,13},{10,... | collective-permute-start | bytes 196616 | tf_op jit(solution)/shard_map/ppermute | solution.py:39
  51.1 3.3 %collective-permute-done.6 = bf16[2,2,64,128]{3,2,1,0:T(8,128)(2,1)S(1)} collective-permute-done((bf16[2,2,64,128]{3,2,1,0:T(8,128)(2,1)S(1)}, bf16[2,2,64,128]{3,2,1,0:T(8,128)(2,1)S(1)}, u32[]{:S(2)}, u32[]{:S(2)}) %collective-permute-start.6) | collective-permute-done | bytes 65568 | tf_op jit(solution)/shard_map/ppermute | solution.py:39
  54.5 0.0 collective-permute-done.7
  54.5 0.1 add_convert_fusion
  54.6 0.0 copy-start.11
  54.6 3.8 %collective-permute-start.13 = (bf16[2,2,64,128]{3,2,1,0:T(8,128)(2,1)S(1)}, bf16[2,2,64,128]{3,2,1,0:T(8,128)(2,1)S(1)}, u32[]{:S(2)}, u32[]{:S(2)}) collective-permute-start(bf16[2,2,64,128]{3,2,1,0:T(8,128)(2,1)S(1)} %get-tuple-element.45), channel_id=1, source_target_pairs={{0,6},{1,7},{2,4},{3,5},{4,2},{5,3},{6,0},{7,1},{8,14},{9,15},{10,... | collective-permute-start | bytes 196616 | tf_op jit(solution)/shard_map/ppermute | solution.py:39
  58.4 0.0 collective-permute-start.12
  58.4 2.3 %collective-permute-done.13 = bf16[2,2,64,128]{3,2,1,0:T(8,128)(2,1)S(1)} collective-permute-done((bf16[2,2,64,128]{3,2,1,0:T(8,128)(2,1)S(1)}, bf16[2,2,64,128]{3,2,1,0:T(8,128)(2,1)S(1)}, u32[]{:S(2)}, u32[]{:S(2)}) %collective-permute-start.13) | collective-permute-done | bytes 65568 | tf_op jit(solution)/shard_map/ppermute | solution.py:39
  60.7 2.9 %collective-permute-done.12 = bf16[2,2,64,128]{3,2,1,0:T(8,128)(2,1)S(1)} collective-permute-done((bf16[2,2,64,128]{3,2,1,0:T(8,128)(2,1)S(1)}, bf16[2,2,64,128]{3,2,1,0:T(8,128)(2,1)S(1)}, u32[]{:S(2)}, u32[]{:S(2)}) %collective-permute-start.12) | collective-permute-done | bytes 65568 | tf_op jit(solution)/shard_map/ppermute | solution.py:39
  63.6 1.4 collective-permute-done.11
  65.0 0.1 collective-permute-start.14
  65.1 1.5 %collective-permute-done.14.refs_4_ = bf16[4,2,2,64,128]{4,3,2,1,0:T(8,128)(2,1)S(1)} collective-permute-done((bf16[4,2,2,64,128]{4,3,2,1,0:T(8,128)(2,1)S(1)}, bf16[4,2,2,64,128]{4,3,2,1,0:T(8,128)(2,1)S(1)}, u32[]{:S(2)}, u32[]{:S(2)}) %collective-permute-start.14) | collective-permute-done | bytes 262176 | tf_op jit(solution)/shard_map/ppermute | solution.py:39
  66.6 0.7 cut.1.refs_4_
  67.3 0.3 collective-permute-start.17
  67.6 1.5 %collective-permute-start.16 = (bf16[2,2,128,128]{3,2,1,0:T(8,128)(2,1)S(1)}, bf16[2,2,128,128]{3,2,1,0:T(8,128)(2,1)S(1)}, u32[]{:S(2)}, u32[]{:S(2)}) collective-permute-start(bf16[2,2,128,128]{3,2,1,0:T(8,128)(2,1)S(1)} %cut.1.refs_4_), channel_id=1, source_target_pairs={{0,16},{8,24},{16,0},{24,8},{1,17},{9,25},{17,1},{25,9},{2,18},{10... | collective-permute-start | bytes 393224 | tf_op jit(solution)/shard_map/ppermute | solution.py:39
  69.1 19.1 %collective-permute-done.17.refs_7_ = bf16[2,2,128,128]{3,2,1,0:T(8,128)(2,1)S(1)} collective-permute-done((bf16[2,2,128,128]{3,2,1,0:T(8,128)(2,1)S(1)}, bf16[2,2,128,128]{3,2,1,0:T(8,128)(2,1)S(1)}, u32[]{:S(2)}, u32[]{:S(2)}) %collective-permute-start.17) | collective-permute-done | bytes 131104 | tf_op jit(solution)/shard_map/ppermute | solution.py:39
  88.2 2.2 %collective-permute-start.15 = (bf16[2,2,128,128]{3,2,1,0:T(8,128)(2,1)S(1)}, bf16[2,2,128,128]{3,2,1,0:T(8,128)(2,1)S(1)}, u32[]{:S(2)}, u32[]{:S(2)}) collective-permute-start(bf16[2,2,128,128]{3,2,1,0:T(8,128)(2,1)S(1)} %cut.1.refs_4_), channel_id=1, source_target_pairs={{0,8},{8,0},{16,24},{24,16},{1,9},{9,1},{17,25},{25,17},{2,10},{10... | collective-permute-start | bytes 393224 | tf_op jit(solution)/shard_map/ppermute | solution.py:39
  90.4 2.9 %collective-permute-done.16.refs_6_ = bf16[2,2,128,128]{3,2,1,0:T(8,128)(2,1)S(1)} collective-permute-done((bf16[2,2,128,128]{3,2,1,0:T(8,128)(2,1)S(1)}, bf16[2,2,128,128]{3,2,1,0:T(8,128)(2,1)S(1)}, u32[]{:S(2)}, u32[]{:S(2)}) %collective-permute-start.16) | collective-permute-done | bytes 131104 | tf_op jit(solution)/shard_map/ppermute | solution.py:39
  93.3 0.1 collective-permute-done.15.refs_5_
  93.4 1.4 half_step.1
  94.7 3.9 %collective-permute-start.20 = (bf16[2,1,128,128]{3,2,1,0:T(8,128)(2,1)S(1)}, bf16[2,1,128,128]{3,2,1,0:T(8,128)(2,1)S(1)}, u32[]{:S(2)}, u32[]{:S(2)}) collective-permute-start(bf16[2,1,128,128]{3,2,1,0:T(8,128)(2,1)S(1)} %get-tuple-element.40), channel_id=1, source_target_pairs={{0,8},{8,16},{16,24},{24,1},{1,9},{9,17},{17,25},{25,2},{2,10},{10... | collective-permute-start | bytes 196616 | tf_op jit(solution)/shard_map/ppermute | solution.py:643
  98.7 1.3 collective-permute-start.21
  100.0 2.5 %first_part.1 = (bf16[2,8,128,128]{3,2,1,0:T(8,128)(2,1)S(1)}, f32[2,64,128,128]{3,2,1,0:T(8,128)}) custom-call(f32[2,16,128,128]{3,2,1,0:T(8,128)S(1)} %get-tuple-element.38.half_ref), custom_call_target="tpu_custom_call" | custom-call | tf_op jit(solution)/shard_map/first_part/pallas_call | solution.py:464
  102.5 4.1 %collective-permute-start.18 = (bf16[2,8,128,128]{3,2,1,0:T(8,128)(2,1)S(1)}, bf16[2,8,128,128]{3,2,1,0:T(8,128)(2,1)S(1)}, u32[]{:S(2)}, u32[]{:S(2)}) collective-permute-start(bf16[2,8,128,128]{3,2,1,0:T(8,128)(2,1)S(1)} %get-tuple-element.39), channel_id=1, source_target_pairs={{0,8},{8,0},{16,24},{24,16},{1,9},{9,1},{17,25},{25,17},{2,10},{10... | collective-permute-start | bytes 1572872 | tf_op jit(solution)/shard_map/ppermute | solution.py:39
  106.6 2.6 %second_part.1 = (bf16[2,8,128,128]{3,2,1,0:T(8,128)(2,1)S(1)}, f32[2,64,128,128]{3,2,1,0:T(8,128)}) custom-call(f32[2,16,128,128]{3,2,1,0:T(8,128)S(1)} %get-tuple-element.38.half_ref, bf16[2,1,128,128]{3,2,1,0:T(8,128)(2,1)S(1)} %collective-permute-done.20.before_ref, ...), custom_call_target="tpu_custom_call", output_to_operand_aliasing={{1}: (3, {})} | custom-call | tf_op jit(solution)/shard_map/second_part/pallas_call | solution.py:515
  109.3 1.5 %collective-permute-start.22 = (bf16[2,8,128,128]{3,2,1,0:T(8,128)(2,1)S(1)}, bf16[2,8,128,128]{3,2,1,0:T(8,128)(2,1)S(1)}, u32[]{:S(2)}, u32[]{:S(2)}) collective-permute-start(bf16[2,8,128,128]{3,2,1,0:T(8,128)(2,1)S(1)} %get-tuple-element.43), channel_id=1, source_target_pairs={{0,16},{8,24},{16,0},{24,8},{1,17},{9,25},{17,1},{25,9},{2,18},{10... | collective-permute-start | bytes 1572872 | tf_op jit(solution)/shard_map/ppermute | solution.py:39
  110.8 0.5 collective-permute-start.25
  111.4 3.2 %collective-permute-start.24 = (bf16[2,8,128,128]{3,2,1,0:T(8,128)(2,1)S(1)}, bf16[2,8,128,128]{3,2,1,0:T(8,128)(2,1)S(1)}, u32[]{:S(2)}, u32[]{:S(2)}) collective-permute-start(bf16[2,8,128,128]{3,2,1,0:T(8,128)(2,1)S(1)} %get-tuple-element.43), channel_id=1, source_target_pairs={{0,8},{8,0},{16,24},{24,16},{1,9},{9,1},{17,25},{25,17},{2,10},{10... | collective-permute-start | bytes 1572872 | tf_op jit(solution)/shard_map/ppermute | solution.py:39
  114.6 4.8 %collective-permute-done.18.refs_0_ = bf16[2,8,128,128]{3,2,1,0:T(8,128)(2,1)S(1)} collective-permute-done((bf16[2,8,128,128]{3,2,1,0:T(8,128)(2,1)S(1)}, bf16[2,8,128,128]{3,2,1,0:T(8,128)(2,1)S(1)}, u32[]{:S(2)}, u32[]{:S(2)}) %collective-permute-start.18) | collective-permute-done | bytes 524320 | tf_op jit(solution)/shard_map/ppermute | solution.py:39
  119.4 3.5 %collective-permute-start.19 = (bf16[2,8,128,128]{3,2,1,0:T(8,128)(2,1)S(1)}, bf16[2,8,128,128]{3,2,1,0:T(8,128)(2,1)S(1)}, u32[]{:S(2)}, u32[]{:S(2)}) collective-permute-start(bf16[2,8,128,128]{3,2,1,0:T(8,128)(2,1)S(1)} %collective-permute-done.18.refs_0_), channel_id=1, source_target_pairs={{0,16},{8,24},{16,0},{24,8},{1,17},{9,25},{17,1},{25,9},{2,18},{10... | collective-permute-start | bytes 1572872 | tf_op jit(solution)/shard_map/ppermute | solution.py:39
  122.9 1.3 collective-permute-done.22.refs_0_
  124.1 3.2 %collective-permute-start.23 = (bf16[2,8,128,128]{3,2,1,0:T(8,128)(2,1)S(1)}, bf16[2,8,128,128]{3,2,1,0:T(8,128)(2,1)S(1)}, u32[]{:S(2)}, u32[]{:S(2)}) collective-permute-start(bf16[2,8,128,128]{3,2,1,0:T(8,128)(2,1)S(1)} %collective-permute-done.22.refs_0_), channel_id=1, source_target_pairs={{0,8},{8,0},{16,24},{24,16},{1,9},{9,1},{17,25},{25,17},{2,10},{10... | collective-permute-start | bytes 1572872 | tf_op jit(solution)/shard_map/ppermute | solution.py:39
  127.3 0.7 add_subtract_fusion
  128.0 7.3 %collective-permute-done.25.refs_1_ = bf16[2,8,128,128]{3,2,1,0:T(8,128)(2,1)S(1)} collective-permute-done((bf16[2,8,128,128]{3,2,1,0:T(8,128)(2,1)S(1)}, bf16[2,8,128,128]{3,2,1,0:T(8,128)(2,1)S(1)}, u32[]{:S(2)}, u32[]{:S(2)}) %collective-permute-start.25) | collective-permute-done | bytes 524320 | tf_op jit(solution)/shard_map/ppermute | solution.py:39
  135.4 1.4 place.3.refs_2_
  136.8 1.4 place.4.refs_2_
  138.2 5.6 %collective-permute-done.19.refs_0_ = bf16[2,8,128,128]{3,2,1,0:T(8,128)(2,1)S(1)} collective-permute-done((bf16[2,8,128,128]{3,2,1,0:T(8,128)(2,1)S(1)}, bf16[2,8,128,128]{3,2,1,0:T(8,128)(2,1)S(1)}, u32[]{:S(2)}, u32[]{:S(2)}) %collective-permute-start.19) | collective-permute-done | bytes 524320 | tf_op jit(solution)/shard_map/ppermute | solution.py:39
  143.8 1.4 place.5
  (28 shorter events, 0.1 us)
Async XLA Ops:
  0.6 17.6 %copy-start.8 = (bf16[256,256]{1,0:T(8,128)(2,1)S(1)}, bf16[256,256]{1,0:T(8,128)(2,1)}, u32[]{:S(2)}) copy-start(bf16[256,256]{1,0:T(8,128)(2,1)} %constant.18.inverse_ref) | copy-start | bytes 393220
  0.6 17.6 %copy-start.9 = (bf16[256,256]{1,0:T(8,128)(2,1)S(1)}, bf16[256,256]{1,0:T(8,128)(2,1)}, u32[]{:S(2)}) copy-start(bf16[256,256]{1,0:T(8,128)(2,1)} %constant.17.forward_ref) | copy-start | bytes 393220
  0.7 9.0 %copy-start.1 = (f32[2,2,64,128]{3,2,1,0:T(8,128)S(1)}, f32[2,2,64,128]{3,2,1,0:T(8,128)}, u32[]{:S(2)}) copy-start(f32[2,2,64,128]{3,2,1,0:T(8,128)} %own_ref.1) | copy-start | bytes 393220
  0.7 17.6 %copy-start.7 = (s32[2,1]{0,1:T(1,128)S(1)}, s32[2,1]{0,1:T(1,128)}, u32[]{:S(2)}) copy-start(s32[2,1]{0,1:T(1,128)} %param.15) | copy-start | bytes 28
  0.7 17.6 %copy-start.6 = (s32[2,32]{1,0:T(2,128)S(1)}, s32[2,32]{1,0:T(2,128)}, u32[]{:S(2)}) copy-start(s32[2,32]{1,0:T(2,128)} %positions.1) | copy-start | bytes 772
  0.7 17.6 %copy-start.5 = (f32[2,128,128]{2,1,0:T(8,128)S(1)}, f32[2,128,128]{2,1,0:T(8,128)}, u32[]{:S(2)}) copy-start(f32[2,128,128]{2,1,0:T(8,128)} %probe_ref.1) | copy-start | bytes 393220
  3.0 3.4 %copy-start = (f32[2,64,128,128]{3,2,1,0:T(8,128)S(1)}, f32[2,64,128,128]{3,2,1,0:T(8,128)}, u32[]{:S(2)}) copy-start(f32[2,64,128,128]{3,2,1,0:T(8,128)} %volume_ref.1) | copy-start | bytes 25165828
  6.4 0.7 copy-start.2
  7.0 11.3 %copy-start.4 = (s32[2,32,128,128]{3,2,1,0:T(8,128)S(1)}, s32[2,32,128,128]{3,2,1,0:T(8,128)}, u32[]{:S(2)}) copy-start(s32[2,32,128,128]{3,2,1,0:T(8,128)} %counts_ref.1) | copy-start | bytes 12582916
  7.0 47.4 %copy-start.10 = (f32[2,2,64,128]{3,2,1,0:T(8,128)S(1)}, f32[2,2,64,128]{3,2,1,0:T(8,128)}, u32[]{:S(2)}) copy-start(f32[2,2,64,128]{3,2,1,0:T(8,128)} %param.12) | copy-start | bytes 393220
  9.0 57.6 %copy-start.3 = (s32[2,1]{0,1:T(1,128)S(1)}, s32[2,1]{0,1:T(1,128)}, u32[]{:S(2)}) copy-start(s32[2,1]{0,1:T(1,128)} %param.17) | copy-start | bytes 28
  9.1 3.2 %collective-permute-start.2 = (bf16[4,2,2,64,128]{4,3,2,1,0:T(8,128)(2,1)S(1)}, bf16[4,2,2,64,128]{4,3,2,1,0:T(8,128)(2,1)S(1)}, u32[]{:S(2)}, u32[]{:S(2)}) collective-permute-start(bf16[4,2,2,64,128]{4,3,2,1,0:T(8,128)(2,1)S(1)} %get-tuple-element.29), channel_id=1, source_target_pairs={{0,1},{1,0},{2,3},{3,2},{4,5},{5,4},{6,7},{7,6},{8,9},{9,8},{10,11... | collective-permute-start | bytes 786440 | tf_op jit(solution)/shard_map/ppermute | solution.py:39
  9.6 8.6 %collective-permute-start.1 = (f32[2,2,64,128]{3,2,1,0:T(8,128)S(1)}, f32[2,2,64,128]{3,2,1,0:T(8,128)S(1)}, u32[]{:S(2)}, u32[]{:S(2)}) collective-permute-start(f32[2,2,64,128]{3,2,1,0:T(8,128)S(1)} %copy-done.1), channel_id=1, source_target_pairs={{2,0},{3,1},{4,2},{5,3},{6,4},{7,5},{10,8},{11,9},{12,10},{13,11},... | collective-permute-start | bytes 393224 | tf_op jit(solution)/shard_map/ppermute | solution.py:26
  10.9 7.3 %collective-permute-start = (f32[2,2,64,128]{3,2,1,0:T(8,128)S(1)}, f32[2,2,64,128]{3,2,1,0:T(8,128)S(1)}, u32[]{:S(2)}, u32[]{:S(2)}) collective-permute-start(f32[2,2,64,128]{3,2,1,0:T(8,128)S(1)} %copy-done.1), channel_id=1, source_target_pairs={{1,0},{2,1},{3,2},{4,3},{5,4},{6,5},{7,6},{9,8},{10,9},{11,10},{12... | collective-permute-start | bytes 393224 | tf_op jit(solution)/shard_map/ppermute | solution.py:26
  26.3 17.5 %collective-permute-start.3 = (bf16[2,3,64,128]{3,2,1,0:T(8,128)(2,1)S(1)}, bf16[2,3,64,128]{3,2,1,0:T(8,128)(2,1)S(1)}, u32[]{:S(2)}, u32[]{:S(2)}) collective-permute-start(bf16[2,3,64,128]{3,2,1,0:T(8,128)(2,1)S(1)} %get-tuple-element.32), channel_id=1, source_target_pairs={{0,1},{1,2},{2,3},{3,4},{4,5},{5,6},{6,7},{8,9},{9,10},{10,11},{11... | collective-permute-start | bytes 294920 | tf_op jit(solution)/shard_map/ppermute | solution.py:26
  28.5 15.3 %collective-permute-start.4 = (bf16[2,3,64,128]{3,2,1,0:T(8,128)(2,1)S(1)}, bf16[2,3,64,128]{3,2,1,0:T(8,128)(2,1)S(1)}, u32[]{:S(2)}, u32[]{:S(2)}) collective-permute-start(bf16[2,3,64,128]{3,2,1,0:T(8,128)(2,1)S(1)} %get-tuple-element.33), channel_id=1, source_target_pairs={{0,2},{1,3},{2,4},{3,5},{4,6},{5,7},{8,10},{9,11},{10,12},{11,13},... | collective-permute-start | bytes 294920 | tf_op jit(solution)/shard_map/ppermute | solution.py:26
  40.2 53.1 %collective-permute-start.8 = (bf16[2,128,2048]{2,1,0:T(8,128)(2,1)S(1)}, bf16[2,128,2048]{2,1,0:T(8,128)(2,1)S(1)}, u32[]{:S(2)}, u32[]{:S(2)}) collective-permute-start(bf16[2,128,2048]{2,1,0:T(8,128)(2,1)S(1)} %get-tuple-element.25.refs_1_), channel_id=1, source_target_pairs={{0,8},{8,0},{16,24},{24,16},{1,9},{9,1},{17,25},{25,17},{2,10},{10... | collective-permute-start | bytes 3145736 | tf_op jit(solution)/shard_map/ppermute | solution.py:39
  40.3 53.0 %collective-permute-start.9 = (bf16[2,128,2048]{2,1,0:T(8,128)(2,1)S(1)}, bf16[2,128,2048]{2,1,0:T(8,128)(2,1)S(1)}, u32[]{:S(2)}, u32[]{:S(2)}) collective-permute-start(bf16[2,128,2048]{2,1,0:T(8,128)(2,1)S(1)} %get-tuple-element.26.refs_2_), channel_id=1, source_target_pairs={{0,16},{8,24},{16,0},{24,8},{1,17},{9,25},{17,1},{25,9},{2,18},{10... | collective-permute-start | bytes 3145736 | tf_op jit(solution)/shard_map/ppermute | solution.py:39
  40.4 53.0 %collective-permute-start.10 = (bf16[2,128,2048]{2,1,0:T(8,128)(2,1)S(1)}, bf16[2,128,2048]{2,1,0:T(8,128)(2,1)S(1)}, u32[]{:S(2)}, u32[]{:S(2)}) collective-permute-start(bf16[2,128,2048]{2,1,0:T(8,128)(2,1)S(1)} %get-tuple-element.27.refs_3_), channel_id=1, source_target_pairs={{0,24},{8,16},{16,8},{24,0},{1,25},{9,17},{17,9},{25,1},{2,26},{10... | collective-permute-start | bytes 3145736 | tf_op jit(solution)/shard_map/ppermute | solution.py:39
  43.8 10.7 %collective-permute-start.7 = (bf16[2,2,64,128]{3,2,1,0:T(8,128)(2,1)S(1)}, bf16[2,2,64,128]{3,2,1,0:T(8,128)(2,1)S(1)}, u32[]{:S(2)}, u32[]{:S(2)}) collective-permute-start(bf16[2,2,64,128]{3,2,1,0:T(8,128)(2,1)S(1)} %get-tuple-element.30.token_ref), channel_id=1, source_target_pairs={{0,6},{1,7},{2,4},{3,5},{4,2},{5,3},{6,0},{7,1},{8,14},{9,15},{10,... | collective-permute-start | bytes 196616 | tf_op jit(solution)/shard_map/ppermute | solution.py:39
  43.8 4.8 %collective-permute-start.5 = (bf16[2,2,64,128]{3,2,1,0:T(8,128)(2,1)S(1)}, bf16[2,2,64,128]{3,2,1,0:T(8,128)(2,1)S(1)}, u32[]{:S(2)}, u32[]{:S(2)}) collective-permute-start(bf16[2,2,64,128]{3,2,1,0:T(8,128)(2,1)S(1)} %get-tuple-element.35), channel_id=1, source_target_pairs={{0,2},{1,3},{2,0},{3,1},{4,6},{5,7},{6,4},{7,5},{8,10},{9,11},{10,... | collective-permute-start | bytes 196616 | tf_op jit(solution)/shard_map/ppermute | solution.py:39
  48.6 5.9 %collective-permute-start.6 = (bf16[2,2,64,128]{3,2,1,0:T(8,128)(2,1)S(1)}, bf16[2,2,64,128]{3,2,1,0:T(8,128)(2,1)S(1)}, u32[]{:S(2)}, u32[]{:S(2)}) collective-permute-start(bf16[2,2,64,128]{3,2,1,0:T(8,128)(2,1)S(1)} %get-tuple-element.36), channel_id=1, source_target_pairs={{0,4},{1,5},{2,6},{3,7},{4,0},{5,1},{6,2},{7,3},{8,12},{9,13},{10,... | collective-permute-start | bytes 196616 | tf_op jit(solution)/shard_map/ppermute | solution.py:39
  54.6 72.8 %copy-start.11 = (f32[2,2,64,128]{3,2,1,0:T(8,128)}, f32[2,2,64,128]{3,2,1,0:T(8,128)S(1)}, u32[]{:S(2)}) copy-start(f32[2,2,64,128]{3,2,1,0:T(8,128)S(1)} %get-tuple-element.46) | copy-start | bytes 393220
  54.6 6.1 %collective-permute-start.13 = (bf16[2,2,64,128]{3,2,1,0:T(8,128)(2,1)S(1)}, bf16[2,2,64,128]{3,2,1,0:T(8,128)(2,1)S(1)}, u32[]{:S(2)}, u32[]{:S(2)}) collective-permute-start(bf16[2,2,64,128]{3,2,1,0:T(8,128)(2,1)S(1)} %get-tuple-element.45), channel_id=1, source_target_pairs={{0,6},{1,7},{2,4},{3,5},{4,2},{5,3},{6,0},{7,1},{8,14},{9,15},{10,... | collective-permute-start | bytes 196616 | tf_op jit(solution)/shard_map/ppermute | solution.py:39
  58.4 5.2 %collective-permute-start.12 = (bf16[2,2,64,128]{3,2,1,0:T(8,128)(2,1)S(1)}, bf16[2,2,64,128]{3,2,1,0:T(8,128)(2,1)S(1)}, u32[]{:S(2)}, u32[]{:S(2)}) collective-permute-start(bf16[2,2,64,128]{3,2,1,0:T(8,128)(2,1)S(1)} %get-tuple-element.45), channel_id=1, source_target_pairs={{0,4},{1,5},{2,6},{3,7},{4,0},{5,1},{6,2},{7,3},{8,12},{9,13},{10,... | collective-permute-start | bytes 196616 | tf_op jit(solution)/shard_map/ppermute | solution.py:39
  60.7 4.3 %collective-permute-start.11 = (bf16[2,2,64,128]{3,2,1,0:T(8,128)(2,1)S(1)}, bf16[2,2,64,128]{3,2,1,0:T(8,128)(2,1)S(1)}, u32[]{:S(2)}, u32[]{:S(2)}) collective-permute-start(bf16[2,2,64,128]{3,2,1,0:T(8,128)(2,1)S(1)} %get-tuple-element.45), channel_id=1, source_target_pairs={{0,2},{1,3},{2,0},{3,1},{4,6},{5,7},{6,4},{7,5},{8,10},{9,11},{10,... | collective-permute-start | bytes 196616 | tf_op jit(solution)/shard_map/ppermute | solution.py:39
  65.0 1.6 %collective-permute-start.14 = (bf16[4,2,2,64,128]{4,3,2,1,0:T(8,128)(2,1)S(1)}, bf16[4,2,2,64,128]{4,3,2,1,0:T(8,128)(2,1)S(1)}, u32[]{:S(2)}, u32[]{:S(2)}) collective-permute-start(bf16[4,2,2,64,128]{4,3,2,1,0:T(8,128)(2,1)S(1)} %pad_maximum_fusion), channel_id=1, source_target_pairs={{0,1},{1,0},{2,3},{3,2},{4,5},{5,4},{6,7},{7,6},{8,9},{9,8},{10,11... | collective-permute-start | bytes 786440 | tf_op jit(solution)/shard_map/ppermute | solution.py:39
  67.3 20.9 %collective-permute-start.17 = (bf16[2,2,128,128]{3,2,1,0:T(8,128)(2,1)S(1)}, bf16[2,2,128,128]{3,2,1,0:T(8,128)(2,1)S(1)}, u32[]{:S(2)}, u32[]{:S(2)}) collective-permute-start(bf16[2,2,128,128]{3,2,1,0:T(8,128)(2,1)S(1)} %cut.1.refs_4_), channel_id=1, source_target_pairs={{0,24},{8,16},{16,8},{24,0},{1,25},{9,17},{17,9},{25,1},{2,26},{10... | collective-permute-start | bytes 393224 | tf_op jit(solution)/shard_map/ppermute | solution.py:39
  67.6 25.7 %collective-permute-start.16 = (bf16[2,2,128,128]{3,2,1,0:T(8,128)(2,1)S(1)}, bf16[2,2,128,128]{3,2,1,0:T(8,128)(2,1)S(1)}, u32[]{:S(2)}, u32[]{:S(2)}) collective-permute-start(bf16[2,2,128,128]{3,2,1,0:T(8,128)(2,1)S(1)} %cut.1.refs_4_), channel_id=1, source_target_pairs={{0,16},{8,24},{16,0},{24,8},{1,17},{9,25},{17,1},{25,9},{2,18},{10... | collective-permute-start | bytes 393224 | tf_op jit(solution)/shard_map/ppermute | solution.py:39
  88.2 5.1 %collective-permute-start.15 = (bf16[2,2,128,128]{3,2,1,0:T(8,128)(2,1)S(1)}, bf16[2,2,128,128]{3,2,1,0:T(8,128)(2,1)S(1)}, u32[]{:S(2)}, u32[]{:S(2)}) collective-permute-start(bf16[2,2,128,128]{3,2,1,0:T(8,128)(2,1)S(1)} %cut.1.refs_4_), channel_id=1, source_target_pairs={{0,8},{8,0},{16,24},{24,16},{1,9},{9,1},{17,25},{25,17},{2,10},{10... | collective-permute-start | bytes 393224 | tf_op jit(solution)/shard_map/ppermute | solution.py:39
  94.7 11.9 %collective-permute-start.20 = (bf16[2,1,128,128]{3,2,1,0:T(8,128)(2,1)S(1)}, bf16[2,1,128,128]{3,2,1,0:T(8,128)(2,1)S(1)}, u32[]{:S(2)}, u32[]{:S(2)}) collective-permute-start(bf16[2,1,128,128]{3,2,1,0:T(8,128)(2,1)S(1)} %get-tuple-element.40), channel_id=1, source_target_pairs={{0,8},{8,16},{16,24},{24,1},{1,9},{9,17},{17,25},{25,2},{2,10},{10... | collective-permute-start | bytes 196616 | tf_op jit(solution)/shard_map/ppermute | solution.py:643
  98.7 7.9 %collective-permute-start.21 = (bf16[2,1,128,128]{3,2,1,0:T(8,128)(2,1)S(1)}, bf16[2,1,128,128]{3,2,1,0:T(8,128)(2,1)S(1)}, u32[]{:S(2)}, u32[]{:S(2)}) collective-permute-start(bf16[2,1,128,128]{3,2,1,0:T(8,128)(2,1)S(1)} %get-tuple-element.41), channel_id=1, source_target_pairs={{8,0},{16,8},{24,16},{1,24},{9,1},{17,9},{25,17},{2,25},{10,2},{18... | collective-permute-start | bytes 196616 | tf_op jit(solution)/shard_map/ppermute | solution.py:644
  102.5 16.8 %collective-permute-start.18 = (bf16[2,8,128,128]{3,2,1,0:T(8,128)(2,1)S(1)}, bf16[2,8,128,128]{3,2,1,0:T(8,128)(2,1)S(1)}, u32[]{:S(2)}, u32[]{:S(2)}) collective-permute-start(bf16[2,8,128,128]{3,2,1,0:T(8,128)(2,1)S(1)} %get-tuple-element.39), channel_id=1, source_target_pairs={{0,8},{8,0},{16,24},{24,16},{1,9},{9,1},{17,25},{25,17},{2,10},{10... | collective-permute-start | bytes 1572872 | tf_op jit(solution)/shard_map/ppermute | solution.py:39
  109.3 14.9 %collective-permute-start.22 = (bf16[2,8,128,128]{3,2,1,0:T(8,128)(2,1)S(1)}, bf16[2,8,128,128]{3,2,1,0:T(8,128)(2,1)S(1)}, u32[]{:S(2)}, u32[]{:S(2)}) collective-permute-start(bf16[2,8,128,128]{3,2,1,0:T(8,128)(2,1)S(1)} %get-tuple-element.43), channel_id=1, source_target_pairs={{0,16},{8,24},{16,0},{24,8},{1,17},{9,25},{17,1},{25,9},{2,18},{10... | collective-permute-start | bytes 1572872 | tf_op jit(solution)/shard_map/ppermute | solution.py:39
  110.8 24.5 %collective-permute-start.25 = (bf16[2,8,128,128]{3,2,1,0:T(8,128)(2,1)S(1)}, bf16[2,8,128,128]{3,2,1,0:T(8,128)(2,1)S(1)}, u32[]{:S(2)}, u32[]{:S(2)}) collective-permute-start(bf16[2,8,128,128]{3,2,1,0:T(8,128)(2,1)S(1)} %get-tuple-element.39), channel_id=1, source_target_pairs={{0,16},{8,24},{16,0},{24,8},{1,17},{9,25},{17,1},{25,9},{2,18},{10... | collective-permute-start | bytes 1572872 | tf_op jit(solution)/shard_map/ppermute | solution.py:39
  111.4 25.4 %collective-permute-start.24 = (bf16[2,8,128,128]{3,2,1,0:T(8,128)(2,1)S(1)}, bf16[2,8,128,128]{3,2,1,0:T(8,128)(2,1)S(1)}, u32[]{:S(2)}, u32[]{:S(2)}) collective-permute-start(bf16[2,8,128,128]{3,2,1,0:T(8,128)(2,1)S(1)} %get-tuple-element.43), channel_id=1, source_target_pairs={{0,8},{8,0},{16,24},{24,16},{1,9},{9,1},{17,25},{25,17},{2,10},{10... | collective-permute-start | bytes 1572872 | tf_op jit(solution)/shard_map/ppermute | solution.py:39
  119.4 24.4 %collective-permute-start.19 = (bf16[2,8,128,128]{3,2,1,0:T(8,128)(2,1)S(1)}, bf16[2,8,128,128]{3,2,1,0:T(8,128)(2,1)S(1)}, u32[]{:S(2)}, u32[]{:S(2)}) collective-permute-start(bf16[2,8,128,128]{3,2,1,0:T(8,128)(2,1)S(1)} %collective-permute-done.18.refs_0_), channel_id=1, source_target_pairs={{0,16},{8,24},{16,0},{24,8},{1,17},{9,25},{17,1},{25,9},{2,18},{10... | collective-permute-start | bytes 1572872 | tf_op jit(solution)/shard_map/ppermute | solution.py:39
  124.1 19.6 %collective-permute-start.23 = (bf16[2,8,128,128]{3,2,1,0:T(8,128)(2,1)S(1)}, bf16[2,8,128,128]{3,2,1,0:T(8,128)(2,1)S(1)}, u32[]{:S(2)}, u32[]{:S(2)}) collective-permute-start(bf16[2,8,128,128]{3,2,1,0:T(8,128)(2,1)S(1)} %collective-permute-done.22.refs_0_), channel_id=1, source_target_pairs={{0,8},{8,0},{16,24},{24,16},{1,9},{9,1},{17,25},{25,17},{2,10},{10... | collective-permute-start | bytes 1572872 | tf_op jit(solution)/shard_map/ppermute | solution.py:39

commit v3 on v2

--- a/solution.py
+++ b/solution.py
@@ -30,6 +30,10 @@
     return tuple(pltpu.with_memory_space_constraint(array, VMEM) for array in arrays)
 
 
+def far(*arrays):
+    return tuple(pltpu.with_memory_space_constraint(array, pltpu.HBM) for array in arrays)
+
+
 def limit(mebibytes):
     return pltpu.CompilerParams(vmem_limit_bytes=mebibytes << 20)
 
@@ -41,6 +45,19 @@
 
 def masks_of(count):
     return [1 << b for b in range(count.bit_length() - 1)]
+
+
+def gray(rank):
+    return rank ^ (rank >> 1)
+
+
+def share_at(j, groups):
+    rank = lax.axis_index("view") ^ j
+    shift = 1
+    while shift < groups:
+        rank = rank ^ (rank >> shift)
+        shift *= 2
+    return jnp.where((lax.axis_index("tile") & 1) == 1, groups - 1 - rank, rank)
 
 
 def dft_block(order_n, inverse):
@@ -52,33 +69,32 @@
     return jnp.asarray(np.block([[re, -im], [im, re]]).astype(np.float32)).astype(BF16)
 
 
-def deal_kernel(weights_ref, *refs):
+def deal_kernel(groups, offsets, weights_ref, *refs):
     *shares, sems = refs
-    group = lax.axis_index("view")
     copies = []
-    for j, ref in list(enumerate(shares))[1:] + [(0, shares[0])]:
+    for n, (j, ref) in enumerate(zip(offsets, shares)):
         size = ref.shape[2]
-        first = pl.multiple_of((group ^ j) * size, size)
+        first = pl.multiple_of(share_at(j, groups) * size, size)
         copies.append(
-            pltpu.make_async_copy(weights_ref.at[:, :, pl.ds(first, size)], ref, sems.at[j])
+            pltpu.make_async_copy(weights_ref.at[:, :, pl.ds(first, size)], ref, sems.at[n])
         )
         copies[-1].start()
     for copy in copies:
         copy.wait()
 
 
-def deal(weights, groups):
+def deal(weights, groups, offsets):
     views, cols, voxels = weights.shape
     vmem = pl.BlockSpec(memory_space=VMEM)
     return pl.pallas_call(
-        deal_kernel,
-        out_shape=(VMEM((views, cols, voxels // groups), BF16),) * groups,
+        functools.partial(deal_kernel, groups, offsets),
+        out_shape=(VMEM((views, cols, voxels // groups), BF16),) * len(offsets),
         in_specs=[pl.BlockSpec(memory_space=pl.ANY)],
-        out_specs=(vmem,) * groups,
-        scratch_shapes=[pltpu.SemaphoreType.DMA((groups,))],
+        out_specs=(vmem,) * len(offsets),
+        scratch_shapes=[pltpu.SemaphoreType.DMA((len(offsets),))],
         compiler_params=limit(8),
         name="deal",
-    )(pltpu.with_memory_space_constraint(weights, pltpu.HBM))
+    )(*far(weights))
 
 
 def ranks(footprints, views, parts, tiles):
@@ -93,25 +109,49 @@
     return found
 
 
-def project_kernel(footprints, volume_ref, *refs):
-    *shares, keep_ref, send_ref, part_ref = refs
-    views, cols, size = shares[0].shape
-    _, count, _, rows = part_ref.shape
+def project_kernel(pieces, footprints_ref, volume_ref, *refs):
+    *shares, keep_ref, send_ref, part_ref, footprints, held, sem, sems = refs
+    groups = len(shares)
+    views, cols, _ = shares[0].shape
+    _, count, depth, rows = part_ref.shape
     half, _, _, width, _ = keep_ref.shape
-    group = lax.axis_index("view")
+    chunk = count // pieces
+    span = chunk * depth
+    spots_copy = pltpu.make_async_copy(footprints_ref, footprints, sem)
+    spots_copy.start()
+    copies = []
+    for j in range(groups):
+        first = share_at(j, groups) * count
+        for i in range(pieces):
+            copies.append(
+                pltpu.make_async_copy(
+                    volume_ref.at[:, pl.ds(first + i * chunk, chunk)],
+                    held.at[j, :, pl.ds(i * chunk, chunk)],
+                    sems.at[j, i],
+                )
+            )
+            copies[-1].start()
     keep_ref[...] = jnp.zeros_like(keep_ref)
     send_ref[...] = jnp.zeros_like(send_ref)
-    part_ref[...] = volume_ref[:, pl.ds(group * count, count)]
     total = jnp.zeros((views * cols, 2 * rows), F32)
     for j, ref in enumerate(shares):
-        first = (group ^ j) * count
-        low = jnp.concatenate(
-            [volume_ref[k, pl.ds(first, count)].reshape(size, rows).astype(BF16) for k in range(2)],
-            axis=1,
-        )
-        total = total + jnp.dot(
-            ref[...].reshape(views * cols, size), low, preferred_element_type=F32
-        )
+        for i in range(pieces):
+            copies[j * pieces + i].wait()
+            low = jnp.concatenate(
+                [
+                    held[j, k, i * chunk : (i + 1) * chunk].reshape(span, rows).astype(BF16)
+                    for k in range(2)
+                ],
+                axis=1,
+            )
+            total = total + jnp.dot(
+                ref[:, :, i * span : (i + 1) * span].reshape(views * cols, span),
+                low,
+                preferred_element_type=F32,
+            )
+        if j == 0:
+            part_ref[...] = held[0]
+    spots_copy.wait()
     spots = ranks(footprints, views, cols // width, 2 * half)
     for v in range(views):
         for part in range(cols // width):
@@ -134,16 +174,25 @@
     groups = len(shares)
     views, _, _ = shares[0].shape
     _, vcols, depth, rows = volume.shape
-    vmem = pl.BlockSpec(memory_space=VMEM)
+    count = vcols // groups
+    pieces = 2 if count % 2 == 0 else 1
+    vmem = pl.BlockSpec(memory_space=VMEM)
+    hbm = pl.BlockSpec(memory_space=pl.ANY)
     placed = VMEM((tiles // 2, views, 2, tile_cols, rows), BF16)
     return pl.pallas_call(
-        project_kernel,
-        out_shape=(placed, placed, VMEM((2, vcols // groups, depth, rows), F32)),
-        in_specs=[pl.BlockSpec(memory_space=SMEM)] + [vmem] * (groups + 1),
+        functools.partial(project_kernel, pieces),
+        out_shape=(placed, placed, VMEM((2, count, depth, rows), F32)),
+        in_specs=[hbm, hbm] + [vmem] * groups,
         out_specs=(vmem,) * 3,
-        compiler_params=limit(16),
+        scratch_shapes=[
+            SMEM(footprints.shape, jnp.int32),
+            VMEM((groups, 2, count, depth, rows), F32),
+            pltpu.SemaphoreType.DMA(()),
+            pltpu.SemaphoreType.DMA((groups, pieces)),
+        ],
+        compiler_params=limit(20),
         name="project",
-    )(footprints, *near(volume, *shares))
+    )(*far(footprints, volume), *near(*shares))
 
 
 def fold_kernel(keep_ref, arrived_ref, *refs):
@@ -163,7 +212,7 @@
     )(*near(keep, arrived))
 
 
-GROUP = 4
+GROUP = 8
 
 
 def patch_kernel(
@@ -370,7 +419,7 @@
     return here - step_size * prior_weight * prior
 
 
-def run_of_columns(half_ref, k, first, count, final, store):
+def run_of_columns(half_ref, k, first, count, store):
     before = half_ref[k, first - 1]
     here = half_ref[k, first]
 
@@ -381,16 +430,23 @@
         store(i, settled(here, behind, ahead))
         return ahead, following
 
-    inner = count if final is None else count - 1
-    behind, here = lax.fori_loop(0, inner, body, (bent(before - here), here), unroll=2)
-    if final is not None:
-        store(count - 1, settled(here, behind, bent(here - final)))
+    lax.fori_loop(0, count, body, (bent(before - here), here), unroll=2)
+
+
+def inner_columns(half_ref, part_ref, fresh_ref, first):
+    for k in range(2):
+
+        def store(i, column):
+            fresh_ref[k, i] = column
+            part_ref[k, i] = column.astype(BF16)
+
+        run_of_columns(half_ref, k, first, part_ref.shape[1], store)
 
 
 def gradient_kernel(groups, pieces, *refs):
     weight_refs = refs[:groups]
     window_refs = refs[groups : 2 * groups]
-    volume_ref, half_ref, low_ref, high_ref = refs[2 * groups :]
+    volume_ref, half_ref, low_ref, high_ref, part_ref, fresh_ref = refs[2 * groups :]
     _, share, depth, rows = half_ref.shape
     views, cols, _ = weight_refs[0].shape
     chunk = share // pieces
@@ -417,6 +473,7 @@
             half_ref[k, held] = volume_ref[k, held] - step_size * plane
     low_ref[...] = half_ref[:, :1].astype(BF16)
     high_ref[...] = half_ref[:, share - 1 :].astype(BF16)
+    inner_columns(half_ref, part_ref, fresh_ref, 1)
 
 
 def half_step_of(weights, windows, volume):
@@ -424,128 +481,107 @@
     _, share, depth, rows = volume.shape
     vmem = pl.BlockSpec(memory_space=VMEM)
     edge = VMEM((2, 1, depth, rows), BF16)
+    inner = (2, share // 2 - 1, depth, rows)
     return pl.pallas_call(
         functools.partial(gradient_kernel, groups, min(4, share)),
-        out_shape=(VMEM((2, share, depth, rows), F32), edge, edge),
+        out_shape=(
+            VMEM((2, share, depth, rows), F32),
+            edge,
+            edge,
+            VMEM(inner, BF16),
+            VMEM(inner, F32),
+        ),
         in_specs=[vmem] * (2 * groups + 1),
-        out_specs=(vmem, vmem, vmem),
+        out_specs=(vmem,) * 5,
         compiler_params=limit(20),
         name="half_step",
     )(*near(*weights, *windows, volume))
 
 
-def first_kernel(half_ref, part_ref, whole_ref, fresh, sems):
-    group = lax.axis_index("view")
+def second_kernel(half_ref, part_ref, fresh_ref):
+    inner_columns(half_ref, part_ref, fresh_ref, part_ref.shape[1] + 1)
+
+
+def second_part(half):
+    _, share, depth, rows = half.shape
+    vmem = pl.BlockSpec(memory_space=VMEM)
+    inner = (2, share // 2 - 1, depth, rows)
+    return pl.pallas_call(
+        second_kernel,
+        out_shape=(VMEM(inner, BF16), VMEM(inner, F32)),
+        in_specs=[vmem],
+        out_specs=(vmem, vmem),
+        compiler_params=limit(16),
+        name="second_part",
+    )(*near(half))
+
+
+def third_kernel(half_ref, before_ref, after_ref, first_ref, second_ref, part_ref, whole_ref, *rest):
+    edges, sems = rest
     share = half_ref.shape[1]
+    inner = first_ref.shape[1]
+    start = share_at(0, whole_ref.shape[1] // share) * share
     puts = []
-    for k in range(2):
-
-        def store(i, column):
-            fresh[k, i] = column
-            part_ref[k, i] = column.astype(BF16)
-
-        run_of_columns(half_ref, k, 1, share // 2, None, store)
+
+    def put(source, target, count):
         puts.append(
             pltpu.make_async_copy(
-                fresh.at[k],
-                whole_ref.at[k, pl.ds(group * share + 1, share // 2)],
-                sems.at[k],
+                source, whole_ref.at[:, pl.ds(start + target, count)], sems.at[len(puts)]
             )
         )
         puts[-1].start()
-    for put in puts:
-        put.wait()
-
-
-def first_part(half, vcols):
-    _, share, depth, rows = half.shape
-    hbm = pl.BlockSpec(memory_space=pl.ANY)
-    vmem = pl.BlockSpec(memory_space=VMEM)
-    return pl.pallas_call(
-        first_kernel,
+
+    put(first_ref, 1, inner)
+    put(second_ref, inner + 1, inner)
+    for k in range(2):
+        for n, (c, before, after) in enumerate(
+            (
+                (0, before_ref[k, 0].astype(F32), half_ref[k, 1]),
+                (share - 1, half_ref[k, share - 2], after_ref[k, 0].astype(F32)),
+            )
+        ):
+            here = half_ref[k, c]
+            column = settled(here, bent(before - here), bent(here - after))
+            edges[k, n] = column
+            part_ref[k, n] = column.astype(BF16)
+    put(edges.at[:, pl.ds(0, 1)], 0, 1)
+    put(edges.at[:, pl.ds(1, 1)], share - 1, 1)
+    for move in puts:
+        move.wait()
+
+
+def third_part(half, before, after, first, second, vcols):
+    _, _, depth, rows = half.shape
+    vmem = pl.BlockSpec(memory_space=VMEM)
+    return pl.pallas_call(
+        third_kernel,
         out_shape=(
-            VMEM((2, share // 2, depth, rows), BF16),
+            VMEM((2, 2, depth, rows), BF16),
             jax.ShapeDtypeStruct((2, vcols, depth, rows), F32),
         ),
-        in_specs=[vmem],
-        out_specs=(vmem, hbm),
-        scratch_shapes=[
-            VMEM((2, share // 2, depth, rows), F32),
-            pltpu.SemaphoreType.DMA((2,)),
-        ],
+        in_specs=[vmem] * 5,
+        out_specs=(vmem, pl.BlockSpec(memory_space=pl.ANY)),
+        scratch_shapes=[VMEM((2, 2, depth, rows), F32), pltpu.SemaphoreType.DMA((4,))],
         compiler_params=limit(16),
-        name="first_part",
-    )(*near(half))
-
-
-def second_kernel(half_ref, before_ref, after_ref, _, part_ref, whole_ref, fresh, sems):
-    group = lax.axis_index("view")
-    share = half_ref.shape[1]
-    middle = share // 2
+        name="third_part",
+    )(*near(half, before, after, first, second))
+
+
+def place_kernel(kinds, groups, *refs):
+    count = len(kinds)
+    parts, whole_ref, fresh, sems = refs[:count], refs[count + 1], refs[count + 2 : -1], refs[-1]
+    share = whole_ref.shape[1] // groups
+    inner = share // 2 - 1
     puts = []
-    for k in range(2):
-
-        def store(i, column):
-            fresh[k, i + 1] = column
-            part_ref[k, i + 1] = column.astype(BF16)
-
-        here = half_ref[k, 0]
-        column = settled(here, bent(before_ref[k, 0].astype(F32) - here), bent(here - half_ref[k, 1]))
-        store(-1, column)
-        run_of_columns(half_ref, k, middle + 1, middle - 1, after_ref[k, 0].astype(F32), store)
-        for place, (source, target, count) in enumerate(
-            ((0, 0, 1), (1, middle + 1, middle - 1))
-        ):
-            puts.append(
-                pltpu.make_async_copy(
-                    fresh.at[k, pl.ds(source, count)],
-                    whole_ref.at[k, pl.ds(group * share + target, count)],
-                    sems.at[k, place],
-                )
-            )
-            puts[-1].start()
-    for put in puts:
-        put.wait()
-
-
-def second_part(half, before, after, whole):
-    _, share, depth, rows = half.shape
-    hbm = pl.BlockSpec(memory_space=pl.ANY)
-    vmem = pl.BlockSpec(memory_space=VMEM)
-    return pl.pallas_call(
-        second_kernel,
-        out_shape=(
-            VMEM((2, share // 2, depth, rows), BF16),
-            jax.ShapeDtypeStruct(whole.shape, F32),
-        ),
-        in_specs=[vmem, vmem, vmem, hbm],
-        out_specs=(vmem, hbm),
-        scratch_shapes=[
-            VMEM((2, share // 2, depth, rows), F32),
-            pltpu.SemaphoreType.DMA((2, 2)),
-        ],
-        input_output_aliases={3: 1},
-        compiler_params=limit(16),
-        name="second_part",
-    )(*near(half, before, after), whole)
-
-
-def place_kernel(kinds, groups, *refs):
-    parts = refs[: len(kinds)]
-    _, whole_ref, fresh, sems = refs[len(kinds) :]
-    group = lax.axis_index("view")
-    share = whole_ref.shape[1] // groups
-    middle = share // 2
-    puts = []
-    for n, ((second, j), ref) in enumerate(zip(kinds, parts)):
-        first = (group ^ j) * share
-        runs = ((0, 0, 1), (1, middle + 1, middle - 1)) if second else ((0, 1, middle),)
+    for n, ((kind, j), ref) in enumerate(zip(kinds, parts)):
+        first = share_at(j, groups) * share
+        runs = ((0, 0, 1), (1, share - 1, 1)) if kind == 2 else ((0, kind * inner + 1, inner),)
         for place, (source, target, count) in enumerate(runs):
             for k in range(2):
-                fresh[n, k, source : source + count] = ref[k, source : source + count].astype(F32)
+                fresh[n][k, source : source + count] = ref[k, source : source + count].astype(F32)
                 puts.append(
                     pltpu.make_async_copy(
-                        fresh.at[n, k, pl.ds(source, count)],
+                        fresh[n].at[k, pl.ds(source, count)],
                         whole_ref.at[k, pl.ds(first + target, count)],
                         sems.at[n, k, place],
                     )
@@ -563,10 +599,8 @@
         out_shape=jax.ShapeDtypeStruct(whole.shape, F32),
         in_specs=[vmem] * len(parts) + [hbm],
         out_specs=hbm,
-        scratch_shapes=[
-            VMEM((len(parts),) + parts[0].shape, F32),
-            pltpu.SemaphoreType.DMA((len(parts), 2, 2)),
-        ],
+        scratch_shapes=[VMEM(part.shape, F32) for part in parts]
+        + [pltpu.SemaphoreType.DMA((len(parts), 2, 2))],
         input_output_aliases={len(parts): 0},
         compiler_params=limit(16),
         name="place",
@@ -591,7 +625,12 @@
     forward = dft_block(probe_field.shape[1], False)
     inverse = dft_block(probe_field.shape[1], True)
 
-    dealt = deal(weights, groups)
+    view_masks = masks_of(groups)
+    later = [j for j in range(groups) if j not in view_masks]
+    early_shares = deal(weights, groups, view_masks)
+    late_shares = deal(weights, groups, later)
+    dealt = dict(zip(view_masks + later, early_shares + late_shares))
+    dealt = [dealt[j] for j in range(groups)]
     weight_pieces = [dealt[0]]
     for j in range(1, groups):
         weight_pieces.append(swapped(dealt[j], "view", j))
@@ -636,30 +675,28 @@
     for j in range(1, groups):
         all_windows.append(swapped(windows, "view", j))
 
-    half, low_edge, high_edge = half_step_of(weight_pieces, all_windows, volume_own)
-    view_masks = masks_of(groups)
-    order = [g * tiles + t for t in range(tiles) for g in range(groups)]
+    half, low_edge, high_edge, part_a, fresh_a = half_step_of(
+        weight_pieces, all_windows, volume_own
+    )
+    order = []
+    for t in range(tiles):
+        order += [gray(r) * tiles + t for r in range(groups)][:: -1 if t % 2 else 1]
     up = list(zip(order[:-1], order[1:]))
     before = lax.ppermute(high_edge, ("view", "tile"), up)
     after = lax.ppermute(low_edge, ("view", "tile"), [(b, a) for a, b in up])
-    part, volume_new = first_part(half, volume.shape[1])
-    other, volume_new = second_part(half, before, after, volume_new)
-    held = {(False, 0): part, (True, 0): other}
-    for masks in zip(view_masks, view_masks[::-1]):
+    part_b, fresh_b = second_part(half)
+    part_c, volume_new = third_part(half, before, after, fresh_a, fresh_b, volume.shape[1])
+    held = {(0, 0): part_a, (1, 0): part_b, (2, 0): part_c}
+    for masks in zip(view_masks, view_masks[::-1], view_masks):
         arrived = {}
-        for kind, mask in zip((False, True), masks):
-            for (second, j), value in held.items():
-                if second == kind:
-                    arrived[kind, j ^ mask] = swapped(value, "view", mask)
+        for (kind, j), value in held.items():
+            arrived[kind, j ^ masks[kind]] = swapped(value, "view", masks[kind])
         held.update(arrived)
-    waiting = [key for key in held if key[1]]
-    near_keys = [key for key in waiting if key[1] in view_masks]
-    rounds = [[key for key in near_keys if not key[0]], [key for key in near_keys if key[0]]]
-    far_keys = [key for key in waiting if key not in near_keys]
-    rounds += [far_keys[n : n + 2] for n in range(0, len(far_keys), 2)]
+    rounds = [[(kind, mask) for mask in view_masks] for kind in range(3)]
+    far_keys = [j for j in range(1, groups) if j not in view_masks]
+    rounds += [[(0, j), (1, j)] for j in far_keys] + [[(2, j)] for j in far_keys]
     for keys in rounds:
-        if keys:
-            volume_new = place(keys, [held[key] for key in keys], volume_new, groups)
+        volume_new = place(keys, [held[key] for key in keys], volume_new, groups)
     return (object_new, dual_new, volume_new)
 
 

time: 145 us -> 144 us (level)
  waiting for transfers between devices: 62 us -> 82.7 us
  starting transfers between devices: 53.5 us -> 33.1 us
  local copies, waits for them, and re-layouts: 4.08 us -> 0.06 us
  Pallas kernels: 23.7 us -> 26.2 us
    ppermute x1, waiting for transfers between devices: 0.01 us -> 16.3 us  [per_device(): after = lax.ppermute(low_edge, ('view', 'tile'), [(b, a) for a, b in up])]
    ppermute x20 -> x23, starting transfers between devices: 31.8 us -> 16 us  [swapped(): return lax.ppermute(value, axis, [(i, i ^ mask) for i in range(count)])]
    unnamed x24 -> x20, local copies, waits for them, and re-layouts: 4.08 us -> 0.06 us
    ppermute x4, starting transfers between devices: 16.5 us -> 12.6 us  [passed_along(): lax.ppermute(value, axis, [(source, source + steps) for source in range(i...]
    ppermute x20 -> x23, waiting for transfers between devices: 56 us -> 58.5 us  [swapped(): return lax.ppermute(value, axis, [(i, i ^ mask) for i in range(count)])]
    pallas_call x1, Pallas kernels: 7.96 us -> 5.56 us  [patches(): pl.pallas_call(patch_kernel, out_shape=(VMEM((views, 3, width, rows), F32...]
    ppermute x4, waiting for transfers between devices: 5.96 us -> 7.9 us  [passed_along(): lax.ppermute(value, axis, [(source, source + steps) for source in range(i...]
    pallas_call x4 -> x5, Pallas kernels: 9.47 us -> 11.3 us  [the longest x1 4.78 us: project(): pl.pallas_call(functools.partial(project_kernel, pieces), out_shape=(plac...]
  transfers between devices with their start and end apart: 26 -> 29, of which waited for: 14 -> 15; matrix products, arithmetic and copies ran while one was open for 1% -> 1% of each run, Pallas kernels for 6% -> 5%
where the time goes in v3:
time: 144 us
  waiting for transfers between devices  82.7 us (57%)
  starting transfers between devices  33.1 us (23%)
  Pallas kernels  26.2 us (18%)
    ppermute x23, waiting for transfers between devices, swapped(): return lax.ppermute(value, axis, [(i, i ^ mask) for i in range(count)])  58.5 us
    ppermute x1, waiting for transfers between devices, per_device(): after = lax.ppermute(low_edge, ('view', 'tile'), [(b, a) for a, b in up])  16.3 us
    ppermute x23, starting transfers between devices, swapped(): return lax.ppermute(value, axis, [(i, i ^ mask) for i in range(count)])  16 us
    ppermute x4, starting transfers between devices, passed_along(): lax.ppermute(value, axis, [(source, source + steps) for source in range(i...  12.6 us
    ppermute x4, waiting for transfers between devices, passed_along(): lax.ppermute(value, axis, [(source, source + steps) for source in range(i...  7.9 us
    pallas_call x5, Pallas kernels, place(): pl.pallas_call(functools.partial(place_kernel, kinds, groups), out_shape=...  5.58 us
    pallas_call x1, Pallas kernels, patches(): pl.pallas_call(patch_kernel, out_shape=(VMEM((views, 3, width, rows), F32...  5.56 us
    pallas_call x1, Pallas kernels, project(): pl.pallas_call(functools.partial(project_kernel, pieces), out_shape=(plac...  4.78 us
  transfers between devices with their start and end apart: 29, of which 15 were waited for; matrix products, arithmetic and copies ran while one was open for 1% of the time, Pallas kernels for 5%

profile of v3, /device:TPU:0, one launch (start us, length us, event | category | flops | bytes accessed | tf_op | source)
XLA Modules:
  0.0 143.9 jit_solution(12139785869990119570)
XLA Ops:
  0.6 1.6 %deal.2 = (bf16[2,128,2048]{2,1,0:T(8,128)(2,1)S(1)}, bf16[2,128,2048]{2,1,0:T(8,128)(2,1)S(1)}) custom-call(bf16[2,128,8192]{2,1,0:T(8,128)(2,1)} %weights_ref.3), custom_call_target="tpu_custom_call" | custom-call | tf_op jit(solution)/shard_map/deal/pallas_call | solution.py:89
  2.2 0.0 copy-start
  2.2 0.0 copy-start.2
  2.2 0.0 copy-start.3
  2.3 0.0 copy-start.5
  2.3 0.0 copy-start.6
  2.3 0.0 copy-start.7
  2.3 1.7 %deal.3 = (bf16[2,128,2048]{2,1,0:T(8,128)(2,1)S(1)}, bf16[2,128,2048]{2,1,0:T(8,128)(2,1)S(1)}) custom-call(bf16[2,128,8192]{2,1,0:T(8,128)(2,1)} %weights_ref.3), custom_call_target="tpu_custom_call" | custom-call | tf_op jit(solution)/shard_map/deal/pallas_call | solution.py:89
  4.0 0.0 copy-start.8
  4.0 4.8 %project.1 = (bf16[4,2,2,64,128]{4,3,2,1,0:T(8,128)(2,1)S(1)}, bf16[4,2,2,64,128]{4,3,2,1,0:T(8,128)(2,1)S(1)}, f32[2,16,128,128]{3,2,1,0:T(8,128)S(1)}) custom-call(s32[2]{0:T(128)} %bitcast.16, f32[2,64,128,128]{3,2,1,0:T(8,128)} %volume_ref.1, bf16[2,128,2048]{2,1,0:T(8,128)(2,1)S(1)} %get-tuple-element.26.refs_0_, ...), custom_call_target="tpu_custom_call" | custom-call | tf_op jit(solution)/shard_map/project/pallas_call | solution.py:182
  8.8 0.6 collective-permute-start.2
  9.4 1.3 collective-permute-start
  10.7 1.3 collective-permute-start.1
  12.0 0.1 fold.1
  12.1 0.6 collective-permute-done.one_ref
  12.6 7.3 %collective-permute-done.1.two_ref = f32[2,2,64,128]{3,2,1,0:T(8,128)S(1)} collective-permute-done((f32[2,2,64,128]{3,2,1,0:T(8,128)S(1)}, f32[2,2,64,128]{3,2,1,0:T(8,128)S(1)}, u32[]{:S(2)}, u32[]{:S(2)}) %collective-permute-start.1) | collective-permute-done | bytes 131104 | tf_op jit(solution)/shard_map/ppermute | solution.py:26
  20.0 5.6 %patches.1 = (f32[2,3,64,128]{3,2,1,0:T(8,128)S(1)}, bf16[2,3,64,128]{3,2,1,0:T(8,128)(2,1)S(1)}, bf16[2,3,64,128]{3,2,1,0:T(8,128)(2,1)S(1)}) custom-call(s32[2,32]{1,0:T(2,128)S(1)} %copy-done.4, s32[2]{0:T(128)S(1)} %bitcast.18, f32[2,2,64,128]{3,2,1,0:T(8,128)S(1)} %copy-done, f32[2,2,64,128]{3,2,1,0:T(8,128)S(1)} %collective-permute-done.one_ref, ...), custom_call_target="tpu_custom_call" | custom-call | flops 2147483648 | bytes 4194304 | tf_op jit(solution)/shard_map/patches/pallas_call | solution.py:348
  25.6 1.8 %collective-permute-start.3 = (bf16[2,3,64,128]{3,2,1,0:T(8,128)(2,1)S(1)}, bf16[2,3,64,128]{3,2,1,0:T(8,128)(2,1)S(1)}, u32[]{:S(2)}, u32[]{:S(2)}) collective-permute-start(bf16[2,3,64,128]{3,2,1,0:T(8,128)(2,1)S(1)} %get-tuple-element.34), channel_id=1, source_target_pairs={{0,1},{1,2},{2,3},{3,4},{4,5},{5,6},{6,7},{8,9},{9,10},{10,11},{11... | collective-permute-start | bytes 294920 | tf_op jit(solution)/shard_map/ppermute | solution.py:26
  27.4 8.2 %collective-permute-start.4 = (bf16[2,3,64,128]{3,2,1,0:T(8,128)(2,1)S(1)}, bf16[2,3,64,128]{3,2,1,0:T(8,128)(2,1)S(1)}, u32[]{:S(2)}, u32[]{:S(2)}) collective-permute-start(bf16[2,3,64,128]{3,2,1,0:T(8,128)(2,1)S(1)} %get-tuple-element.35), channel_id=1, source_target_pairs={{0,2},{1,3},{2,4},{3,5},{4,6},{5,7},{8,10},{9,11},{10,12},{11,13},... | collective-permute-start | bytes 294920 | tf_op jit(solution)/shard_map/ppermute | solution.py:26
  35.6 0.1 collective-permute-start.10
  35.7 1.0 collective-permute-start.8
  36.7 2.5 %collective-permute-start.9 = (bf16[2,128,2048]{2,1,0:T(8,128)(2,1)S(1)}, bf16[2,128,2048]{2,1,0:T(8,128)(2,1)S(1)}, u32[]{:S(2)}, u32[]{:S(2)}) collective-permute-start(bf16[2,128,2048]{2,1,0:T(8,128)(2,1)S(1)} %get-tuple-element.28.refs_2_), channel_id=1, source_target_pairs={{0,16},{8,24},{16,0},{24,8},{1,17},{9,25},{17,1},{25,9},{2,18},{10... | collective-permute-start | bytes 3145736 | tf_op jit(solution)/shard_map/ppermute | solution.py:43
  39.2 1.1 collective-permute-start.5
  40.3 5.4 %collective-permute-done.7 = bf16[2,2,64,128]{3,2,1,0:T(8,128)(2,1)S(1)} collective-permute-done((bf16[2,2,64,128]{3,2,1,0:T(8,128)(2,1)S(1)}, bf16[2,2,64,128]{3,2,1,0:T(8,128)(2,1)S(1)}, u32[]{:S(2)}, u32[]{:S(2)}) %collective-permute-start.7) | collective-permute-done | bytes 65568 | tf_op jit(solution)/shard_map/ppermute | solution.py:43
  45.8 5.2 %collective-permute-done.6 = bf16[2,2,64,128]{3,2,1,0:T(8,128)(2,1)S(1)} collective-permute-done((bf16[2,2,64,128]{3,2,1,0:T(8,128)(2,1)S(1)}, bf16[2,2,64,128]{3,2,1,0:T(8,128)(2,1)S(1)}, u32[]{:S(2)}, u32[]{:S(2)}) %collective-permute-start.6) | collective-permute-done | bytes 65568 | tf_op jit(solution)/shard_map/ppermute | solution.py:43
  51.0 0.1 add_convert_fusion
  51.1 0.0 copy-start.9
  51.1 0.1 collective-permute-start.11
  51.2 0.1 collective-permute-start.12
  51.3 4.2 %collective-permute-done.11 = bf16[2,2,64,128]{3,2,1,0:T(8,128)(2,1)S(1)} collective-permute-done((bf16[2,2,64,128]{3,2,1,0:T(8,128)(2,1)S(1)}, bf16[2,2,64,128]{3,2,1,0:T(8,128)(2,1)S(1)}, u32[]{:S(2)}, u32[]{:S(2)}) %collective-permute-start.11) | collective-permute-done | bytes 65568 | tf_op jit(solution)/shard_map/ppermute | solution.py:43
  55.4 0.1 collective-permute-start.13
  55.6 0.9 collective-permute-done.12
  56.4 5.1 %collective-permute-done.13 = bf16[2,2,64,128]{3,2,1,0:T(8,128)(2,1)S(1)} collective-permute-done((bf16[2,2,64,128]{3,2,1,0:T(8,128)(2,1)S(1)}, bf16[2,2,64,128]{3,2,1,0:T(8,128)(2,1)S(1)}, u32[]{:S(2)}, u32[]{:S(2)}) %collective-permute-start.13) | collective-permute-done | bytes 65568 | tf_op jit(solution)/shard_map/ppermute | solution.py:43
  61.6 0.1 collective-permute-start.14
  61.6 1.5 %collective-permute-done.14.refs_4_ = bf16[4,2,2,64,128]{4,3,2,1,0:T(8,128)(2,1)S(1)} collective-permute-done((bf16[4,2,2,64,128]{4,3,2,1,0:T(8,128)(2,1)S(1)}, bf16[4,2,2,64,128]{4,3,2,1,0:T(8,128)(2,1)S(1)}, u32[]{:S(2)}, u32[]{:S(2)}) %collective-permute-start.14) | collective-permute-done | bytes 262176 | tf_op jit(solution)/shard_map/ppermute | solution.py:43
  63.2 0.7 cut.1.refs_4_
  63.8 0.1 collective-permute-start.15
  63.9 0.1 collective-permute-start.16
  64.0 20.5 %collective-permute-done.15.refs_5_ = bf16[2,2,128,128]{3,2,1,0:T(8,128)(2,1)S(1)} collective-permute-done((bf16[2,2,128,128]{3,2,1,0:T(8,128)(2,1)S(1)}, bf16[2,2,128,128]{3,2,1,0:T(8,128)(2,1)S(1)}, u32[]{:S(2)}, u32[]{:S(2)}) %collective-permute-start.15) | collective-permute-done | bytes 131104 | tf_op jit(solution)/shard_map/ppermute | solution.py:43
  84.5 1.7 %collective-permute-start.17 = (bf16[2,2,128,128]{3,2,1,0:T(8,128)(2,1)S(1)}, bf16[2,2,128,128]{3,2,1,0:T(8,128)(2,1)S(1)}, u32[]{:S(2)}, u32[]{:S(2)}) collective-permute-start(bf16[2,2,128,128]{3,2,1,0:T(8,128)(2,1)S(1)} %cut.1.refs_4_), channel_id=1, source_target_pairs={{0,24},{8,16},{16,8},{24,0},{1,25},{9,17},{17,9},{25,1},{2,26},{10... | collective-permute-start | bytes 393224 | tf_op jit(solution)/shard_map/ppermute | solution.py:43
  86.2 0.4 collective-permute-done.16.refs_6_
  86.6 3.8 %collective-permute-done.17.refs_7_ = bf16[2,2,128,128]{3,2,1,0:T(8,128)(2,1)S(1)} collective-permute-done((bf16[2,2,128,128]{3,2,1,0:T(8,128)(2,1)S(1)}, bf16[2,2,128,128]{3,2,1,0:T(8,128)(2,1)S(1)}, u32[]{:S(2)}, u32[]{:S(2)}) %collective-permute-start.17) | collective-permute-done | bytes 131104 | tf_op jit(solution)/shard_map/ppermute | solution.py:43
  90.4 2.9 %half_step.1 = (f32[2,16,128,128]{3,2,1,0:T(8,128)S(1)}, bf16[2,1,128,128]{3,2,1,0:T(8,128)(2,1)S(1)}, bf16[2,1,128,128]{3,2,1,0:T(8,128)(2,1)S(1)}, bf16[2,7,12...) custom-call(bf16[2,128,2048]{2,1,0:T(8,128)(2,1)S(1)} %get-tuple-element.26.refs_0_, ...), custom_call_target="tpu_custom_call" | custom-call | tf_op jit(solution)/shard_map/half_step/pallas_call | solution.py:485
  93.3 1.6 %second_part.1 = (bf16[2,7,128,128]{3,2,1,0:T(8,128)(2,1)S(1)}, f32[2,7,128,128]{3,2,1,0:T(8,128)S(1)}) custom-call(f32[2,16,128,128]{3,2,1,0:T(8,128)S(1)} %get-tuple-element.40.half_ref), custom_call_target="tpu_custom_call" | custom-call | tf_op jit(solution)/shard_map/second_part/pallas_call | solution.py:509
  95.0 2.8 %collective-permute-start.24 = (bf16[2,7,128,128]{3,2,1,0:T(8,128)(2,1)S(1)}, bf16[2,7,128,128]{3,2,1,0:T(8,128)(2,1)S(1)}, u32[]{:S(2)}, u32[]{:S(2)}) collective-permute-start(bf16[2,7,128,128]{3,2,1,0:T(8,128)(2,1)S(1)} %get-tuple-element.47), channel_id=1, source_target_pairs={{0,16},{8,24},{16,0},{24,8},{1,17},{9,25},{17,1},{25,9},{2,18},{10... | collective-permute-start | bytes 1376264 | tf_op jit(solution)/shard_map/ppermute | solution.py:43
  97.8 0.8 collective-permute-start.28
  98.6 3.2 %collective-permute-start.18 = (bf16[2,1,128,128]{3,2,1,0:T(8,128)(2,1)S(1)}, bf16[2,1,128,128]{3,2,1,0:T(8,128)(2,1)S(1)}, u32[]{:S(2)}, u32[]{:S(2)}) collective-permute-start(bf16[2,1,128,128]{3,2,1,0:T(8,128)(2,1)S(1)} %get-tuple-element.41), channel_id=1, source_target_pairs={{0,8},{8,24},{24,16},{16,17},{17,25},{25,9},{9,1},{1,2},{2,10},{10... | collective-permute-start | bytes 196616 | tf_op jit(solution)/shard_map/ppermute | solution.py:685
  101.8 2.0 %collective-permute-start.27 = (bf16[2,7,128,128]{3,2,1,0:T(8,128)(2,1)S(1)}, bf16[2,7,128,128]{3,2,1,0:T(8,128)(2,1)S(1)}, u32[]{:S(2)}, u32[]{:S(2)}) collective-permute-start(bf16[2,7,128,128]{3,2,1,0:T(8,128)(2,1)S(1)} %get-tuple-element.47), channel_id=1, source_target_pairs={{0,8},{8,0},{16,24},{24,16},{1,9},{9,1},{17,25},{25,17},{2,10},{10... | collective-permute-start | bytes 1376264 | tf_op jit(solution)/shard_map/ppermute | solution.py:43
  103.8 5.3 %collective-permute-done.24.refs_1_ = bf16[2,7,128,128]{3,2,1,0:T(8,128)(2,1)S(1)} collective-permute-done((bf16[2,7,128,128]{3,2,1,0:T(8,128)(2,1)S(1)}, bf16[2,7,128,128]{3,2,1,0:T(8,128)(2,1)S(1)}, u32[]{:S(2)}, u32[]{:S(2)}) %collective-permute-start.24) | collective-permute-done | bytes 458784 | tf_op jit(solution)/shard_map/ppermute | solution.py:43
  109.1 0.8 collective-permute-start.25
  110.0 1.2 collective-permute-done.22.refs_0_
  111.1 0.1 collective-permute-start.23
  111.2 1.3 collective-permute-start.19
  112.5 16.3 %collective-permute-done.19.after_ref = bf16[2,1,128,128]{3,2,1,0:T(8,128)(2,1)S(1)} collective-permute-done((bf16[2,1,128,128]{3,2,1,0:T(8,128)(2,1)S(1)}, bf16[2,1,128,128]{3,2,1,0:T(8,128)(2,1)S(1)}, u32[]{:S(2)}, u32[]{:S(2)}) %collective-permute-start.19) | collective-permute-done | bytes 65568 | tf_op jit(solution)/shard_map/ppermute | solution.py:686
  128.8 1.6 %third_part.1 = (bf16[2,2,128,128]{3,2,1,0:T(8,128)(2,1)S(1)}, f32[2,64,128,128]{3,2,1,0:T(8,128)}) custom-call(f32[2,16,128,128]{3,2,1,0:T(8,128)S(1)} %get-tuple-element.40.half_ref, bf16[2,1,128,128]{3,2,1,0:T(8,128)(2,1)S(1)} %collective-permute-done.18.before_ref, bf16[2,1,128,128]{3,2,1,0:T(8,128)(2,1)S(1)} %collective-permute-done.19.after_ref, ...), custom_call_target="tpu_custom_call" | custom-call | tf_op jit(solution)/shard_map/third_part/pallas_call | solution.py:556
  130.5 0.1 collective-permute-start.20
  130.6 5.0 %collective-permute-done.20.refs_0_ = bf16[2,2,128,128]{3,2,1,0:T(8,128)(2,1)S(1)} collective-permute-done((bf16[2,2,128,128]{3,2,1,0:T(8,128)(2,1)S(1)}, bf16[2,2,128,128]{3,2,1,0:T(8,128)(2,1)S(1)}, u32[]{:S(2)}, u32[]{:S(2)}) %collective-permute-start.20) | collective-permute-done | bytes 131104 | tf_op jit(solution)/shard_map/ppermute | solution.py:43
  135.5 2.0 %collective-permute-start.21 = (bf16[2,2,128,128]{3,2,1,0:T(8,128)(2,1)S(1)}, bf16[2,2,128,128]{3,2,1,0:T(8,128)(2,1)S(1)}, u32[]{:S(2)}, u32[]{:S(2)}) collective-permute-start(bf16[2,2,128,128]{3,2,1,0:T(8,128)(2,1)S(1)} %collective-permute-done.20.refs_0_), channel_id=1, source_target_pairs={{0,16},{8,24},{16,0},{24,8},{1,17},{9,25},{17,1},{25,9},{2,18},{10... | collective-permute-start | bytes 393224 | tf_op jit(solution)/shard_map/ppermute | solution.py:43
  137.5 0.7 add_subtract_fusion
  138.2 1.3 place.5.refs_2_
  139.6 1.3 place.6.refs_2_
  140.9 0.9 place.7.refs_2_
  141.8 1.3 place.8.refs_1_
  143.1 0.7 place.9
  (33 shorter events, 0.2 us)
Async XLA Ops:
  2.2 7.2 %copy-start = (f32[2,2,64,128]{3,2,1,0:T(8,128)S(1)}, f32[2,2,64,128]{3,2,1,0:T(8,128)}, u32[]{:S(2)}) copy-start(f32[2,2,64,128]{3,2,1,0:T(8,128)} %own_ref.1) | copy-start | bytes 393220
  2.2 17.8 %copy-start.2 = (s32[2,32,128,128]{3,2,1,0:T(8,128)S(1)}, s32[2,32,128,128]{3,2,1,0:T(8,128)}, u32[]{:S(2)}) copy-start(s32[2,32,128,128]{3,2,1,0:T(8,128)} %counts_ref.1) | copy-start | bytes 12582916
  2.2 17.7 %copy-start.3 = (f32[2,128,128]{2,1,0:T(8,128)S(1)}, f32[2,128,128]{2,1,0:T(8,128)}, u32[]{:S(2)}) copy-start(f32[2,128,128]{2,1,0:T(8,128)} %probe_ref.1) | copy-start | bytes 393220
  2.2 17.7 %copy-start.4 = (s32[2,32]{1,0:T(2,128)S(1)}, s32[2,32]{1,0:T(2,128)}, u32[]{:S(2)}) copy-start(s32[2,32]{1,0:T(2,128)} %positions.1) | copy-start | bytes 772
  2.3 17.7 %copy-start.5 = (s32[2,1]{0,1:T(1,128)S(1)}, s32[2,1]{0,1:T(1,128)}, u32[]{:S(2)}) copy-start(s32[2,1]{0,1:T(1,128)} %param.15) | copy-start | bytes 28
  2.3 17.7 %copy-start.6 = (bf16[256,256]{1,0:T(8,128)(2,1)S(1)}, bf16[256,256]{1,0:T(8,128)(2,1)}, u32[]{:S(2)}) copy-start(bf16[256,256]{1,0:T(8,128)(2,1)} %constant.17.forward_ref) | copy-start | bytes 393220
  2.3 17.7 %copy-start.7 = (bf16[256,256]{1,0:T(8,128)(2,1)S(1)}, bf16[256,256]{1,0:T(8,128)(2,1)}, u32[]{:S(2)}) copy-start(bf16[256,256]{1,0:T(8,128)(2,1)} %constant.18.inverse_ref) | copy-start | bytes 393220
  4.0 47.0 %copy-start.8 = (f32[2,2,64,128]{3,2,1,0:T(8,128)S(1)}, f32[2,2,64,128]{3,2,1,0:T(8,128)}, u32[]{:S(2)}) copy-start(f32[2,2,64,128]{3,2,1,0:T(8,128)} %param.12) | copy-start | bytes 393220
  8.8 54.3 %copy-start.1 = (s32[2,1]{0,1:T(1,128)S(1)}, s32[2,1]{0,1:T(1,128)}, u32[]{:S(2)}) copy-start(s32[2,1]{0,1:T(1,128)} %param.17) | copy-start | bytes 28
  8.8 3.2 %collective-permute-start.2 = (bf16[4,2,2,64,128]{4,3,2,1,0:T(8,128)(2,1)S(1)}, bf16[4,2,2,64,128]{4,3,2,1,0:T(8,128)(2,1)S(1)}, u32[]{:S(2)}, u32[]{:S(2)}) collective-permute-start(bf16[4,2,2,64,128]{4,3,2,1,0:T(8,128)(2,1)S(1)} %get-tuple-element.31), channel_id=1, source_target_pairs={{0,1},{1,0},{2,3},{3,2},{4,5},{5,4},{6,7},{7,6},{8,9},{9,8},{10,11... | collective-permute-start | bytes 786440 | tf_op jit(solution)/shard_map/ppermute | solution.py:43
  9.4 3.2 %collective-permute-start = (f32[2,2,64,128]{3,2,1,0:T(8,128)S(1)}, f32[2,2,64,128]{3,2,1,0:T(8,128)S(1)}, u32[]{:S(2)}, u32[]{:S(2)}) collective-permute-start(f32[2,2,64,128]{3,2,1,0:T(8,128)S(1)} %copy-done), channel_id=1, source_target_pairs={{1,0},{2,1},{3,2},{4,3},{5,4},{6,5},{7,6},{9,8},{10,9},{11,10},{12... | collective-permute-start | bytes 393224 | tf_op jit(solution)/shard_map/ppermute | solution.py:26
  10.7 9.3 %collective-permute-start.1 = (f32[2,2,64,128]{3,2,1,0:T(8,128)S(1)}, f32[2,2,64,128]{3,2,1,0:T(8,128)S(1)}, u32[]{:S(2)}, u32[]{:S(2)}) collective-permute-start(f32[2,2,64,128]{3,2,1,0:T(8,128)S(1)} %copy-done), channel_id=1, source_target_pairs={{2,0},{3,1},{4,2},{5,3},{6,4},{7,5},{10,8},{11,9},{12,10},{13,11},... | collective-permute-start | bytes 393224 | tf_op jit(solution)/shard_map/ppermute | solution.py:26
  25.6 13.6 %collective-permute-start.3 = (bf16[2,3,64,128]{3,2,1,0:T(8,128)(2,1)S(1)}, bf16[2,3,64,128]{3,2,1,0:T(8,128)(2,1)S(1)}, u32[]{:S(2)}, u32[]{:S(2)}) collective-permute-start(bf16[2,3,64,128]{3,2,1,0:T(8,128)(2,1)S(1)} %get-tuple-element.34), channel_id=1, source_target_pairs={{0,1},{1,2},{2,3},{3,4},{4,5},{5,6},{6,7},{8,9},{9,10},{10,11},{11... | collective-permute-start | bytes 294920 | tf_op jit(solution)/shard_map/ppermute | solution.py:26
  27.4 11.8 %collective-permute-start.4 = (bf16[2,3,64,128]{3,2,1,0:T(8,128)(2,1)S(1)}, bf16[2,3,64,128]{3,2,1,0:T(8,128)(2,1)S(1)}, u32[]{:S(2)}, u32[]{:S(2)}) collective-permute-start(bf16[2,3,64,128]{3,2,1,0:T(8,128)(2,1)S(1)} %get-tuple-element.35), channel_id=1, source_target_pairs={{0,2},{1,3},{2,4},{3,5},{4,6},{5,7},{8,10},{9,11},{10,12},{11,13},... | collective-permute-start | bytes 294920 | tf_op jit(solution)/shard_map/ppermute | solution.py:26
  35.6 54.8 %collective-permute-start.10 = (bf16[2,128,2048]{2,1,0:T(8,128)(2,1)S(1)}, bf16[2,128,2048]{2,1,0:T(8,128)(2,1)S(1)}, u32[]{:S(2)}, u32[]{:S(2)}) collective-permute-start(bf16[2,128,2048]{2,1,0:T(8,128)(2,1)S(1)} %get-tuple-element.29.refs_3_), channel_id=1, source_target_pairs={{0,24},{8,16},{16,8},{24,0},{1,25},{9,17},{17,9},{25,1},{2,26},{10... | collective-permute-start | bytes 3145736 | tf_op jit(solution)/shard_map/ppermute | solution.py:43
  35.7 54.7 %collective-permute-start.8 = (bf16[2,128,2048]{2,1,0:T(8,128)(2,1)S(1)}, bf16[2,128,2048]{2,1,0:T(8,128)(2,1)S(1)}, u32[]{:S(2)}, u32[]{:S(2)}) collective-permute-start(bf16[2,128,2048]{2,1,0:T(8,128)(2,1)S(1)} %get-tuple-element.27.refs_1_), channel_id=1, source_target_pairs={{0,8},{8,0},{16,24},{24,16},{1,9},{9,1},{17,25},{25,17},{2,10},{10... | collective-permute-start | bytes 3145736 | tf_op jit(solution)/shard_map/ppermute | solution.py:43
  36.7 53.7 %collective-permute-start.9 = (bf16[2,128,2048]{2,1,0:T(8,128)(2,1)S(1)}, bf16[2,128,2048]{2,1,0:T(8,128)(2,1)S(1)}, u32[]{:S(2)}, u32[]{:S(2)}) collective-permute-start(bf16[2,128,2048]{2,1,0:T(8,128)(2,1)S(1)} %get-tuple-element.28.refs_2_), channel_id=1, source_target_pairs={{0,16},{8,24},{16,0},{24,8},{1,17},{9,25},{17,1},{25,9},{2,18},{10... | collective-permute-start | bytes 3145736 | tf_op jit(solution)/shard_map/ppermute | solution.py:43
  39.1 6.6 %collective-permute-start.7 = (bf16[2,2,64,128]{3,2,1,0:T(8,128)(2,1)S(1)}, bf16[2,2,64,128]{3,2,1,0:T(8,128)(2,1)S(1)}, u32[]{:S(2)}, u32[]{:S(2)}) collective-permute-start(bf16[2,2,64,128]{3,2,1,0:T(8,128)(2,1)S(1)} %get-tuple-element.32.token_ref), channel_id=1, source_target_pairs={{0,6},{1,7},{2,4},{3,5},{4,2},{5,3},{6,0},{7,1},{8,14},{9,15},{10,... | collective-permute-start | bytes 196616 | tf_op jit(solution)/shard_map/ppermute | solution.py:43
  39.2 6.6 %collective-permute-start.5 = (bf16[2,2,64,128]{3,2,1,0:T(8,128)(2,1)S(1)}, bf16[2,2,64,128]{3,2,1,0:T(8,128)(2,1)S(1)}, u32[]{:S(2)}, u32[]{:S(2)}) collective-permute-start(bf16[2,2,64,128]{3,2,1,0:T(8,128)(2,1)S(1)} %get-tuple-element.37), channel_id=1, source_target_pairs={{0,2},{1,3},{2,0},{3,1},{4,6},{5,7},{6,4},{7,5},{8,10},{9,11},{10,... | collective-permute-start | bytes 196616 | tf_op jit(solution)/shard_map/ppermute | solution.py:43
  45.7 5.3 %collective-permute-start.6 = (bf16[2,2,64,128]{3,2,1,0:T(8,128)(2,1)S(1)}, bf16[2,2,64,128]{3,2,1,0:T(8,128)(2,1)S(1)}, u32[]{:S(2)}, u32[]{:S(2)}) collective-permute-start(bf16[2,2,64,128]{3,2,1,0:T(8,128)(2,1)S(1)} %get-tuple-element.38), channel_id=1, source_target_pairs={{0,4},{1,5},{2,6},{3,7},{4,0},{5,1},{6,2},{7,3},{8,12},{9,13},{10,... | collective-permute-start | bytes 196616 | tf_op jit(solution)/shard_map/ppermute | solution.py:43
  51.1 88.4 %copy-start.9 = (f32[2,2,64,128]{3,2,1,0:T(8,128)}, f32[2,2,64,128]{3,2,1,0:T(8,128)S(1)}, u32[]{:S(2)}) copy-start(f32[2,2,64,128]{3,2,1,0:T(8,128)S(1)} %get-tuple-element.50) | copy-start | bytes 393220
  51.1 4.3 %collective-permute-start.11 = (bf16[2,2,64,128]{3,2,1,0:T(8,128)(2,1)S(1)}, bf16[2,2,64,128]{3,2,1,0:T(8,128)(2,1)S(1)}, u32[]{:S(2)}, u32[]{:S(2)}) collective-permute-start(bf16[2,2,64,128]{3,2,1,0:T(8,128)(2,1)S(1)} %get-tuple-element.49), channel_id=1, source_target_pairs={{0,2},{1,3},{2,0},{3,1},{4,6},{5,7},{6,4},{7,5},{8,10},{9,11},{10,... | collective-permute-start | bytes 196616 | tf_op jit(solution)/shard_map/ppermute | solution.py:43
  51.2 5.2 %collective-permute-start.12 = (bf16[2,2,64,128]{3,2,1,0:T(8,128)(2,1)S(1)}, bf16[2,2,64,128]{3,2,1,0:T(8,128)(2,1)S(1)}, u32[]{:S(2)}, u32[]{:S(2)}) collective-permute-start(bf16[2,2,64,128]{3,2,1,0:T(8,128)(2,1)S(1)} %get-tuple-element.49), channel_id=1, source_target_pairs={{0,4},{1,5},{2,6},{3,7},{4,0},{5,1},{6,2},{7,3},{8,12},{9,13},{10,... | collective-permute-start | bytes 196616 | tf_op jit(solution)/shard_map/ppermute | solution.py:43
  55.4 6.1 %collective-permute-start.13 = (bf16[2,2,64,128]{3,2,1,0:T(8,128)(2,1)S(1)}, bf16[2,2,64,128]{3,2,1,0:T(8,128)(2,1)S(1)}, u32[]{:S(2)}, u32[]{:S(2)}) collective-permute-start(bf16[2,2,64,128]{3,2,1,0:T(8,128)(2,1)S(1)} %get-tuple-element.49), channel_id=1, source_target_pairs={{0,6},{1,7},{2,4},{3,5},{4,2},{5,3},{6,0},{7,1},{8,14},{9,15},{10,... | collective-permute-start | bytes 196616 | tf_op jit(solution)/shard_map/ppermute | solution.py:43
  61.6 1.6 %collective-permute-start.14 = (bf16[4,2,2,64,128]{4,3,2,1,0:T(8,128)(2,1)S(1)}, bf16[4,2,2,64,128]{4,3,2,1,0:T(8,128)(2,1)S(1)}, u32[]{:S(2)}, u32[]{:S(2)}) collective-permute-start(bf16[4,2,2,64,128]{4,3,2,1,0:T(8,128)(2,1)S(1)} %pad_maximum_fusion), channel_id=1, source_target_pairs={{0,1},{1,0},{2,3},{3,2},{4,5},{5,4},{6,7},{7,6},{8,9},{9,8},{10,11... | collective-permute-start | bytes 786440 | tf_op jit(solution)/shard_map/ppermute | solution.py:43
  63.8 20.7 %collective-permute-start.15 = (bf16[2,2,128,128]{3,2,1,0:T(8,128)(2,1)S(1)}, bf16[2,2,128,128]{3,2,1,0:T(8,128)(2,1)S(1)}, u32[]{:S(2)}, u32[]{:S(2)}) collective-permute-start(bf16[2,2,128,128]{3,2,1,0:T(8,128)(2,1)S(1)} %cut.1.refs_4_), channel_id=1, source_target_pairs={{0,8},{8,0},{16,24},{24,16},{1,9},{9,1},{17,25},{25,17},{2,10},{10... | collective-permute-start | bytes 393224 | tf_op jit(solution)/shard_map/ppermute | solution.py:43
  63.9 22.7 %collective-permute-start.16 = (bf16[2,2,128,128]{3,2,1,0:T(8,128)(2,1)S(1)}, bf16[2,2,128,128]{3,2,1,0:T(8,128)(2,1)S(1)}, u32[]{:S(2)}, u32[]{:S(2)}) collective-permute-start(bf16[2,2,128,128]{3,2,1,0:T(8,128)(2,1)S(1)} %cut.1.refs_4_), channel_id=1, source_target_pairs={{0,16},{8,24},{16,0},{24,8},{1,17},{9,25},{17,1},{25,9},{2,18},{10... | collective-permute-start | bytes 393224 | tf_op jit(solution)/shard_map/ppermute | solution.py:43
  84.5 5.9 %collective-permute-start.17 = (bf16[2,2,128,128]{3,2,1,0:T(8,128)(2,1)S(1)}, bf16[2,2,128,128]{3,2,1,0:T(8,128)(2,1)S(1)}, u32[]{:S(2)}, u32[]{:S(2)}) collective-permute-start(bf16[2,2,128,128]{3,2,1,0:T(8,128)(2,1)S(1)} %cut.1.refs_4_), channel_id=1, source_target_pairs={{0,24},{8,16},{16,8},{24,0},{1,25},{9,17},{17,9},{25,1},{2,26},{10... | collective-permute-start | bytes 393224 | tf_op jit(solution)/shard_map/ppermute | solution.py:43
  95.0 14.2 %collective-permute-start.24 = (bf16[2,7,128,128]{3,2,1,0:T(8,128)(2,1)S(1)}, bf16[2,7,128,128]{3,2,1,0:T(8,128)(2,1)S(1)}, u32[]{:S(2)}, u32[]{:S(2)}) collective-permute-start(bf16[2,7,128,128]{3,2,1,0:T(8,128)(2,1)S(1)} %get-tuple-element.47), channel_id=1, source_target_pairs={{0,16},{8,24},{16,0},{24,8},{1,17},{9,25},{17,1},{25,9},{2,18},{10... | collective-permute-start | bytes 1376264 | tf_op jit(solution)/shard_map/ppermute | solution.py:43
  97.8 13.4 %collective-permute-start.22 = (bf16[2,7,128,128]{3,2,1,0:T(8,128)(2,1)S(1)}, bf16[2,7,128,128]{3,2,1,0:T(8,128)(2,1)S(1)}, u32[]{:S(2)}, u32[]{:S(2)}) collective-permute-start(bf16[2,7,128,128]{3,2,1,0:T(8,128)(2,1)S(1)} %get-tuple-element.46), channel_id=1, source_target_pairs={{0,8},{8,0},{16,24},{24,16},{1,9},{9,1},{17,25},{25,17},{2,10},{10... | collective-permute-start | bytes 1376264 | tf_op jit(solution)/shard_map/ppermute | solution.py:43
  97.8 37.8 %collective-permute-start.28 = (bf16[2,7,128,128]{3,2,1,0:T(8,128)(2,1)S(1)}, bf16[2,7,128,128]{3,2,1,0:T(8,128)(2,1)S(1)}, u32[]{:S(2)}, u32[]{:S(2)}) collective-permute-start(bf16[2,7,128,128]{3,2,1,0:T(8,128)(2,1)S(1)} %get-tuple-element.46), channel_id=1, source_target_pairs={{0,16},{8,24},{16,0},{24,8},{1,17},{9,25},{17,1},{25,9},{2,18},{10... | collective-permute-start | bytes 1376264 | tf_op jit(solution)/shard_map/ppermute | solution.py:43
  98.6 12.6 %collective-permute-start.18 = (bf16[2,1,128,128]{3,2,1,0:T(8,128)(2,1)S(1)}, bf16[2,1,128,128]{3,2,1,0:T(8,128)(2,1)S(1)}, u32[]{:S(2)}, u32[]{:S(2)}) collective-permute-start(bf16[2,1,128,128]{3,2,1,0:T(8,128)(2,1)S(1)} %get-tuple-element.41), channel_id=1, source_target_pairs={{0,8},{8,24},{24,16},{16,17},{17,25},{25,9},{9,1},{1,2},{2,10},{10... | collective-permute-start | bytes 196616 | tf_op jit(solution)/shard_map/ppermute | solution.py:685
  101.8 37.8 %collective-permute-start.27 = (bf16[2,7,128,128]{3,2,1,0:T(8,128)(2,1)S(1)}, bf16[2,7,128,128]{3,2,1,0:T(8,128)(2,1)S(1)}, u32[]{:S(2)}, u32[]{:S(2)}) collective-permute-start(bf16[2,7,128,128]{3,2,1,0:T(8,128)(2,1)S(1)} %get-tuple-element.47), channel_id=1, source_target_pairs={{0,8},{8,0},{16,24},{24,16},{1,9},{9,1},{17,25},{25,17},{2,10},{10... | collective-permute-start | bytes 1376264 | tf_op jit(solution)/shard_map/ppermute | solution.py:43
  109.1 32.7 %collective-permute-start.25 = (bf16[2,7,128,128]{3,2,1,0:T(8,128)(2,1)S(1)}, bf16[2,7,128,128]{3,2,1,0:T(8,128)(2,1)S(1)}, u32[]{:S(2)}, u32[]{:S(2)}) collective-permute-start(bf16[2,7,128,128]{3,2,1,0:T(8,128)(2,1)S(1)} %collective-permute-done.24.refs_1_), channel_id=1, source_target_pairs={{0,8},{8,0},{16,24},{24,16},{1,9},{9,1},{17,25},{25,17},{2,10},{10... | collective-permute-start | bytes 1376264 | tf_op jit(solution)/shard_map/ppermute | solution.py:43
  111.1 30.6 %collective-permute-start.23 = (bf16[2,7,128,128]{3,2,1,0:T(8,128)(2,1)S(1)}, bf16[2,7,128,128]{3,2,1,0:T(8,128)(2,1)S(1)}, u32[]{:S(2)}, u32[]{:S(2)}) collective-permute-start(bf16[2,7,128,128]{3,2,1,0:T(8,128)(2,1)S(1)} %collective-permute-done.22.refs_0_), channel_id=1, source_target_pairs={{0,16},{8,24},{16,0},{24,8},{1,17},{9,25},{17,1},{25,9},{2,18},{10... | collective-permute-start | bytes 1376264 | tf_op jit(solution)/shard_map/ppermute | solution.py:43
  111.2 17.6 %collective-permute-start.19 = (bf16[2,1,128,128]{3,2,1,0:T(8,128)(2,1)S(1)}, bf16[2,1,128,128]{3,2,1,0:T(8,128)(2,1)S(1)}, u32[]{:S(2)}, u32[]{:S(2)}) collective-permute-start(bf16[2,1,128,128]{3,2,1,0:T(8,128)(2,1)S(1)} %get-tuple-element.42), channel_id=1, source_target_pairs={{8,0},{24,8},{16,24},{17,16},{25,17},{9,25},{1,9},{2,1},{10,2},{26... | collective-permute-start | bytes 196616 | tf_op jit(solution)/shard_map/ppermute | solution.py:686
  130.5 5.0 %collective-permute-start.20 = (bf16[2,2,128,128]{3,2,1,0:T(8,128)(2,1)S(1)}, bf16[2,2,128,128]{3,2,1,0:T(8,128)(2,1)S(1)}, u32[]{:S(2)}, u32[]{:S(2)}) collective-permute-start(bf16[2,2,128,128]{3,2,1,0:T(8,128)(2,1)S(1)} %get-tuple-element.45), channel_id=1, source_target_pairs={{0,8},{8,0},{16,24},{24,16},{1,9},{9,1},{17,25},{25,17},{2,10},{10... | collective-permute-start | bytes 393224 | tf_op jit(solution)/shard_map/ppermute | solution.py:43
  135.5 5.4 %collective-permute-start.26 = (bf16[2,2,128,128]{3,2,1,0:T(8,128)(2,1)S(1)}, bf16[2,2,128,128]{3,2,1,0:T(8,128)(2,1)S(1)}, u32[]{:S(2)}, u32[]{:S(2)}) collective-permute-start(bf16[2,2,128,128]{3,2,1,0:T(8,128)(2,1)S(1)} %get-tuple-element.45), channel_id=1, source_target_pairs={{0,16},{8,24},{16,0},{24,8},{1,17},{9,25},{17,1},{25,9},{2,18},{10... | collective-permute-start | bytes 393224 | tf_op jit(solution)/shard_map/ppermute | solution.py:43
  135.5 7.6 %collective-permute-start.21 = (bf16[2,2,128,128]{3,2,1,0:T(8,128)(2,1)S(1)}, bf16[2,2,128,128]{3,2,1,0:T(8,128)(2,1)S(1)}, u32[]{:S(2)}, u32[]{:S(2)}) collective-permute-start(bf16[2,2,128,128]{3,2,1,0:T(8,128)(2,1)S(1)} %collective-permute-done.20.refs_0_), channel_id=1, source_target_pairs={{0,16},{8,24},{16,0},{24,8},{1,17},{9,25},{17,1},{25,9},{2,18},{10... | collective-permute-start | bytes 393224 | tf_op jit(solution)/shard_map/ppermute | solution.py:43

commit v4 on v3

--- a/solution.py
+++ b/solution.py
@@ -110,7 +110,7 @@
 
 
 def project_kernel(pieces, footprints_ref, volume_ref, *refs):
-    *shares, keep_ref, send_ref, part_ref, footprints, held, sem, sems = refs
+    *shares, keep_ref, send_ref, part_ref, footprints, sem = refs
     groups = len(shares)
     views, cols, _ = shares[0].shape
     _, count, depth, rows = part_ref.shape
@@ -119,27 +119,15 @@
     span = chunk * depth
     spots_copy = pltpu.make_async_copy(footprints_ref, footprints, sem)
     spots_copy.start()
-    copies = []
-    for j in range(groups):
-        first = share_at(j, groups) * count
-        for i in range(pieces):
-            copies.append(
-                pltpu.make_async_copy(
-                    volume_ref.at[:, pl.ds(first + i * chunk, chunk)],
-                    held.at[j, :, pl.ds(i * chunk, chunk)],
-                    sems.at[j, i],
-                )
-            )
-            copies[-1].start()
     keep_ref[...] = jnp.zeros_like(keep_ref)
     send_ref[...] = jnp.zeros_like(send_ref)
     total = jnp.zeros((views * cols, 2 * rows), F32)
     for j, ref in enumerate(shares):
+        at = share_at(j, groups) * count
         for i in range(pieces):
-            copies[j * pieces + i].wait()
             low = jnp.concatenate(
                 [
-                    held[j, k, i * chunk : (i + 1) * chunk].reshape(span, rows).astype(BF16)
+                    volume_ref[k, pl.ds(at + i * chunk, chunk)].reshape(span, rows).astype(BF16)
                     for k in range(2)
                 ],
                 axis=1,
@@ -150,7 +138,7 @@
                 preferred_element_type=F32,
             )
         if j == 0:
-            part_ref[...] = held[0]
+            part_ref[...] = volume_ref[:, pl.ds(at, count)]
     spots_copy.wait()
     spots = ranks(footprints, views, cols // width, 2 * half)
     for v in range(views):
@@ -182,17 +170,15 @@
     return pl.pallas_call(
         functools.partial(project_kernel, pieces),
         out_shape=(placed, placed, VMEM((2, count, depth, rows), F32)),
-        in_specs=[hbm, hbm] + [vmem] * groups,
+        in_specs=[hbm, vmem] + [vmem] * groups,
         out_specs=(vmem,) * 3,
         scratch_shapes=[
             SMEM(footprints.shape, jnp.int32),
-            VMEM((groups, 2, count, depth, rows), F32),
             pltpu.SemaphoreType.DMA(()),
-            pltpu.SemaphoreType.DMA((groups, pieces)),
         ],
         compiler_params=limit(20),
         name="project",
-    )(*far(footprints, volume), *near(*shares))
+    )(*far(footprints), volume, *near(*shares))
 
 
 def fold_kernel(keep_ref, arrived_ref, *refs):
@@ -238,7 +224,7 @@
     cols = probe_ref.shape[1]
     span = 3 * width
     for part, ref in enumerate((own_ref, one_ref, two_ref)):
-        reach[:, :, part * width : (part + 1) * width, :] = ref[...]
+        reach[:, :, part * width : (part + 1) * width, :] = ref[...].astype(F32)
     total[...] = jnp.zeros_like(total)
     starts = [0]
     for v in range(views):
@@ -401,6 +387,11 @@
     )(footprints, *near(*pieces))
 
 
+def inner_runs(share):
+    first = max(1, share // 2 - 2)
+    return ((1, first), (1 + first, share - 2 - first))
+
+
 def bent(d):
     return d * lax.rsqrt(1.0 + d * d)
 
@@ -473,7 +464,7 @@
             half_ref[k, held] = volume_ref[k, held] - step_size * plane
     low_ref[...] = half_ref[:, :1].astype(BF16)
     high_ref[...] = half_ref[:, share - 1 :].astype(BF16)
-    inner_columns(half_ref, part_ref, fresh_ref, 1)
+    inner_columns(half_ref, part_ref, fresh_ref, inner_runs(share)[0][0])
 
 
 def half_step_of(weights, windows, volume):
@@ -481,7 +472,7 @@
     _, share, depth, rows = volume.shape
     vmem = pl.BlockSpec(memory_space=VMEM)
     edge = VMEM((2, 1, depth, rows), BF16)
-    inner = (2, share // 2 - 1, depth, rows)
+    inner = (2, inner_runs(share)[0][1], depth, rows)
     return pl.pallas_call(
         functools.partial(gradient_kernel, groups, min(4, share)),
         out_shape=(
@@ -499,13 +490,13 @@
 
 
 def second_kernel(half_ref, part_ref, fresh_ref):
-    inner_columns(half_ref, part_ref, fresh_ref, part_ref.shape[1] + 1)
+    inner_columns(half_ref, part_ref, fresh_ref, inner_runs(half_ref.shape[1])[1][0])
 
 
 def second_part(half):
     _, share, depth, rows = half.shape
     vmem = pl.BlockSpec(memory_space=VMEM)
-    inner = (2, share // 2 - 1, depth, rows)
+    inner = (2, inner_runs(share)[1][1], depth, rows)
     return pl.pallas_call(
         second_kernel,
         out_shape=(VMEM(inner, BF16), VMEM(inner, F32)),
@@ -519,7 +510,6 @@
 def third_kernel(half_ref, before_ref, after_ref, first_ref, second_ref, part_ref, whole_ref, *rest):
     edges, sems = rest
     share = half_ref.shape[1]
-    inner = first_ref.shape[1]
     start = share_at(0, whole_ref.shape[1] // share) * share
     puts = []
 
@@ -531,8 +521,8 @@
         )
         puts[-1].start()
 
-    put(first_ref, 1, inner)
-    put(second_ref, inner + 1, inner)
+    for ref, run in zip((first_ref, second_ref), inner_runs(share)):
+        put(ref, *run)
     for k in range(2):
         for n, (c, before, after) in enumerate(
             (
@@ -571,11 +561,10 @@
     count = len(kinds)
     parts, whole_ref, fresh, sems = refs[:count], refs[count + 1], refs[count + 2 : -1], refs[-1]
     share = whole_ref.shape[1] // groups
-    inner = share // 2 - 1
     puts = []
     for n, ((kind, j), ref) in enumerate(zip(kinds, parts)):
         first = share_at(j, groups) * share
-        runs = ((0, 0, 1), (1, share - 1, 1)) if kind == 2 else ((0, kind * inner + 1, inner),)
+        runs = ((0, 0, 1), (1, share - 1, 1)) if kind == 2 else ((0, *inner_runs(share)[kind]),)
         for place, (source, target, count) in enumerate(runs):
             for k in range(2):
                 fresh[n][k, source : source + count] = ref[k, source : source + count].astype(F32)
@@ -627,6 +616,7 @@
 
     view_masks = masks_of(groups)
     later = [j for j in range(groups) if j not in view_masks]
+    object_low = object_band.astype(BF16)
     early_shares = deal(weights, groups, view_masks)
     late_shares = deal(weights, groups, later)
     dealt = dict(zip(view_masks + later, early_shares + late_shares))
@@ -635,8 +625,8 @@
     for j in range(1, groups):
         weight_pieces.append(swapped(dealt[j], "view", j))
     keep, send, volume_own = project(footprints, dealt, volume, tiles, tile_cols)
-    ahead_one = passed_along(object_band, "tile", -1)
-    ahead_two = passed_along(object_band, "tile", -2)
+    ahead_one = passed_along(object_low, "tile", -1)
+    ahead_two = passed_along(object_low, "tile", -2)
     arrived = swapped(send, "tile", 1)
     projection, *rest = fold(keep, arrived)
     token = rest[-1]
@@ -694,7 +684,7 @@
         held.update(arrived)
     rounds = [[(kind, mask) for mask in view_masks] for kind in range(3)]
     far_keys = [j for j in range(1, groups) if j not in view_masks]
-    rounds += [[(0, j), (1, j)] for j in far_keys] + [[(2, j)] for j in far_keys]
+    rounds += [[(0, j)] for j in far_keys] + [[(2, j), (1, j)] for j in far_keys]
     for keys in rounds:
         volume_new = place(keys, [held[key] for key in keys], volume_new, groups)
     return (object_new, dual_new, volume_new)

time: 144 us -> 146 us (1.014)
  starting transfers between devices: 33.1 us -> 37.4 us
  Pallas kernels: 26.2 us -> 23.8 us
    ppermute x1, waiting for transfers between devices: 16.3 us -> 2.07 us  [per_device(): after = lax.ppermute(low_edge, ('view', 'tile'), [(b, a) for a, b in up])]
    ppermute x1, waiting for transfers between devices: 0.01 us -> 12.7 us  [per_device(): before = lax.ppermute(high_edge, ('view', 'tile'), up)]
    ppermute x23, starting transfers between devices: 16 us -> 20.5 us  [swapped(): return lax.ppermute(value, axis, [(i, i ^ mask) for i in range(count)])]
    pallas_call x1, Pallas kernels: 4.78 us -> 1.84 us  [project(): pl.pallas_call(functools.partial(project_kernel, pieces), out_shape=(plac...]
    ppermute x23, waiting for transfers between devices: 58.5 us -> 61.3 us  [swapped(): return lax.ppermute(value, axis, [(i, i ^ mask) for i in range(count)])]
where the time goes in v4:
time: 146 us
  waiting for transfers between devices  82.6 us (57%)
  starting transfers between devices  37.4 us (26%)
  Pallas kernels  23.8 us (16%)
    ppermute x23, waiting for transfers between devices, swapped(): return lax.ppermute(value, axis, [(i, i ^ mask) for i in range(count)])  61.3 us
    ppermute x23, starting transfers between devices, swapped(): return lax.ppermute(value, axis, [(i, i ^ mask) for i in range(count)])  20.5 us
    ppermute x1, waiting for transfers between devices, per_device(): before = lax.ppermute(high_edge, ('view', 'tile'), up)  12.7 us
    ppermute x4, starting transfers between devices, passed_along(): lax.ppermute(value, axis, [(source, source + steps) for source in range(i...  12.5 us
    ppermute x4, waiting for transfers between devices, passed_along(): lax.ppermute(value, axis, [(source, source + steps) for source in range(i...  6.49 us
    pallas_call x5, Pallas kernels, place(): pl.pallas_call(functools.partial(place_kernel, kinds, groups), out_shape=...  5.59 us
    pallas_call x1, Pallas kernels, patches(): pl.pallas_call(patch_kernel, out_shape=(VMEM((views, 3, width, rows), F32...  5.57 us
    pallas_call x2, Pallas kernels, deal(): pl.pallas_call(functools.partial(deal_kernel, groups, offsets), out_shape...  4.07 us
  transfers between devices with their start and end apart: 29, of which 15 were waited for; matrix products, arithmetic and copies ran while one was open for 1% of the time, Pallas kernels for 5%

profile of v4, /device:TPU:0, one launch (start us, length us, event | category | flops | bytes accessed | tf_op | source)
XLA Modules:
  0.0 146.2 jit_solution(2068435169797313508)
XLA Ops:
  0.6 1.7 %deal.2 = (bf16[2,128,2048]{2,1,0:T(8,128)(2,1)S(1)}, bf16[2,128,2048]{2,1,0:T(8,128)(2,1)S(1)}) custom-call(bf16[2,128,8192]{2,1,0:T(8,128)(2,1)} %weights_ref.3), custom_call_target="tpu_custom_call" | custom-call | tf_op jit(solution)/shard_map/deal/pallas_call | solution.py:89
  2.4 0.0 copy-start.1
  2.4 0.0 copy-start.5
  2.4 0.0 copy-start.6
  2.4 0.0 copy-start.7
  2.4 0.0 copy-start.8
  2.5 2.3 %deal.3 = (bf16[2,128,2048]{2,1,0:T(8,128)(2,1)S(1)}, bf16[2,128,2048]{2,1,0:T(8,128)(2,1)S(1)}) custom-call(bf16[2,128,8192]{2,1,0:T(8,128)(2,1)} %weights_ref.3), custom_call_target="tpu_custom_call" | custom-call | tf_op jit(solution)/shard_map/deal/pallas_call | solution.py:89
  4.8 0.5 copy-done
  5.3 1.8 %project.1 = (bf16[4,2,2,64,128]{4,3,2,1,0:T(8,128)(2,1)S(1)}, bf16[4,2,2,64,128]{4,3,2,1,0:T(8,128)(2,1)S(1)}, f32[2,16,128,128]{3,2,1,0:T(8,128)S(1)}) custom-call(s32[2]{0:T(128)} %bitcast.16, f32[2,64,128,128]{3,2,1,0:T(8,128)S(1)} %copy-done, bf16[2,128,2048]{2,1,0:T(8,128)(2,1)S(1)} %get-tuple-element.26.refs_0_, ...), custom_call_target="tpu_custom_call" | custom-call | tf_op jit(solution)/shard_map/project/pallas_call | solution.py:170
  7.1 0.0 copy-start.2
  7.1 0.6 collective-permute-start.2
  7.7 1.3 collective-permute-start
  9.0 1.3 collective-permute-start.1
  10.3 0.1 fold.1
  10.4 0.5 collective-permute-done.one_ref
  10.9 6.0 %collective-permute-done.1.two_ref = bf16[2,2,64,128]{3,2,1,0:T(8,128)(2,1)S(1)} collective-permute-done((bf16[2,2,64,128]{3,2,1,0:T(8,128)(2,1)S(1)}, bf16[2,2,64,128]{3,2,1,0:T(8,128)(2,1)S(1)}, u32[]{:S(2)}, u32[]{:S(2)}) %collective-permute-start.1) | collective-permute-done | bytes 65568 | tf_op jit(solution)/shard_map/ppermute | solution.py:26
  16.9 5.6 %patches.1 = (f32[2,3,64,128]{3,2,1,0:T(8,128)S(1)}, bf16[2,3,64,128]{3,2,1,0:T(8,128)(2,1)S(1)}, bf16[2,3,64,128]{3,2,1,0:T(8,128)(2,1)S(1)}) custom-call(s32[2,32]{1,0:T(2,128)S(1)} %copy-done.5, s32[2]{0:T(128)S(1)} %bitcast.18, f32[2,2,64,128]{3,2,1,0:T(8,128)S(1)} %copy-done.1, bf16[2,2,64,128]{3,2,1,0:T(8,128)(2,1)S(1)} %collective-permute-done.one_ref, ...), custom_call_target="tpu_custom_call" | custom-call | flops 2147483648 | bytes 4194304 | tf_op jit(solution)/shard_map/patches/pallas_call | solution.py:334
  22.5 1.8 %collective-permute-start.3 = (bf16[2,3,64,128]{3,2,1,0:T(8,128)(2,1)S(1)}, bf16[2,3,64,128]{3,2,1,0:T(8,128)(2,1)S(1)}, u32[]{:S(2)}, u32[]{:S(2)}) collective-permute-start(bf16[2,3,64,128]{3,2,1,0:T(8,128)(2,1)S(1)} %get-tuple-element.34), channel_id=1, source_target_pairs={{0,1},{1,2},{2,3},{3,4},{4,5},{5,6},{6,7},{8,9},{9,10},{10,11},{11... | collective-permute-start | bytes 294920 | tf_op jit(solution)/shard_map/ppermute | solution.py:26
  24.3 8.1 %collective-permute-start.4 = (bf16[2,3,64,128]{3,2,1,0:T(8,128)(2,1)S(1)}, bf16[2,3,64,128]{3,2,1,0:T(8,128)(2,1)S(1)}, u32[]{:S(2)}, u32[]{:S(2)}) collective-permute-start(bf16[2,3,64,128]{3,2,1,0:T(8,128)(2,1)S(1)} %get-tuple-element.35), channel_id=1, source_target_pairs={{0,2},{1,3},{2,4},{3,5},{4,6},{5,7},{8,10},{9,11},{10,12},{11,13},... | collective-permute-start | bytes 294920 | tf_op jit(solution)/shard_map/ppermute | solution.py:26
  32.5 0.1 collective-permute-start.10
  32.5 1.3 collective-permute-start.8
  33.9 2.1 %collective-permute-start.9 = (bf16[2,128,2048]{2,1,0:T(8,128)(2,1)S(1)}, bf16[2,128,2048]{2,1,0:T(8,128)(2,1)S(1)}, u32[]{:S(2)}, u32[]{:S(2)}) collective-permute-start(bf16[2,128,2048]{2,1,0:T(8,128)(2,1)S(1)} %get-tuple-element.28.refs_2_), channel_id=1, source_target_pairs={{0,16},{8,24},{16,0},{24,8},{1,17},{9,25},{17,1},{25,9},{2,18},{10... | collective-permute-start | bytes 3145736 | tf_op jit(solution)/shard_map/ppermute | solution.py:43
  36.0 1.1 collective-permute-start.5
  37.2 5.4 %collective-permute-done.7 = bf16[2,2,64,128]{3,2,1,0:T(8,128)(2,1)S(1)} collective-permute-done((bf16[2,2,64,128]{3,2,1,0:T(8,128)(2,1)S(1)}, bf16[2,2,64,128]{3,2,1,0:T(8,128)(2,1)S(1)}, u32[]{:S(2)}, u32[]{:S(2)}) %collective-permute-start.7) | collective-permute-done | bytes 65568 | tf_op jit(solution)/shard_map/ppermute | solution.py:43
  42.6 5.2 %collective-permute-done.6 = bf16[2,2,64,128]{3,2,1,0:T(8,128)(2,1)S(1)} collective-permute-done((bf16[2,2,64,128]{3,2,1,0:T(8,128)(2,1)S(1)}, bf16[2,2,64,128]{3,2,1,0:T(8,128)(2,1)S(1)}, u32[]{:S(2)}, u32[]{:S(2)}) %collective-permute-start.6) | collective-permute-done | bytes 65568 | tf_op jit(solution)/shard_map/ppermute | solution.py:43
  47.9 0.1 add_convert_fusion
  48.0 0.0 copy-start.10
  48.0 0.1 collective-permute-start.11
  48.1 0.1 collective-permute-start.12
  48.1 4.2 %collective-permute-done.11 = bf16[2,2,64,128]{3,2,1,0:T(8,128)(2,1)S(1)} collective-permute-done((bf16[2,2,64,128]{3,2,1,0:T(8,128)(2,1)S(1)}, bf16[2,2,64,128]{3,2,1,0:T(8,128)(2,1)S(1)}, u32[]{:S(2)}, u32[]{:S(2)}) %collective-permute-start.11) | collective-permute-done | bytes 65568 | tf_op jit(solution)/shard_map/ppermute | solution.py:43
  52.3 0.1 collective-permute-start.13
  52.4 0.9 collective-permute-done.12
  53.3 5.1 %collective-permute-done.13 = bf16[2,2,64,128]{3,2,1,0:T(8,128)(2,1)S(1)} collective-permute-done((bf16[2,2,64,128]{3,2,1,0:T(8,128)(2,1)S(1)}, bf16[2,2,64,128]{3,2,1,0:T(8,128)(2,1)S(1)}, u32[]{:S(2)}, u32[]{:S(2)}) %collective-permute-start.13) | collective-permute-done | bytes 65568 | tf_op jit(solution)/shard_map/ppermute | solution.py:43
  58.4 0.1 collective-permute-start.14
  58.5 1.5 %collective-permute-done.14.refs_4_ = bf16[4,2,2,64,128]{4,3,2,1,0:T(8,128)(2,1)S(1)} collective-permute-done((bf16[4,2,2,64,128]{4,3,2,1,0:T(8,128)(2,1)S(1)}, bf16[4,2,2,64,128]{4,3,2,1,0:T(8,128)(2,1)S(1)}, u32[]{:S(2)}, u32[]{:S(2)}) %collective-permute-start.14) | collective-permute-done | bytes 262176 | tf_op jit(solution)/shard_map/ppermute | solution.py:43
  60.0 0.7 cut.1.refs_4_
  60.7 0.1 collective-permute-start.15
  60.8 0.1 collective-permute-start.16
  60.9 20.9 %collective-permute-done.15.refs_5_ = bf16[2,2,128,128]{3,2,1,0:T(8,128)(2,1)S(1)} collective-permute-done((bf16[2,2,128,128]{3,2,1,0:T(8,128)(2,1)S(1)}, bf16[2,2,128,128]{3,2,1,0:T(8,128)(2,1)S(1)}, u32[]{:S(2)}, u32[]{:S(2)}) %collective-permute-start.15) | collective-permute-done | bytes 131104 | tf_op jit(solution)/shard_map/ppermute | solution.py:43
  81.7 1.4 collective-permute-start.17
  83.1 0.4 collective-permute-done.16.refs_6_
  83.5 4.1 %collective-permute-done.17.refs_7_ = bf16[2,2,128,128]{3,2,1,0:T(8,128)(2,1)S(1)} collective-permute-done((bf16[2,2,128,128]{3,2,1,0:T(8,128)(2,1)S(1)}, bf16[2,2,128,128]{3,2,1,0:T(8,128)(2,1)S(1)}, u32[]{:S(2)}, u32[]{:S(2)}) %collective-permute-start.17) | collective-permute-done | bytes 131104 | tf_op jit(solution)/shard_map/ppermute | solution.py:43
  87.6 2.6 %half_step.1 = (f32[2,16,128,128]{3,2,1,0:T(8,128)S(1)}, bf16[2,1,128,128]{3,2,1,0:T(8,128)(2,1)S(1)}, bf16[2,1,128,128]{3,2,1,0:T(8,128)(2,1)S(1)}, bf16[2,6,12...) custom-call(bf16[2,128,2048]{2,1,0:T(8,128)(2,1)S(1)} %get-tuple-element.26.refs_0_, ...), custom_call_target="tpu_custom_call" | custom-call | tf_op jit(solution)/shard_map/half_step/pallas_call | solution.py:476
  90.2 1.7 %second_part.1 = (bf16[2,8,128,128]{3,2,1,0:T(8,128)(2,1)S(1)}, f32[2,8,128,128]{3,2,1,0:T(8,128)S(1)}) custom-call(f32[2,16,128,128]{3,2,1,0:T(8,128)S(1)} %get-tuple-element.40.half_ref), custom_call_target="tpu_custom_call" | custom-call | tf_op jit(solution)/shard_map/second_part/pallas_call | solution.py:500
  91.9 2.4 %collective-permute-start.22 = (bf16[2,8,128,128]{3,2,1,0:T(8,128)(2,1)S(1)}, bf16[2,8,128,128]{3,2,1,0:T(8,128)(2,1)S(1)}, u32[]{:S(2)}, u32[]{:S(2)}) collective-permute-start(bf16[2,8,128,128]{3,2,1,0:T(8,128)(2,1)S(1)} %get-tuple-element.46), channel_id=1, source_target_pairs={{0,16},{8,24},{16,0},{24,8},{1,17},{9,25},{17,1},{25,9},{2,18},{10... | collective-permute-start | bytes 1572872 | tf_op jit(solution)/shard_map/ppermute | solution.py:43
  94.4 0.8 collective-permute-start.28
  95.2 1.3 collective-permute-start.27
  96.5 10.7 %collective-permute-done.22.refs_1_ = bf16[2,8,128,128]{3,2,1,0:T(8,128)(2,1)S(1)} collective-permute-done((bf16[2,8,128,128]{3,2,1,0:T(8,128)(2,1)S(1)}, bf16[2,8,128,128]{3,2,1,0:T(8,128)(2,1)S(1)}, u32[]{:S(2)}, u32[]{:S(2)}) %collective-permute-start.22) | collective-permute-done | bytes 524320 | tf_op jit(solution)/shard_map/ppermute | solution.py:43
  107.2 0.8 collective-permute-start.23
  108.0 3.1 %collective-permute-start.18 = (bf16[2,1,128,128]{3,2,1,0:T(8,128)(2,1)S(1)}, bf16[2,1,128,128]{3,2,1,0:T(8,128)(2,1)S(1)}, u32[]{:S(2)}, u32[]{:S(2)}) collective-permute-start(bf16[2,1,128,128]{3,2,1,0:T(8,128)(2,1)S(1)} %get-tuple-element.41), channel_id=1, source_target_pairs={{0,8},{8,24},{24,16},{16,17},{17,25},{25,9},{9,1},{1,2},{2,10},{10... | collective-permute-start | bytes 196616 | tf_op jit(solution)/shard_map/ppermute | solution.py:675
  111.1 12.7 %collective-permute-done.18.before_ref = bf16[2,1,128,128]{3,2,1,0:T(8,128)(2,1)S(1)} collective-permute-done((bf16[2,1,128,128]{3,2,1,0:T(8,128)(2,1)S(1)}, bf16[2,1,128,128]{3,2,1,0:T(8,128)(2,1)S(1)}, u32[]{:S(2)}, u32[]{:S(2)}) %collective-permute-start.18) | collective-permute-done | bytes 65568 | tf_op jit(solution)/shard_map/ppermute | solution.py:675
  123.8 1.3 collective-permute-start.19
  125.1 3.3 %collective-permute-start.25 = (bf16[2,6,128,128]{3,2,1,0:T(8,128)(2,1)S(1)}, bf16[2,6,128,128]{3,2,1,0:T(8,128)(2,1)S(1)}, u32[]{:S(2)}, u32[]{:S(2)}) collective-permute-start(bf16[2,6,128,128]{3,2,1,0:T(8,128)(2,1)S(1)} %collective-permute-done.24.refs_0_), channel_id=1, source_target_pairs={{0,16},{8,24},{16,0},{24,8},{1,17},{9,25},{17,1},{25,9},{2,18},{10... | collective-permute-start | bytes 1179656 | tf_op jit(solution)/shard_map/ppermute | solution.py:43
  128.4 2.1 %collective-permute-done.19.after_ref = bf16[2,1,128,128]{3,2,1,0:T(8,128)(2,1)S(1)} collective-permute-done((bf16[2,1,128,128]{3,2,1,0:T(8,128)(2,1)S(1)}, bf16[2,1,128,128]{3,2,1,0:T(8,128)(2,1)S(1)}, u32[]{:S(2)}, u32[]{:S(2)}) %collective-permute-start.19) | collective-permute-done | bytes 65568 | tf_op jit(solution)/shard_map/ppermute | solution.py:676
  130.5 1.6 %third_part.1 = (bf16[2,2,128,128]{3,2,1,0:T(8,128)(2,1)S(1)}, f32[2,64,128,128]{3,2,1,0:T(8,128)}) custom-call(f32[2,16,128,128]{3,2,1,0:T(8,128)S(1)} %get-tuple-element.40.half_ref, bf16[2,1,128,128]{3,2,1,0:T(8,128)(2,1)S(1)} %collective-permute-done.18.before_ref, bf16[2,1,128,128]{3,2,1,0:T(8,128)(2,1)S(1)} %collective-permute-done.19.after_ref, ...), custom_call_target="tpu_custom_call" | custom-call | tf_op jit(solution)/shard_map/third_part/pallas_call | solution.py:546
  132.1 2.8 %collective-permute-start.20 = (bf16[2,2,128,128]{3,2,1,0:T(8,128)(2,1)S(1)}, bf16[2,2,128,128]{3,2,1,0:T(8,128)(2,1)S(1)}, u32[]{:S(2)}, u32[]{:S(2)}) collective-permute-start(bf16[2,2,128,128]{3,2,1,0:T(8,128)(2,1)S(1)} %get-tuple-element.45), channel_id=1, source_target_pairs={{0,8},{8,0},{16,24},{24,16},{1,9},{9,1},{17,25},{25,17},{2,10},{10... | collective-permute-start | bytes 393224 | tf_op jit(solution)/shard_map/ppermute | solution.py:43
  134.9 2.9 %collective-permute-done.20.refs_0_ = bf16[2,2,128,128]{3,2,1,0:T(8,128)(2,1)S(1)} collective-permute-done((bf16[2,2,128,128]{3,2,1,0:T(8,128)(2,1)S(1)}, bf16[2,2,128,128]{3,2,1,0:T(8,128)(2,1)S(1)}, u32[]{:S(2)}, u32[]{:S(2)}) %collective-permute-start.20) | collective-permute-done | bytes 131104 | tf_op jit(solution)/shard_map/ppermute | solution.py:43
  137.8 2.0 %collective-permute-start.21 = (bf16[2,2,128,128]{3,2,1,0:T(8,128)(2,1)S(1)}, bf16[2,2,128,128]{3,2,1,0:T(8,128)(2,1)S(1)}, u32[]{:S(2)}, u32[]{:S(2)}) collective-permute-start(bf16[2,2,128,128]{3,2,1,0:T(8,128)(2,1)S(1)} %collective-permute-done.20.refs_0_), channel_id=1, source_target_pairs={{0,16},{8,24},{16,0},{24,8},{1,17},{9,25},{17,1},{25,9},{2,18},{10... | collective-permute-start | bytes 393224 | tf_op jit(solution)/shard_map/ppermute | solution.py:43
  139.9 0.7 add_subtract_fusion
  140.5 1.2 place.5.refs_2_
  141.8 1.4 place.6.refs_2_
  143.2 0.9 place.7.refs_1_
  144.1 0.9 place.8.refs_2_
  145.1 1.1 place.9
  (36 shorter events, 0.2 us)
Async XLA Ops:
  0.6 4.7 %copy-start = (f32[2,64,128,128]{3,2,1,0:T(8,128)S(1)}, f32[2,64,128,128]{3,2,1,0:T(8,128)}, u32[]{:S(2)}) copy-start(f32[2,64,128,128]{3,2,1,0:T(8,128)} %volume_ref.1) | copy-start | bytes 25165828
  2.4 5.3 %copy-start.1 = (f32[2,2,64,128]{3,2,1,0:T(8,128)S(1)}, f32[2,2,64,128]{3,2,1,0:T(8,128)}, u32[]{:S(2)}) copy-start(f32[2,2,64,128]{3,2,1,0:T(8,128)} %own_ref.1) | copy-start | bytes 393220
  2.4 14.5 %copy-start.3 = (s32[2,32,128,128]{3,2,1,0:T(8,128)S(1)}, s32[2,32,128,128]{3,2,1,0:T(8,128)}, u32[]{:S(2)}) copy-start(s32[2,32,128,128]{3,2,1,0:T(8,128)} %counts_ref.1) | copy-start | bytes 12582916
  2.4 14.5 %copy-start.4 = (f32[2,128,128]{2,1,0:T(8,128)S(1)}, f32[2,128,128]{2,1,0:T(8,128)}, u32[]{:S(2)}) copy-start(f32[2,128,128]{2,1,0:T(8,128)} %probe_ref.1) | copy-start | bytes 393220
  2.4 14.5 %copy-start.5 = (s32[2,32]{1,0:T(2,128)S(1)}, s32[2,32]{1,0:T(2,128)}, u32[]{:S(2)}) copy-start(s32[2,32]{1,0:T(2,128)} %positions.1) | copy-start | bytes 772
  2.4 14.5 %copy-start.6 = (s32[2,1]{0,1:T(1,128)S(1)}, s32[2,1]{0,1:T(1,128)}, u32[]{:S(2)}) copy-start(s32[2,1]{0,1:T(1,128)} %param.15) | copy-start | bytes 28
  2.4 14.5 %copy-start.7 = (bf16[256,256]{1,0:T(8,128)(2,1)S(1)}, bf16[256,256]{1,0:T(8,128)(2,1)}, u32[]{:S(2)}) copy-start(bf16[256,256]{1,0:T(8,128)(2,1)} %constant.17.forward_ref) | copy-start | bytes 393220
  2.4 14.5 %copy-start.8 = (bf16[256,256]{1,0:T(8,128)(2,1)S(1)}, bf16[256,256]{1,0:T(8,128)(2,1)}, u32[]{:S(2)}) copy-start(bf16[256,256]{1,0:T(8,128)(2,1)} %constant.18.inverse_ref) | copy-start | bytes 393220
  5.3 42.6 %copy-start.9 = (f32[2,2,64,128]{3,2,1,0:T(8,128)S(1)}, f32[2,2,64,128]{3,2,1,0:T(8,128)}, u32[]{:S(2)}) copy-start(f32[2,2,64,128]{3,2,1,0:T(8,128)} %param.12) | copy-start | bytes 393220
  7.1 52.9 %copy-start.2 = (s32[2,1]{0,1:T(1,128)S(1)}, s32[2,1]{0,1:T(1,128)}, u32[]{:S(2)}) copy-start(s32[2,1]{0,1:T(1,128)} %param.17) | copy-start | bytes 28
  7.1 3.2 %collective-permute-start.2 = (bf16[4,2,2,64,128]{4,3,2,1,0:T(8,128)(2,1)S(1)}, bf16[4,2,2,64,128]{4,3,2,1,0:T(8,128)(2,1)S(1)}, u32[]{:S(2)}, u32[]{:S(2)}) collective-permute-start(bf16[4,2,2,64,128]{4,3,2,1,0:T(8,128)(2,1)S(1)} %get-tuple-element.31), channel_id=1, source_target_pairs={{0,1},{1,0},{2,3},{3,2},{4,5},{5,4},{6,7},{7,6},{8,9},{9,8},{10,11... | collective-permute-start | bytes 786440 | tf_op jit(solution)/shard_map/ppermute | solution.py:43
  7.7 3.1 %collective-permute-start = (bf16[2,2,64,128]{3,2,1,0:T(8,128)(2,1)S(1)}, bf16[2,2,64,128]{3,2,1,0:T(8,128)(2,1)S(1)}, u32[]{:S(2)}, u32[]{:S(2)}) collective-permute-start(bf16[2,2,64,128]{3,2,1,0:T(8,128)(2,1)S(1)} %convert_element_type.27), channel_id=1, source_target_pairs={{1,0},{2,1},{3,2},{4,3},{5,4},{6,5},{7,6},{9,8},{10,9},{11,10},{12... | collective-permute-start | bytes 196616 | tf_op jit(solution)/shard_map/ppermute | solution.py:26
  9.0 7.9 %collective-permute-start.1 = (bf16[2,2,64,128]{3,2,1,0:T(8,128)(2,1)S(1)}, bf16[2,2,64,128]{3,2,1,0:T(8,128)(2,1)S(1)}, u32[]{:S(2)}, u32[]{:S(2)}) collective-permute-start(bf16[2,2,64,128]{3,2,1,0:T(8,128)(2,1)S(1)} %convert_element_type.27), channel_id=1, source_target_pairs={{2,0},{3,1},{4,2},{5,3},{6,4},{7,5},{10,8},{11,9},{12,10},{13,11},... | collective-permute-start | bytes 196616 | tf_op jit(solution)/shard_map/ppermute | solution.py:26
  22.5 13.5 %collective-permute-start.3 = (bf16[2,3,64,128]{3,2,1,0:T(8,128)(2,1)S(1)}, bf16[2,3,64,128]{3,2,1,0:T(8,128)(2,1)S(1)}, u32[]{:S(2)}, u32[]{:S(2)}) collective-permute-start(bf16[2,3,64,128]{3,2,1,0:T(8,128)(2,1)S(1)} %get-tuple-element.34), channel_id=1, source_target_pairs={{0,1},{1,2},{2,3},{3,4},{4,5},{5,6},{6,7},{8,9},{9,10},{10,11},{11... | collective-permute-start | bytes 294920 | tf_op jit(solution)/shard_map/ppermute | solution.py:26
  24.3 11.7 %collective-permute-start.4 = (bf16[2,3,64,128]{3,2,1,0:T(8,128)(2,1)S(1)}, bf16[2,3,64,128]{3,2,1,0:T(8,128)(2,1)S(1)}, u32[]{:S(2)}, u32[]{:S(2)}) collective-permute-start(bf16[2,3,64,128]{3,2,1,0:T(8,128)(2,1)S(1)} %get-tuple-element.35), channel_id=1, source_target_pairs={{0,2},{1,3},{2,4},{3,5},{4,6},{5,7},{8,10},{9,11},{10,12},{11,13},... | collective-permute-start | bytes 294920 | tf_op jit(solution)/shard_map/ppermute | solution.py:26
  32.5 55.1 %collective-permute-start.10 = (bf16[2,128,2048]{2,1,0:T(8,128)(2,1)S(1)}, bf16[2,128,2048]{2,1,0:T(8,128)(2,1)S(1)}, u32[]{:S(2)}, u32[]{:S(2)}) collective-permute-start(bf16[2,128,2048]{2,1,0:T(8,128)(2,1)S(1)} %get-tuple-element.29.refs_3_), channel_id=1, source_target_pairs={{0,24},{8,16},{16,8},{24,0},{1,25},{9,17},{17,9},{25,1},{2,26},{10... | collective-permute-start | bytes 3145736 | tf_op jit(solution)/shard_map/ppermute | solution.py:43
  32.5 55.1 %collective-permute-start.8 = (bf16[2,128,2048]{2,1,0:T(8,128)(2,1)S(1)}, bf16[2,128,2048]{2,1,0:T(8,128)(2,1)S(1)}, u32[]{:S(2)}, u32[]{:S(2)}) collective-permute-start(bf16[2,128,2048]{2,1,0:T(8,128)(2,1)S(1)} %get-tuple-element.27.refs_1_), channel_id=1, source_target_pairs={{0,8},{8,0},{16,24},{24,16},{1,9},{9,1},{17,25},{25,17},{2,10},{10... | collective-permute-start | bytes 3145736 | tf_op jit(solution)/shard_map/ppermute | solution.py:43
  33.9 53.7 %collective-permute-start.9 = (bf16[2,128,2048]{2,1,0:T(8,128)(2,1)S(1)}, bf16[2,128,2048]{2,1,0:T(8,128)(2,1)S(1)}, u32[]{:S(2)}, u32[]{:S(2)}) collective-permute-start(bf16[2,128,2048]{2,1,0:T(8,128)(2,1)S(1)} %get-tuple-element.28.refs_2_), channel_id=1, source_target_pairs={{0,16},{8,24},{16,0},{24,8},{1,17},{9,25},{17,1},{25,9},{2,18},{10... | collective-permute-start | bytes 3145736 | tf_op jit(solution)/shard_map/ppermute | solution.py:43
  36.0 6.6 %collective-permute-start.7 = (bf16[2,2,64,128]{3,2,1,0:T(8,128)(2,1)S(1)}, bf16[2,2,64,128]{3,2,1,0:T(8,128)(2,1)S(1)}, u32[]{:S(2)}, u32[]{:S(2)}) collective-permute-start(bf16[2,2,64,128]{3,2,1,0:T(8,128)(2,1)S(1)} %get-tuple-element.32.token_ref), channel_id=1, source_target_pairs={{0,6},{1,7},{2,4},{3,5},{4,2},{5,3},{6,0},{7,1},{8,14},{9,15},{10,... | collective-permute-start | bytes 196616 | tf_op jit(solution)/shard_map/ppermute | solution.py:43
  36.0 6.6 %collective-permute-start.5 = (bf16[2,2,64,128]{3,2,1,0:T(8,128)(2,1)S(1)}, bf16[2,2,64,128]{3,2,1,0:T(8,128)(2,1)S(1)}, u32[]{:S(2)}, u32[]{:S(2)}) collective-permute-start(bf16[2,2,64,128]{3,2,1,0:T(8,128)(2,1)S(1)} %get-tuple-element.37), channel_id=1, source_target_pairs={{0,2},{1,3},{2,0},{3,1},{4,6},{5,7},{6,4},{7,5},{8,10},{9,11},{10,... | collective-permute-start | bytes 196616 | tf_op jit(solution)/shard_map/ppermute | solution.py:43
  42.6 5.3 %collective-permute-start.6 = (bf16[2,2,64,128]{3,2,1,0:T(8,128)(2,1)S(1)}, bf16[2,2,64,128]{3,2,1,0:T(8,128)(2,1)S(1)}, u32[]{:S(2)}, u32[]{:S(2)}) collective-permute-start(bf16[2,2,64,128]{3,2,1,0:T(8,128)(2,1)S(1)} %get-tuple-element.38), channel_id=1, source_target_pairs={{0,4},{1,5},{2,6},{3,7},{4,0},{5,1},{6,2},{7,3},{8,12},{9,13},{10,... | collective-permute-start | bytes 196616 | tf_op jit(solution)/shard_map/ppermute | solution.py:43
  48.0 93.8 %copy-start.10 = (f32[2,2,64,128]{3,2,1,0:T(8,128)}, f32[2,2,64,128]{3,2,1,0:T(8,128)S(1)}, u32[]{:S(2)}) copy-start(f32[2,2,64,128]{3,2,1,0:T(8,128)S(1)} %get-tuple-element.50) | copy-start | bytes 393220
  48.0 4.3 %collective-permute-start.11 = (bf16[2,2,64,128]{3,2,1,0:T(8,128)(2,1)S(1)}, bf16[2,2,64,128]{3,2,1,0:T(8,128)(2,1)S(1)}, u32[]{:S(2)}, u32[]{:S(2)}) collective-permute-start(bf16[2,2,64,128]{3,2,1,0:T(8,128)(2,1)S(1)} %get-tuple-element.49), channel_id=1, source_target_pairs={{0,2},{1,3},{2,0},{3,1},{4,6},{5,7},{6,4},{7,5},{8,10},{9,11},{10,... | collective-permute-start | bytes 196616 | tf_op jit(solution)/shard_map/ppermute | solution.py:43
  48.1 5.2 %collective-permute-start.12 = (bf16[2,2,64,128]{3,2,1,0:T(8,128)(2,1)S(1)}, bf16[2,2,64,128]{3,2,1,0:T(8,128)(2,1)S(1)}, u32[]{:S(2)}, u32[]{:S(2)}) collective-permute-start(bf16[2,2,64,128]{3,2,1,0:T(8,128)(2,1)S(1)} %get-tuple-element.49), channel_id=1, source_target_pairs={{0,4},{1,5},{2,6},{3,7},{4,0},{5,1},{6,2},{7,3},{8,12},{9,13},{10,... | collective-permute-start | bytes 196616 | tf_op jit(solution)/shard_map/ppermute | solution.py:43
  52.3 6.1 %collective-permute-start.13 = (bf16[2,2,64,128]{3,2,1,0:T(8,128)(2,1)S(1)}, bf16[2,2,64,128]{3,2,1,0:T(8,128)(2,1)S(1)}, u32[]{:S(2)}, u32[]{:S(2)}) collective-permute-start(bf16[2,2,64,128]{3,2,1,0:T(8,128)(2,1)S(1)} %get-tuple-element.49), channel_id=1, source_target_pairs={{0,6},{1,7},{2,4},{3,5},{4,2},{5,3},{6,0},{7,1},{8,14},{9,15},{10,... | collective-permute-start | bytes 196616 | tf_op jit(solution)/shard_map/ppermute | solution.py:43
  58.4 1.6 %collective-permute-start.14 = (bf16[4,2,2,64,128]{4,3,2,1,0:T(8,128)(2,1)S(1)}, bf16[4,2,2,64,128]{4,3,2,1,0:T(8,128)(2,1)S(1)}, u32[]{:S(2)}, u32[]{:S(2)}) collective-permute-start(bf16[4,2,2,64,128]{4,3,2,1,0:T(8,128)(2,1)S(1)} %pad_maximum_fusion), channel_id=1, source_target_pairs={{0,1},{1,0},{2,3},{3,2},{4,5},{5,4},{6,7},{7,6},{8,9},{9,8},{10,11... | collective-permute-start | bytes 786440 | tf_op jit(solution)/shard_map/ppermute | solution.py:43
  60.7 21.0 %collective-permute-start.15 = (bf16[2,2,128,128]{3,2,1,0:T(8,128)(2,1)S(1)}, bf16[2,2,128,128]{3,2,1,0:T(8,128)(2,1)S(1)}, u32[]{:S(2)}, u32[]{:S(2)}) collective-permute-start(bf16[2,2,128,128]{3,2,1,0:T(8,128)(2,1)S(1)} %cut.1.refs_4_), channel_id=1, source_target_pairs={{0,8},{8,0},{16,24},{24,16},{1,9},{9,1},{17,25},{25,17},{2,10},{10... | collective-permute-start | bytes 393224 | tf_op jit(solution)/shard_map/ppermute | solution.py:43
  60.8 22.7 %collective-permute-start.16 = (bf16[2,2,128,128]{3,2,1,0:T(8,128)(2,1)S(1)}, bf16[2,2,128,128]{3,2,1,0:T(8,128)(2,1)S(1)}, u32[]{:S(2)}, u32[]{:S(2)}) collective-permute-start(bf16[2,2,128,128]{3,2,1,0:T(8,128)(2,1)S(1)} %cut.1.refs_4_), channel_id=1, source_target_pairs={{0,16},{8,24},{16,0},{24,8},{1,17},{9,25},{17,1},{25,9},{2,18},{10... | collective-permute-start | bytes 393224 | tf_op jit(solution)/shard_map/ppermute | solution.py:43
  81.7 5.9 %collective-permute-start.17 = (bf16[2,2,128,128]{3,2,1,0:T(8,128)(2,1)S(1)}, bf16[2,2,128,128]{3,2,1,0:T(8,128)(2,1)S(1)}, u32[]{:S(2)}, u32[]{:S(2)}) collective-permute-start(bf16[2,2,128,128]{3,2,1,0:T(8,128)(2,1)S(1)} %cut.1.refs_4_), channel_id=1, source_target_pairs={{0,24},{8,16},{16,8},{24,0},{1,25},{9,17},{17,9},{25,1},{2,26},{10... | collective-permute-start | bytes 393224 | tf_op jit(solution)/shard_map/ppermute | solution.py:43
  91.9 15.2 %collective-permute-start.22 = (bf16[2,8,128,128]{3,2,1,0:T(8,128)(2,1)S(1)}, bf16[2,8,128,128]{3,2,1,0:T(8,128)(2,1)S(1)}, u32[]{:S(2)}, u32[]{:S(2)}) collective-permute-start(bf16[2,8,128,128]{3,2,1,0:T(8,128)(2,1)S(1)} %get-tuple-element.46), channel_id=1, source_target_pairs={{0,16},{8,24},{16,0},{24,8},{1,17},{9,25},{17,1},{25,9},{2,18},{10... | collective-permute-start | bytes 1572872 | tf_op jit(solution)/shard_map/ppermute | solution.py:43
  94.4 30.7 %collective-permute-start.24 = (bf16[2,6,128,128]{3,2,1,0:T(8,128)(2,1)S(1)}, bf16[2,6,128,128]{3,2,1,0:T(8,128)(2,1)S(1)}, u32[]{:S(2)}, u32[]{:S(2)}) collective-permute-start(bf16[2,6,128,128]{3,2,1,0:T(8,128)(2,1)S(1)} %get-tuple-element.47), channel_id=1, source_target_pairs={{0,8},{8,0},{16,24},{24,16},{1,9},{9,1},{17,25},{25,17},{2,10},{10... | collective-permute-start | bytes 1179656 | tf_op jit(solution)/shard_map/ppermute | solution.py:43
  94.4 43.4 %collective-permute-start.28 = (bf16[2,6,128,128]{3,2,1,0:T(8,128)(2,1)S(1)}, bf16[2,6,128,128]{3,2,1,0:T(8,128)(2,1)S(1)}, u32[]{:S(2)}, u32[]{:S(2)}) collective-permute-start(bf16[2,6,128,128]{3,2,1,0:T(8,128)(2,1)S(1)} %get-tuple-element.47), channel_id=1, source_target_pairs={{0,16},{8,24},{16,0},{24,8},{1,17},{9,25},{17,1},{25,9},{2,18},{10... | collective-permute-start | bytes 1179656 | tf_op jit(solution)/shard_map/ppermute | solution.py:43
  95.2 46.5 %collective-permute-start.27 = (bf16[2,8,128,128]{3,2,1,0:T(8,128)(2,1)S(1)}, bf16[2,8,128,128]{3,2,1,0:T(8,128)(2,1)S(1)}, u32[]{:S(2)}, u32[]{:S(2)}) collective-permute-start(bf16[2,8,128,128]{3,2,1,0:T(8,128)(2,1)S(1)} %get-tuple-element.46), channel_id=1, source_target_pairs={{0,8},{8,0},{16,24},{24,16},{1,9},{9,1},{17,25},{25,17},{2,10},{10... | collective-permute-start | bytes 1572872 | tf_op jit(solution)/shard_map/ppermute | solution.py:43
  107.2 37.9 %collective-permute-start.23 = (bf16[2,8,128,128]{3,2,1,0:T(8,128)(2,1)S(1)}, bf16[2,8,128,128]{3,2,1,0:T(8,128)(2,1)S(1)}, u32[]{:S(2)}, u32[]{:S(2)}) collective-permute-start(bf16[2,8,128,128]{3,2,1,0:T(8,128)(2,1)S(1)} %collective-permute-done.22.refs_1_), channel_id=1, source_target_pairs={{0,8},{8,0},{16,24},{24,16},{1,9},{9,1},{17,25},{25,17},{2,10},{10... | collective-permute-start | bytes 1572872 | tf_op jit(solution)/shard_map/ppermute | solution.py:43
  108.0 15.8 %collective-permute-start.18 = (bf16[2,1,128,128]{3,2,1,0:T(8,128)(2,1)S(1)}, bf16[2,1,128,128]{3,2,1,0:T(8,128)(2,1)S(1)}, u32[]{:S(2)}, u32[]{:S(2)}) collective-permute-start(bf16[2,1,128,128]{3,2,1,0:T(8,128)(2,1)S(1)} %get-tuple-element.41), channel_id=1, source_target_pairs={{0,8},{8,24},{24,16},{16,17},{17,25},{25,9},{9,1},{1,2},{2,10},{10... | collective-permute-start | bytes 196616 | tf_op jit(solution)/shard_map/ppermute | solution.py:675
  123.8 6.6 %collective-permute-start.19 = (bf16[2,1,128,128]{3,2,1,0:T(8,128)(2,1)S(1)}, bf16[2,1,128,128]{3,2,1,0:T(8,128)(2,1)S(1)}, u32[]{:S(2)}, u32[]{:S(2)}) collective-permute-start(bf16[2,1,128,128]{3,2,1,0:T(8,128)(2,1)S(1)} %get-tuple-element.42), channel_id=1, source_target_pairs={{8,0},{24,8},{16,24},{17,16},{25,17},{9,25},{1,9},{2,1},{10,2},{26... | collective-permute-start | bytes 196616 | tf_op jit(solution)/shard_map/ppermute | solution.py:676
  125.1 19.0 %collective-permute-start.25 = (bf16[2,6,128,128]{3,2,1,0:T(8,128)(2,1)S(1)}, bf16[2,6,128,128]{3,2,1,0:T(8,128)(2,1)S(1)}, u32[]{:S(2)}, u32[]{:S(2)}) collective-permute-start(bf16[2,6,128,128]{3,2,1,0:T(8,128)(2,1)S(1)} %collective-permute-done.24.refs_0_), channel_id=1, source_target_pairs={{0,16},{8,24},{16,0},{24,8},{1,17},{9,25},{17,1},{25,9},{2,18},{10... | collective-permute-start | bytes 1179656 | tf_op jit(solution)/shard_map/ppermute | solution.py:43
  132.1 5.7 %collective-permute-start.20 = (bf16[2,2,128,128]{3,2,1,0:T(8,128)(2,1)S(1)}, bf16[2,2,128,128]{3,2,1,0:T(8,128)(2,1)S(1)}, u32[]{:S(2)}, u32[]{:S(2)}) collective-permute-start(bf16[2,2,128,128]{3,2,1,0:T(8,128)(2,1)S(1)} %get-tuple-element.45), channel_id=1, source_target_pairs={{0,8},{8,0},{16,24},{24,16},{1,9},{9,1},{17,25},{25,17},{2,10},{10... | collective-permute-start | bytes 393224 | tf_op jit(solution)/shard_map/ppermute | solution.py:43
  137.8 5.4 %collective-permute-start.26 = (bf16[2,2,128,128]{3,2,1,0:T(8,128)(2,1)S(1)}, bf16[2,2,128,128]{3,2,1,0:T(8,128)(2,1)S(1)}, u32[]{:S(2)}, u32[]{:S(2)}) collective-permute-start(bf16[2,2,128,128]{3,2,1,0:T(8,128)(2,1)S(1)} %get-tuple-element.45), channel_id=1, source_target_pairs={{0,16},{8,24},{16,0},{24,8},{1,17},{9,25},{17,1},{25,9},{2,18},{10... | collective-permute-start | bytes 393224 | tf_op jit(solution)/shard_map/ppermute | solution.py:43
  137.8 7.2 %collective-permute-start.21 = (bf16[2,2,128,128]{3,2,1,0:T(8,128)(2,1)S(1)}, bf16[2,2,128,128]{3,2,1,0:T(8,128)(2,1)S(1)}, u32[]{:S(2)}, u32[]{:S(2)}) collective-permute-start(bf16[2,2,128,128]{3,2,1,0:T(8,128)(2,1)S(1)} %collective-permute-done.20.refs_0_), channel_id=1, source_target_pairs={{0,16},{8,24},{16,0},{24,8},{1,17},{9,25},{17,1},{25,9},{2,18},{10... | collective-permute-start | bytes 393224 | tf_op jit(solution)/shard_map/ppermute | solution.py:43

commit v5 on v4

--- a/solution.py
+++ b/solution.py
@@ -36,6 +36,11 @@
 
 def limit(mebibytes):
     return pltpu.CompilerParams(vmem_limit_bytes=mebibytes << 20)
+
+
+def window_order(groups):
+    masks = masks_of(groups)
+    return masks[-1:] + [j for j in range(1, groups) if j not in masks] + masks[:-1]
 
 
 def swapped(value, axis, mask):
@@ -181,18 +186,20 @@
     )(*far(footprints), volume, *near(*shares))
 
 
-def fold_kernel(keep_ref, arrived_ref, *refs):
-    for n, ref in enumerate(refs):
-        ref[...] = (keep_ref[n].astype(F32) + arrived_ref[n].astype(F32)).astype(ref.dtype)
+def fold_kernel(keep_ref, arrived_ref, near_ref, send_ref):
+    half = near_ref.shape[0]
+    near_ref[...] = keep_ref[:half].astype(F32) + arrived_ref[:half].astype(F32)
+    send_ref[...] = (keep_ref[half:].astype(F32) + arrived_ref[half:].astype(F32)).astype(BF16)
 
 
 def fold(keep, arrived):
     vmem = pl.BlockSpec(memory_space=VMEM)
+    shape = (keep.shape[0] // 2,) + keep.shape[1:]
     return pl.pallas_call(
         fold_kernel,
-        out_shape=tuple(VMEM(keep.shape[1:], BF16 if n else F32) for n in range(keep.shape[0])),
+        out_shape=(VMEM(shape, F32), VMEM(shape, BF16)),
         in_specs=[vmem] * 2,
-        out_specs=(vmem,) * keep.shape[0],
+        out_specs=(vmem,) * 2,
         compiler_params=limit(8),
         name="fold",
     )(*near(keep, arrived))
@@ -434,10 +441,10 @@
         run_of_columns(half_ref, k, first, part_ref.shape[1], store)
 
 
-def gradient_kernel(groups, pieces, *refs):
+def gradient_kernel(groups, pieces, final, *refs):
     weight_refs = refs[:groups]
     window_refs = refs[groups : 2 * groups]
-    volume_ref, half_ref, low_ref, high_ref, part_ref, fresh_ref = refs[2 * groups :]
+    volume_ref, half_ref = refs[2 * groups : 2 * groups + 2]
     _, share, depth, rows = half_ref.shape
     views, cols, _ = weight_refs[0].shape
     chunk = share // pieces
@@ -462,28 +469,27 @@
             plane = gradient[:, k * rows : (k + 1) * rows].reshape(chunk, depth, rows)
             held = slice(i * chunk, (i + 1) * chunk)
             half_ref[k, held] = volume_ref[k, held] - step_size * plane
-    low_ref[...] = half_ref[:, :1].astype(BF16)
-    high_ref[...] = half_ref[:, share - 1 :].astype(BF16)
-    inner_columns(half_ref, part_ref, fresh_ref, inner_runs(share)[0][0])
-
-
-def half_step_of(weights, windows, volume):
+    if final:
+        low_ref, high_ref, part_ref, fresh_ref = refs[2 * groups + 2 :]
+        low_ref[...] = half_ref[:, :1].astype(BF16)
+        high_ref[...] = half_ref[:, share - 1 :].astype(BF16)
+        inner_columns(half_ref, part_ref, fresh_ref, inner_runs(share)[0][0])
+
+
+def half_step_of(weights, windows, volume, final):
     groups = len(windows)
     _, share, depth, rows = volume.shape
     vmem = pl.BlockSpec(memory_space=VMEM)
     edge = VMEM((2, 1, depth, rows), BF16)
     inner = (2, inner_runs(share)[0][1], depth, rows)
-    return pl.pallas_call(
-        functools.partial(gradient_kernel, groups, min(4, share)),
-        out_shape=(
-            VMEM((2, share, depth, rows), F32),
-            edge,
-            edge,
-            VMEM(inner, BF16),
-            VMEM(inner, F32),
-        ),
+    outs = (VMEM((2, share, depth, rows), F32),)
+    if final:
+        outs += (edge, edge, VMEM(inner, BF16), VMEM(inner, F32))
+    return pl.pallas_call(
+        functools.partial(gradient_kernel, groups, min(4, share), final),
+        out_shape=outs,
         in_specs=[vmem] * (2 * groups + 1),
-        out_specs=(vmem,) * 5,
+        out_specs=(vmem,) * len(outs),
         compiler_params=limit(20),
         name="half_step",
     )(*near(*weights, *windows, volume))
@@ -627,11 +633,13 @@
     keep, send, volume_own = project(footprints, dealt, volume, tiles, tile_cols)
     ahead_one = passed_along(object_low, "tile", -1)
     ahead_two = passed_along(object_low, "tile", -2)
-    arrived = swapped(send, "tile", 1)
-    projection, *rest = fold(keep, arrived)
-    token = rest[-1]
-    for n, block in enumerate(rest):
-        projection = projection + swapped(block, "tile", 2 * (n + 1)).astype(F32)
+    token = None
+    for mask in [1] + masks_of(tiles)[:0:-1]:
+        arrived = swapped(send, "tile", mask)
+        if keep.shape[0] > 1:
+            keep, send = fold(keep, arrived)
+            token = send if token is None else token
+    projection = keep[0] + arrived[0].astype(F32)
 
     own_update, spill_one, spill_two = patches(
         positions,
@@ -662,11 +670,14 @@
     others = swapped(jnp.stack(pieces), "tile", 1)
     windows = cut(footprints, [piece[None] for piece in pieces] + [others], foot_cols, tiles)
     all_windows = [windows]
-    for j in range(1, groups):
+    for j in window_order(groups):
         all_windows.append(swapped(windows, "view", j))
-
+    weight_pieces = [weight_pieces[j] for j in [0] + window_order(groups)]
+
+    middle = groups // 2
+    (half,) = half_step_of(weight_pieces[:middle], all_windows[:middle], volume_own, False)
     half, low_edge, high_edge, part_a, fresh_a = half_step_of(
-        weight_pieces, all_windows, volume_own
+        weight_pieces[middle:], all_windows[middle:], half, True
     )
     order = []
     for t in range(tiles):

time: 146 us -> 147 us (level)
  the two profiles are of different devices: /device:TPU:0 before, /device:TPU:1 now
where the time goes in v5:
time: 147 us; the launch traced here: 145 us
  waiting for transfers between devices  77 us (52%)
  starting transfers between devices  41.2 us (28%)
  Pallas kernels  24 us (16%)
    ppermute x22, waiting for transfers between devices, swapped(): return lax.ppermute(value, axis, [(i, i ^ mask) for i in range(count)])  59.3 us
    ppermute x22, starting transfers between devices, swapped(): return lax.ppermute(value, axis, [(i, i ^ mask) for i in range(count)])  17.6 us
    ppermute x4, starting transfers between devices, passed_along(): lax.ppermute(value, axis, [(source, source + steps) for source in range(i...  13.5 us
    ppermute x1, waiting for transfers between devices, per_device(): before = lax.ppermute(high_edge, ('view', 'tile'), up)  12.4 us
    ppermute x1, starting transfers between devices, per_device(): before = lax.ppermute(high_edge, ('view', 'tile'), up)  8.26 us
    pallas_call x5, Pallas kernels, place(): pl.pallas_call(functools.partial(place_kernel, kinds, groups), out_shape=...  5.58 us
    pallas_call x1, Pallas kernels, patches(): pl.pallas_call(patch_kernel, out_shape=(VMEM((views, 3, width, rows), F32...  5.53 us
    ppermute x4, waiting for transfers between devices, passed_along(): lax.ppermute(value, axis, [(source, source + steps) for source in range(i...  5.29 us
  transfers between devices with their start and end apart: 28, of which 15 were waited for; matrix products, arithmetic and copies ran while one was open for 1% of the time, Pallas kernels for 5%

profile of v5, /device:TPU:1, one launch (start us, length us, event | category | flops | bytes accessed | tf_op | source)
XLA Modules:
  0.0 144.6 jit_solution(14306562848164154636)
XLA Ops:
  0.6 1.7 %deal.2 = (bf16[2,128,2048]{2,1,0:T(8,128)(2,1)S(1)}, bf16[2,128,2048]{2,1,0:T(8,128)(2,1)S(1)}) custom-call(bf16[2,128,8192]{2,1,0:T(8,128)(2,1)} %weights_ref.3), custom_call_target="tpu_custom_call" | custom-call | tf_op jit(solution)/shard_map/deal/pallas_call | solution.py:94
  2.4 0.0 copy-start.3
  2.4 0.0 copy-start.4
  2.4 0.0 copy-start.7
  2.4 0.0 copy-start.8
  2.5 2.3 %deal.3 = (bf16[2,128,2048]{2,1,0:T(8,128)(2,1)S(1)}, bf16[2,128,2048]{2,1,0:T(8,128)(2,1)S(1)}) custom-call(bf16[2,128,8192]{2,1,0:T(8,128)(2,1)} %weights_ref.3), custom_call_target="tpu_custom_call" | custom-call | tf_op jit(solution)/shard_map/deal/pallas_call | solution.py:94
  4.8 0.5 copy-done
  5.3 1.8 %project.1 = (bf16[4,2,2,64,128]{4,3,2,1,0:T(8,128)(2,1)S(1)}, bf16[4,2,2,64,128]{4,3,2,1,0:T(8,128)(2,1)S(1)}, f32[2,16,128,128]{3,2,1,0:T(8,128)S(1)}) custom-call(s32[2]{0:T(128)} %bitcast.33, f32[2,64,128,128]{3,2,1,0:T(8,128)S(1)} %copy-done, bf16[2,128,2048]{2,1,0:T(8,128)(2,1)S(1)} %get-tuple-element.26.refs_0_, ...), custom_call_target="tpu_custom_call" | custom-call | tf_op jit(solution)/shard_map/project/pallas_call | solution.py:175
  7.1 0.1 collective-permute-start.2
  7.3 2.4 %collective-permute-start = (bf16[2,2,64,128]{3,2,1,0:T(8,128)(2,1)S(1)}, bf16[2,2,64,128]{3,2,1,0:T(8,128)(2,1)S(1)}, u32[]{:S(2)}, u32[]{:S(2)}) collective-permute-start(bf16[2,2,64,128]{3,2,1,0:T(8,128)(2,1)S(1)} %convert_element_type.22), channel_id=1, source_target_pairs={{1,0},{2,1},{3,2},{4,3},{5,4},{6,5},{7,6},{9,8},{10,9},{11,10},{12... | collective-permute-start | bytes 196616 | tf_op jit(solution)/shard_map/ppermute | solution.py:26
  9.7 1.3 collective-permute-start.1
  11.0 0.1 fold.2
  11.0 2.7 %collective-permute-done.one_ref = bf16[2,2,64,128]{3,2,1,0:T(8,128)(2,1)S(1)} collective-permute-done((bf16[2,2,64,128]{3,2,1,0:T(8,128)(2,1)S(1)}, bf16[2,2,64,128]{3,2,1,0:T(8,128)(2,1)S(1)}, u32[]{:S(2)}, u32[]{:S(2)}) %collective-permute-start) | collective-permute-done | bytes 65568 | tf_op jit(solution)/shard_map/ppermute | solution.py:26
  13.8 2.5 %collective-permute-done.1.two_ref = bf16[2,2,64,128]{3,2,1,0:T(8,128)(2,1)S(1)} collective-permute-done((bf16[2,2,64,128]{3,2,1,0:T(8,128)(2,1)S(1)}, bf16[2,2,64,128]{3,2,1,0:T(8,128)(2,1)S(1)}, u32[]{:S(2)}, u32[]{:S(2)}) %collective-permute-start.1) | collective-permute-done | bytes 65568 | tf_op jit(solution)/shard_map/ppermute | solution.py:26
  16.4 5.5 %patches.1 = (f32[2,3,64,128]{3,2,1,0:T(8,128)S(1)}, bf16[2,3,64,128]{3,2,1,0:T(8,128)(2,1)S(1)}, bf16[2,3,64,128]{3,2,1,0:T(8,128)(2,1)S(1)}) custom-call(s32[2,32]{1,0:T(2,128)S(1)} %copy-done.5, s32[2]{0:T(128)S(1)} %bitcast.35, f32[2,2,64,128]{3,2,1,0:T(8,128)S(1)} %copy-done.1, bf16[2,2,64,128]{3,2,1,0:T(8,128)(2,1)S(1)} %collective-permute-done.one_ref, ...), custom_call_target="tpu_custom_call" | custom-call | flops 2147483648 | bytes 4194304 | tf_op jit(solution)/shard_map/patches/pallas_call | solution.py:341
  21.9 1.9 %collective-permute-start.3 = (bf16[2,3,64,128]{3,2,1,0:T(8,128)(2,1)S(1)}, bf16[2,3,64,128]{3,2,1,0:T(8,128)(2,1)S(1)}, u32[]{:S(2)}, u32[]{:S(2)}) collective-permute-start(bf16[2,3,64,128]{3,2,1,0:T(8,128)(2,1)S(1)} %get-tuple-element.34), channel_id=1, source_target_pairs={{0,1},{1,2},{2,3},{3,4},{4,5},{5,6},{6,7},{8,9},{9,10},{10,11},{11... | collective-permute-start | bytes 294920 | tf_op jit(solution)/shard_map/ppermute | solution.py:26
  23.8 7.9 %collective-permute-start.4 = (bf16[2,3,64,128]{3,2,1,0:T(8,128)(2,1)S(1)}, bf16[2,3,64,128]{3,2,1,0:T(8,128)(2,1)S(1)}, u32[]{:S(2)}, u32[]{:S(2)}) collective-permute-start(bf16[2,3,64,128]{3,2,1,0:T(8,128)(2,1)S(1)} %get-tuple-element.35), channel_id=1, source_target_pairs={{0,2},{1,3},{2,4},{3,5},{4,6},{5,7},{8,10},{9,11},{10,12},{11,13},... | collective-permute-start | bytes 294920 | tf_op jit(solution)/shard_map/ppermute | solution.py:26
  31.7 0.1 collective-permute-start.15
  31.8 0.1 collective-permute-start.7
  31.9 2.6 %collective-permute-start.8 = (bf16[2,128,2048]{2,1,0:T(8,128)(2,1)S(1)}, bf16[2,128,2048]{2,1,0:T(8,128)(2,1)S(1)}, u32[]{:S(2)}, u32[]{:S(2)}) collective-permute-start(bf16[2,128,2048]{2,1,0:T(8,128)(2,1)S(1)} %get-tuple-element.27.refs_1_), channel_id=1, source_target_pairs={{0,8},{8,0},{16,24},{24,16},{1,9},{9,1},{17,25},{25,17},{2,10},{10... | collective-permute-start | bytes 3145736 | tf_op jit(solution)/shard_map/ppermute | solution.py:48
  34.5 8.5 %collective-permute-done.5.arrived_ref = bf16[2,2,2,64,128]{4,3,2,1,0:T(8,128)(2,1)S(1)} collective-permute-done((bf16[2,2,2,64,128]{4,3,2,1,0:T(8,128)(2,1)S(1)}, bf16[2,2,2,64,128]{4,3,2,1,0:T(8,128)(2,1)S(1)}, u32[]{:S(2)}, u32[]{:S(2)}) %collective-permute-start.5) | collective-permute-done | bytes 131104 | tf_op jit(solution)/shard_map/ppermute | solution.py:48
  43.0 0.1 collective-permute-start.6
  43.1 3.4 %collective-permute-done.6 = bf16[1,2,2,64,128]{4,3,2,1,0:T(8,128)(2,1)S(1)} collective-permute-done((bf16[1,2,2,64,128]{4,3,2,1,0:T(8,128)(2,1)S(1)}, bf16[1,2,2,64,128]{4,3,2,1,0:T(8,128)(2,1)S(1)}, u32[]{:S(2)}, u32[]{:S(2)}) %collective-permute-start.6) | collective-permute-done | bytes 65568 | tf_op jit(solution)/shard_map/ppermute | solution.py:48
  46.5 0.1 fusion.6
  46.5 0.0 copy-start.10
  46.6 0.1 collective-permute-start.9
  46.6 0.1 collective-permute-start.10
  46.7 3.3 %collective-permute-done.9 = bf16[2,2,64,128]{3,2,1,0:T(8,128)(2,1)S(1)} collective-permute-done((bf16[2,2,64,128]{3,2,1,0:T(8,128)(2,1)S(1)}, bf16[2,2,64,128]{3,2,1,0:T(8,128)(2,1)S(1)}, u32[]{:S(2)}, u32[]{:S(2)}) %collective-permute-start.9) | collective-permute-done | bytes 65568 | tf_op jit(solution)/shard_map/ppermute | solution.py:48
  50.0 0.1 collective-permute-start.11
  50.2 0.8 collective-permute-done.10
  51.0 3.9 %collective-permute-done.11 = bf16[2,2,64,128]{3,2,1,0:T(8,128)(2,1)S(1)} collective-permute-done((bf16[2,2,64,128]{3,2,1,0:T(8,128)(2,1)S(1)}, bf16[2,2,64,128]{3,2,1,0:T(8,128)(2,1)S(1)}, u32[]{:S(2)}, u32[]{:S(2)}) %collective-permute-start.11) | collective-permute-done | bytes 65568 | tf_op jit(solution)/shard_map/ppermute | solution.py:48
  55.0 3.7 %collective-permute-start.12 = (bf16[4,2,2,64,128]{4,3,2,1,0:T(8,128)(2,1)S(1)}, bf16[4,2,2,64,128]{4,3,2,1,0:T(8,128)(2,1)S(1)}, u32[]{:S(2)}, u32[]{:S(2)}) collective-permute-start(bf16[4,2,2,64,128]{4,3,2,1,0:T(8,128)(2,1)S(1)} %pad_maximum_fusion), channel_id=1, source_target_pairs={{0,1},{1,0},{2,3},{3,2},{4,5},{5,4},{6,7},{7,6},{8,9},{9,8},{10,11... | collective-permute-start | bytes 786440 | tf_op jit(solution)/shard_map/ppermute | solution.py:48
  58.7 1.2 collective-permute-done.12.refs_4_
  59.9 0.7 cut.1.refs_2_
  60.5 0.4 collective-permute-start.16
  61.0 1.1 collective-permute-start.13
  62.1 21.9 %collective-permute-done.16.refs_3_ = bf16[2,2,128,128]{3,2,1,0:T(8,128)(2,1)S(1)} collective-permute-done((bf16[2,2,128,128]{3,2,1,0:T(8,128)(2,1)S(1)}, bf16[2,2,128,128]{3,2,1,0:T(8,128)(2,1)S(1)}, u32[]{:S(2)}, u32[]{:S(2)}) %collective-permute-start.16) | collective-permute-done | bytes 131104 | tf_op jit(solution)/shard_map/ppermute | solution.py:48
  84.0 0.8 half_step.2.refs_4_
  84.7 3.0 %collective-permute-done.14.refs_3_ = bf16[2,2,128,128]{3,2,1,0:T(8,128)(2,1)S(1)} collective-permute-done((bf16[2,2,128,128]{3,2,1,0:T(8,128)(2,1)S(1)}, bf16[2,2,128,128]{3,2,1,0:T(8,128)(2,1)S(1)}, u32[]{:S(2)}, u32[]{:S(2)}) %collective-permute-start.14) | collective-permute-done | bytes 131104 | tf_op jit(solution)/shard_map/ppermute | solution.py:48
  87.8 2.1 %half_step.3 = (f32[2,16,128,128]{3,2,1,0:T(8,128)S(1)}, bf16[2,1,128,128]{3,2,1,0:T(8,128)(2,1)S(1)}, bf16[2,1,128,128]{3,2,1,0:T(8,128)(2,1)S(1)}, bf16[2,6,12...) custom-call(bf16[2,128,2048]{2,1,0:T(8,128)(2,1)S(1)} %collective-permute-done.7.refs_0_, ...), custom_call_target="tpu_custom_call" | custom-call | tf_op jit(solution)/shard_map/half_step/pallas_call | solution.py:488
  89.8 1.7 %second_part.1 = (bf16[2,8,128,128]{3,2,1,0:T(8,128)(2,1)S(1)}, f32[2,8,128,128]{3,2,1,0:T(8,128)S(1)}) custom-call(f32[2,16,128,128]{3,2,1,0:T(8,128)S(1)} %get-tuple-element.40.half_ref), custom_call_target="tpu_custom_call" | custom-call | tf_op jit(solution)/shard_map/second_part/pallas_call | solution.py:506
  91.6 0.1 collective-permute-start.21
  91.6 0.1 collective-permute-start.23
  91.7 1.4 collective-permute-start.27
  93.1 1.5 %collective-permute-start.26 = (bf16[2,8,128,128]{3,2,1,0:T(8,128)(2,1)S(1)}, bf16[2,8,128,128]{3,2,1,0:T(8,128)(2,1)S(1)}, u32[]{:S(2)}, u32[]{:S(2)}) collective-permute-start(bf16[2,8,128,128]{3,2,1,0:T(8,128)(2,1)S(1)} %get-tuple-element.46), channel_id=1, source_target_pairs={{0,8},{8,0},{16,24},{24,16},{1,9},{9,1},{17,25},{25,17},{2,10},{10... | collective-permute-start | bytes 1572872 | tf_op jit(solution)/shard_map/ppermute | solution.py:48
  94.6 7.9 %collective-permute-done.21.refs_1_ = bf16[2,8,128,128]{3,2,1,0:T(8,128)(2,1)S(1)} collective-permute-done((bf16[2,8,128,128]{3,2,1,0:T(8,128)(2,1)S(1)}, bf16[2,8,128,128]{3,2,1,0:T(8,128)(2,1)S(1)}, u32[]{:S(2)}, u32[]{:S(2)}) %collective-permute-start.21) | collective-permute-done | bytes 524320 | tf_op jit(solution)/shard_map/ppermute | solution.py:48
  102.5 0.3 collective-permute-start.22
  102.8 8.3 %collective-permute-start.17 = (bf16[2,1,128,128]{3,2,1,0:T(8,128)(2,1)S(1)}, bf16[2,1,128,128]{3,2,1,0:T(8,128)(2,1)S(1)}, u32[]{:S(2)}, u32[]{:S(2)}) collective-permute-start(bf16[2,1,128,128]{3,2,1,0:T(8,128)(2,1)S(1)} %get-tuple-element.41), channel_id=1, source_target_pairs={{0,8},{8,24},{24,16},{16,17},{17,25},{25,9},{9,1},{1,2},{2,10},{10... | collective-permute-start | bytes 196616 | tf_op jit(solution)/shard_map/ppermute | solution.py:686
  111.0 12.4 %collective-permute-done.17.before_ref = bf16[2,1,128,128]{3,2,1,0:T(8,128)(2,1)S(1)} collective-permute-done((bf16[2,1,128,128]{3,2,1,0:T(8,128)(2,1)S(1)}, bf16[2,1,128,128]{3,2,1,0:T(8,128)(2,1)S(1)}, u32[]{:S(2)}, u32[]{:S(2)}) %collective-permute-start.17) | collective-permute-done | bytes 65568 | tf_op jit(solution)/shard_map/ppermute | solution.py:686
  123.4 1.9 %collective-permute-start.18 = (bf16[2,1,128,128]{3,2,1,0:T(8,128)(2,1)S(1)}, bf16[2,1,128,128]{3,2,1,0:T(8,128)(2,1)S(1)}, u32[]{:S(2)}, u32[]{:S(2)}) collective-permute-start(bf16[2,1,128,128]{3,2,1,0:T(8,128)(2,1)S(1)} %get-tuple-element.42), channel_id=1, source_target_pairs={{8,0},{24,8},{16,24},{17,16},{25,17},{9,25},{1,9},{2,1},{10,2},{26... | collective-permute-start | bytes 196616 | tf_op jit(solution)/shard_map/ppermute | solution.py:687
  125.3 4.4 %collective-permute-start.24 = (bf16[2,6,128,128]{3,2,1,0:T(8,128)(2,1)S(1)}, bf16[2,6,128,128]{3,2,1,0:T(8,128)(2,1)S(1)}, u32[]{:S(2)}, u32[]{:S(2)}) collective-permute-start(bf16[2,6,128,128]{3,2,1,0:T(8,128)(2,1)S(1)} %collective-permute-done.23.refs_0_), channel_id=1, source_target_pairs={{0,16},{8,24},{16,0},{24,8},{1,17},{9,25},{17,1},{25,9},{2,18},{10... | collective-permute-start | bytes 1179656 | tf_op jit(solution)/shard_map/ppermute | solution.py:48
  129.8 1.6 %third_part.1 = (bf16[2,2,128,128]{3,2,1,0:T(8,128)(2,1)S(1)}, f32[2,64,128,128]{3,2,1,0:T(8,128)}) custom-call(f32[2,16,128,128]{3,2,1,0:T(8,128)S(1)} %get-tuple-element.40.half_ref, bf16[2,1,128,128]{3,2,1,0:T(8,128)(2,1)S(1)} %collective-permute-done.17.before_ref, bf16[2,1,128,128]{3,2,1,0:T(8,128)(2,1)S(1)} %collective-permute-done.18.after_ref, ...), custom_call_target="tpu_custom_call" | custom-call | tf_op jit(solution)/shard_map/third_part/pallas_call | solution.py:552
  131.4 0.1 collective-permute-start.19
  131.5 4.1 %collective-permute-done.19.refs_0_ = bf16[2,2,128,128]{3,2,1,0:T(8,128)(2,1)S(1)} collective-permute-done((bf16[2,2,128,128]{3,2,1,0:T(8,128)(2,1)S(1)}, bf16[2,2,128,128]{3,2,1,0:T(8,128)(2,1)S(1)}, u32[]{:S(2)}, u32[]{:S(2)}) %collective-permute-start.19) | collective-permute-done | bytes 131104 | tf_op jit(solution)/shard_map/ppermute | solution.py:48
  135.6 0.8 collective-permute-start.25
  136.4 0.7 collective-permute-start.20
  137.1 0.7 fusion.4
  137.8 1.2 place.5.refs_2_
  139.0 1.4 place.6.refs_2_
  140.4 0.2 collective-permute-done.25.refs_1_
  140.6 0.9 place.7.refs_1_
  141.5 0.9 place.8.refs_2_
  142.5 1.0 collective-permute-done.20.refs_0_
  143.5 1.1 place.9
  (36 shorter events, 0.2 us)
Async XLA Ops:
  0.6 4.7 %copy-start = (f32[2,64,128,128]{3,2,1,0:T(8,128)S(1)}, f32[2,64,128,128]{3,2,1,0:T(8,128)}, u32[]{:S(2)}) copy-start(f32[2,64,128,128]{3,2,1,0:T(8,128)} %volume_ref.1) | copy-start | bytes 25165828
  2.4 4.9 %copy-start.1 = (f32[2,2,64,128]{3,2,1,0:T(8,128)S(1)}, f32[2,2,64,128]{3,2,1,0:T(8,128)}, u32[]{:S(2)}) copy-start(f32[2,2,64,128]{3,2,1,0:T(8,128)} %own_ref.1) | copy-start | bytes 393220
  2.4 13.9 %copy-start.3 = (s32[2,32,128,128]{3,2,1,0:T(8,128)S(1)}, s32[2,32,128,128]{3,2,1,0:T(8,128)}, u32[]{:S(2)}) copy-start(s32[2,32,128,128]{3,2,1,0:T(8,128)} %counts_ref.1) | copy-start | bytes 12582916
  2.4 13.9 %copy-start.4 = (f32[2,128,128]{2,1,0:T(8,128)S(1)}, f32[2,128,128]{2,1,0:T(8,128)}, u32[]{:S(2)}) copy-start(f32[2,128,128]{2,1,0:T(8,128)} %probe_ref.1) | copy-start | bytes 393220
  2.4 13.9 %copy-start.5 = (s32[2,32]{1,0:T(2,128)S(1)}, s32[2,32]{1,0:T(2,128)}, u32[]{:S(2)}) copy-start(s32[2,32]{1,0:T(2,128)} %positions.1) | copy-start | bytes 772
  2.4 13.9 %copy-start.6 = (s32[2,1]{0,1:T(1,128)S(1)}, s32[2,1]{0,1:T(1,128)}, u32[]{:S(2)}) copy-start(s32[2,1]{0,1:T(1,128)} %param.15) | copy-start | bytes 28
  2.4 13.9 %copy-start.7 = (bf16[256,256]{1,0:T(8,128)(2,1)S(1)}, bf16[256,256]{1,0:T(8,128)(2,1)}, u32[]{:S(2)}) copy-start(bf16[256,256]{1,0:T(8,128)(2,1)} %constant.17.forward_ref) | copy-start | bytes 393220
  2.4 13.9 %copy-start.8 = (bf16[256,256]{1,0:T(8,128)(2,1)S(1)}, bf16[256,256]{1,0:T(8,128)(2,1)}, u32[]{:S(2)}) copy-start(bf16[256,256]{1,0:T(8,128)(2,1)} %constant.18.inverse_ref) | copy-start | bytes 393220
  5.3 41.2 %copy-start.9 = (f32[2,2,64,128]{3,2,1,0:T(8,128)S(1)}, f32[2,2,64,128]{3,2,1,0:T(8,128)}, u32[]{:S(2)}) copy-start(f32[2,2,64,128]{3,2,1,0:T(8,128)} %param.12) | copy-start | bytes 393220
  7.1 52.7 %copy-start.2 = (s32[2,1]{0,1:T(1,128)S(1)}, s32[2,1]{0,1:T(1,128)}, u32[]{:S(2)}) copy-start(s32[2,1]{0,1:T(1,128)} %param.17) | copy-start | bytes 28
  7.1 3.8 %collective-permute-start.2 = (bf16[4,2,2,64,128]{4,3,2,1,0:T(8,128)(2,1)S(1)}, bf16[4,2,2,64,128]{4,3,2,1,0:T(8,128)(2,1)S(1)}, u32[]{:S(2)}, u32[]{:S(2)}) collective-permute-start(bf16[4,2,2,64,128]{4,3,2,1,0:T(8,128)(2,1)S(1)} %get-tuple-element.31), channel_id=1, source_target_pairs={{0,1},{1,0},{2,3},{3,2},{4,5},{5,4},{6,7},{7,6},{8,9},{9,8},{10,11... | collective-permute-start | bytes 786440 | tf_op jit(solution)/shard_map/ppermute | solution.py:48
  7.3 6.5 %collective-permute-start = (bf16[2,2,64,128]{3,2,1,0:T(8,128)(2,1)S(1)}, bf16[2,2,64,128]{3,2,1,0:T(8,128)(2,1)S(1)}, u32[]{:S(2)}, u32[]{:S(2)}) collective-permute-start(bf16[2,2,64,128]{3,2,1,0:T(8,128)(2,1)S(1)} %convert_element_type.22), channel_id=1, source_target_pairs={{1,0},{2,1},{3,2},{4,3},{5,4},{6,5},{7,6},{9,8},{10,9},{11,10},{12... | collective-permute-start | bytes 196616 | tf_op jit(solution)/shard_map/ppermute | solution.py:26
  9.7 6.7 %collective-permute-start.1 = (bf16[2,2,64,128]{3,2,1,0:T(8,128)(2,1)S(1)}, bf16[2,2,64,128]{3,2,1,0:T(8,128)(2,1)S(1)}, u32[]{:S(2)}, u32[]{:S(2)}) collective-permute-start(bf16[2,2,64,128]{3,2,1,0:T(8,128)(2,1)S(1)} %convert_element_type.22), channel_id=1, source_target_pairs={{2,0},{3,1},{4,2},{5,3},{6,4},{7,5},{10,8},{11,9},{12,10},{13,11},... | collective-permute-start | bytes 196616 | tf_op jit(solution)/shard_map/ppermute | solution.py:26
  21.9 12.5 %collective-permute-start.3 = (bf16[2,3,64,128]{3,2,1,0:T(8,128)(2,1)S(1)}, bf16[2,3,64,128]{3,2,1,0:T(8,128)(2,1)S(1)}, u32[]{:S(2)}, u32[]{:S(2)}) collective-permute-start(bf16[2,3,64,128]{3,2,1,0:T(8,128)(2,1)S(1)} %get-tuple-element.34), channel_id=1, source_target_pairs={{0,1},{1,2},{2,3},{3,4},{4,5},{5,6},{6,7},{8,9},{9,10},{10,11},{11... | collective-permute-start | bytes 294920 | tf_op jit(solution)/shard_map/ppermute | solution.py:26
  23.8 10.6 %collective-permute-start.4 = (bf16[2,3,64,128]{3,2,1,0:T(8,128)(2,1)S(1)}, bf16[2,3,64,128]{3,2,1,0:T(8,128)(2,1)S(1)}, u32[]{:S(2)}, u32[]{:S(2)}) collective-permute-start(bf16[2,3,64,128]{3,2,1,0:T(8,128)(2,1)S(1)} %get-tuple-element.35), channel_id=1, source_target_pairs={{0,2},{1,3},{2,4},{3,5},{4,6},{5,7},{8,10},{9,11},{10,12},{11,13},... | collective-permute-start | bytes 294920 | tf_op jit(solution)/shard_map/ppermute | solution.py:26
  31.7 52.3 %collective-permute-start.15 = (bf16[2,128,2048]{2,1,0:T(8,128)(2,1)S(1)}, bf16[2,128,2048]{2,1,0:T(8,128)(2,1)S(1)}, u32[]{:S(2)}, u32[]{:S(2)}) collective-permute-start(bf16[2,128,2048]{2,1,0:T(8,128)(2,1)S(1)} %get-tuple-element.28.refs_2_), channel_id=1, source_target_pairs={{0,16},{8,24},{16,0},{24,8},{1,17},{9,25},{17,1},{25,9},{2,18},{10... | collective-permute-start | bytes 3145736 | tf_op jit(solution)/shard_map/ppermute | solution.py:48
  31.8 56.0 %collective-permute-start.7 = (bf16[2,128,2048]{2,1,0:T(8,128)(2,1)S(1)}, bf16[2,128,2048]{2,1,0:T(8,128)(2,1)S(1)}, u32[]{:S(2)}, u32[]{:S(2)}) collective-permute-start(bf16[2,128,2048]{2,1,0:T(8,128)(2,1)S(1)} %get-tuple-element.29.refs_3_), channel_id=1, source_target_pairs={{0,24},{8,16},{16,8},{24,0},{1,25},{9,17},{17,9},{25,1},{2,26},{10... | collective-permute-start | bytes 3145736 | tf_op jit(solution)/shard_map/ppermute | solution.py:48
  31.9 55.9 %collective-permute-start.8 = (bf16[2,128,2048]{2,1,0:T(8,128)(2,1)S(1)}, bf16[2,128,2048]{2,1,0:T(8,128)(2,1)S(1)}, u32[]{:S(2)}, u32[]{:S(2)}) collective-permute-start(bf16[2,128,2048]{2,1,0:T(8,128)(2,1)S(1)} %get-tuple-element.27.refs_1_), channel_id=1, source_target_pairs={{0,8},{8,0},{16,24},{24,16},{1,9},{9,1},{17,25},{25,17},{2,10},{10... | collective-permute-start | bytes 3145736 | tf_op jit(solution)/shard_map/ppermute | solution.py:48
  34.4 8.6 %collective-permute-start.5 = (bf16[2,2,2,64,128]{4,3,2,1,0:T(8,128)(2,1)S(1)}, bf16[2,2,2,64,128]{4,3,2,1,0:T(8,128)(2,1)S(1)}, u32[]{:S(2)}, u32[]{:S(2)}) collective-permute-start(bf16[2,2,2,64,128]{4,3,2,1,0:T(8,128)(2,1)S(1)} %get-tuple-element.32.token_ref), channel_id=1, source_target_pairs={{0,4},{1,5},{2,6},{3,7},{4,0},{5,1},{6,2},{7,3},{8,12},{9,13},{10,... | collective-permute-start | bytes 393224 | tf_op jit(solution)/shard_map/ppermute | solution.py:48
  43.0 3.5 %collective-permute-start.6 = (bf16[1,2,2,64,128]{4,3,2,1,0:T(8,128)(2,1)S(1)}, bf16[1,2,2,64,128]{4,3,2,1,0:T(8,128)(2,1)S(1)}, u32[]{:S(2)}, u32[]{:S(2)}) collective-permute-start(bf16[1,2,2,64,128]{4,3,2,1,0:T(8,128)(2,1)S(1)} %get-tuple-element.38), channel_id=1, source_target_pairs={{0,2},{1,3},{2,0},{3,1},{4,6},{5,7},{6,4},{7,5},{8,10},{9,11},{10,... | collective-permute-start | bytes 196616 | tf_op jit(solution)/shard_map/ppermute | solution.py:48
  46.5 90.5 %copy-start.10 = (f32[2,2,64,128]{3,2,1,0:T(8,128)}, f32[2,2,64,128]{3,2,1,0:T(8,128)S(1)}, u32[]{:S(2)}) copy-start(f32[2,2,64,128]{3,2,1,0:T(8,128)S(1)} %get-tuple-element.50) | copy-start | bytes 393220
  46.6 3.5 %collective-permute-start.9 = (bf16[2,2,64,128]{3,2,1,0:T(8,128)(2,1)S(1)}, bf16[2,2,64,128]{3,2,1,0:T(8,128)(2,1)S(1)}, u32[]{:S(2)}, u32[]{:S(2)}) collective-permute-start(bf16[2,2,64,128]{3,2,1,0:T(8,128)(2,1)S(1)} %get-tuple-element.49), channel_id=1, source_target_pairs={{0,2},{1,3},{2,0},{3,1},{4,6},{5,7},{6,4},{7,5},{8,10},{9,11},{10,... | collective-permute-start | bytes 196616 | tf_op jit(solution)/shard_map/ppermute | solution.py:48
  46.6 4.4 %collective-permute-start.10 = (bf16[2,2,64,128]{3,2,1,0:T(8,128)(2,1)S(1)}, bf16[2,2,64,128]{3,2,1,0:T(8,128)(2,1)S(1)}, u32[]{:S(2)}, u32[]{:S(2)}) collective-permute-start(bf16[2,2,64,128]{3,2,1,0:T(8,128)(2,1)S(1)} %get-tuple-element.49), channel_id=1, source_target_pairs={{0,4},{1,5},{2,6},{3,7},{4,0},{5,1},{6,2},{7,3},{8,12},{9,13},{10,... | collective-permute-start | bytes 196616 | tf_op jit(solution)/shard_map/ppermute | solution.py:48
  50.0 4.9 %collective-permute-start.11 = (bf16[2,2,64,128]{3,2,1,0:T(8,128)(2,1)S(1)}, bf16[2,2,64,128]{3,2,1,0:T(8,128)(2,1)S(1)}, u32[]{:S(2)}, u32[]{:S(2)}) collective-permute-start(bf16[2,2,64,128]{3,2,1,0:T(8,128)(2,1)S(1)} %get-tuple-element.49), channel_id=1, source_target_pairs={{0,6},{1,7},{2,4},{3,5},{4,2},{5,3},{6,0},{7,1},{8,14},{9,15},{10,... | collective-permute-start | bytes 196616 | tf_op jit(solution)/shard_map/ppermute | solution.py:48
  55.0 4.9 %collective-permute-start.12 = (bf16[4,2,2,64,128]{4,3,2,1,0:T(8,128)(2,1)S(1)}, bf16[4,2,2,64,128]{4,3,2,1,0:T(8,128)(2,1)S(1)}, u32[]{:S(2)}, u32[]{:S(2)}) collective-permute-start(bf16[4,2,2,64,128]{4,3,2,1,0:T(8,128)(2,1)S(1)} %pad_maximum_fusion), channel_id=1, source_target_pairs={{0,1},{1,0},{2,3},{3,2},{4,5},{5,4},{6,7},{7,6},{8,9},{9,8},{10,11... | collective-permute-start | bytes 786440 | tf_op jit(solution)/shard_map/ppermute | solution.py:48
  60.5 23.4 %collective-permute-start.16 = (bf16[2,2,128,128]{3,2,1,0:T(8,128)(2,1)S(1)}, bf16[2,2,128,128]{3,2,1,0:T(8,128)(2,1)S(1)}, u32[]{:S(2)}, u32[]{:S(2)}) collective-permute-start(bf16[2,2,128,128]{3,2,1,0:T(8,128)(2,1)S(1)} %cut.1.refs_2_), channel_id=1, source_target_pairs={{0,16},{8,24},{16,0},{24,8},{1,17},{9,25},{17,1},{25,9},{2,18},{10... | collective-permute-start | bytes 393224 | tf_op jit(solution)/shard_map/ppermute | solution.py:48
  61.0 23.8 %collective-permute-start.13 = (bf16[2,2,128,128]{3,2,1,0:T(8,128)(2,1)S(1)}, bf16[2,2,128,128]{3,2,1,0:T(8,128)(2,1)S(1)}, u32[]{:S(2)}, u32[]{:S(2)}) collective-permute-start(bf16[2,2,128,128]{3,2,1,0:T(8,128)(2,1)S(1)} %cut.1.refs_2_), channel_id=1, source_target_pairs={{0,24},{8,16},{16,8},{24,0},{1,25},{9,17},{17,9},{25,1},{2,26},{10... | collective-permute-start | bytes 393224 | tf_op jit(solution)/shard_map/ppermute | solution.py:48
  83.9 3.8 %collective-permute-start.14 = (bf16[2,2,128,128]{3,2,1,0:T(8,128)(2,1)S(1)}, bf16[2,2,128,128]{3,2,1,0:T(8,128)(2,1)S(1)}, u32[]{:S(2)}, u32[]{:S(2)}) collective-permute-start(bf16[2,2,128,128]{3,2,1,0:T(8,128)(2,1)S(1)} %cut.1.refs_2_), channel_id=1, source_target_pairs={{0,8},{8,0},{16,24},{24,16},{1,9},{9,1},{17,25},{25,17},{2,10},{10... | collective-permute-start | bytes 393224 | tf_op jit(solution)/shard_map/ppermute | solution.py:48
  91.6 10.9 %collective-permute-start.21 = (bf16[2,8,128,128]{3,2,1,0:T(8,128)(2,1)S(1)}, bf16[2,8,128,128]{3,2,1,0:T(8,128)(2,1)S(1)}, u32[]{:S(2)}, u32[]{:S(2)}) collective-permute-start(bf16[2,8,128,128]{3,2,1,0:T(8,128)(2,1)S(1)} %get-tuple-element.46), channel_id=1, source_target_pairs={{0,16},{8,24},{16,0},{24,8},{1,17},{9,25},{17,1},{25,9},{2,18},{10... | collective-permute-start | bytes 1572872 | tf_op jit(solution)/shard_map/ppermute | solution.py:48
  91.6 33.7 %collective-permute-start.23 = (bf16[2,6,128,128]{3,2,1,0:T(8,128)(2,1)S(1)}, bf16[2,6,128,128]{3,2,1,0:T(8,128)(2,1)S(1)}, u32[]{:S(2)}, u32[]{:S(2)}) collective-permute-start(bf16[2,6,128,128]{3,2,1,0:T(8,128)(2,1)S(1)} %get-tuple-element.47), channel_id=1, source_target_pairs={{0,8},{8,0},{16,24},{24,16},{1,9},{9,1},{17,25},{25,17},{2,10},{10... | collective-permute-start | bytes 1179656 | tf_op jit(solution)/shard_map/ppermute | solution.py:48
  91.7 44.7 %collective-permute-start.27 = (bf16[2,6,128,128]{3,2,1,0:T(8,128)(2,1)S(1)}, bf16[2,6,128,128]{3,2,1,0:T(8,128)(2,1)S(1)}, u32[]{:S(2)}, u32[]{:S(2)}) collective-permute-start(bf16[2,6,128,128]{3,2,1,0:T(8,128)(2,1)S(1)} %get-tuple-element.47), channel_id=1, source_target_pairs={{0,16},{8,24},{16,0},{24,8},{1,17},{9,25},{17,1},{25,9},{2,18},{10... | collective-permute-start | bytes 1179656 | tf_op jit(solution)/shard_map/ppermute | solution.py:48
  93.1 45.9 %collective-permute-start.26 = (bf16[2,8,128,128]{3,2,1,0:T(8,128)(2,1)S(1)}, bf16[2,8,128,128]{3,2,1,0:T(8,128)(2,1)S(1)}, u32[]{:S(2)}, u32[]{:S(2)}) collective-permute-start(bf16[2,8,128,128]{3,2,1,0:T(8,128)(2,1)S(1)} %get-tuple-element.46), channel_id=1, source_target_pairs={{0,8},{8,0},{16,24},{24,16},{1,9},{9,1},{17,25},{25,17},{2,10},{10... | collective-permute-start | bytes 1572872 | tf_op jit(solution)/shard_map/ppermute | solution.py:48
  102.5 41.0 %collective-permute-start.22 = (bf16[2,8,128,128]{3,2,1,0:T(8,128)(2,1)S(1)}, bf16[2,8,128,128]{3,2,1,0:T(8,128)(2,1)S(1)}, u32[]{:S(2)}, u32[]{:S(2)}) collective-permute-start(bf16[2,8,128,128]{3,2,1,0:T(8,128)(2,1)S(1)} %collective-permute-done.21.refs_1_), channel_id=1, source_target_pairs={{0,8},{8,0},{16,24},{24,16},{1,9},{9,1},{17,25},{25,17},{2,10},{10... | collective-permute-start | bytes 1572872 | tf_op jit(solution)/shard_map/ppermute | solution.py:48
  102.8 20.7 %collective-permute-start.17 = (bf16[2,1,128,128]{3,2,1,0:T(8,128)(2,1)S(1)}, bf16[2,1,128,128]{3,2,1,0:T(8,128)(2,1)S(1)}, u32[]{:S(2)}, u32[]{:S(2)}) collective-permute-start(bf16[2,1,128,128]{3,2,1,0:T(8,128)(2,1)S(1)} %get-tuple-element.41), channel_id=1, source_target_pairs={{0,8},{8,24},{24,16},{16,17},{17,25},{25,9},{9,1},{1,2},{2,10},{10... | collective-permute-start | bytes 196616 | tf_op jit(solution)/shard_map/ppermute | solution.py:686
  123.4 6.4 %collective-permute-start.18 = (bf16[2,1,128,128]{3,2,1,0:T(8,128)(2,1)S(1)}, bf16[2,1,128,128]{3,2,1,0:T(8,128)(2,1)S(1)}, u32[]{:S(2)}, u32[]{:S(2)}) collective-permute-start(bf16[2,1,128,128]{3,2,1,0:T(8,128)(2,1)S(1)} %get-tuple-element.42), channel_id=1, source_target_pairs={{8,0},{24,8},{16,24},{17,16},{25,17},{9,25},{1,9},{2,1},{10,2},{26... | collective-permute-start | bytes 196616 | tf_op jit(solution)/shard_map/ppermute | solution.py:687
  125.3 16.2 %collective-permute-start.24 = (bf16[2,6,128,128]{3,2,1,0:T(8,128)(2,1)S(1)}, bf16[2,6,128,128]{3,2,1,0:T(8,128)(2,1)S(1)}, u32[]{:S(2)}, u32[]{:S(2)}) collective-permute-start(bf16[2,6,128,128]{3,2,1,0:T(8,128)(2,1)S(1)} %collective-permute-done.23.refs_0_), channel_id=1, source_target_pairs={{0,16},{8,24},{16,0},{24,8},{1,17},{9,25},{17,1},{25,9},{2,18},{10... | collective-permute-start | bytes 1179656 | tf_op jit(solution)/shard_map/ppermute | solution.py:48
  131.4 4.2 %collective-permute-start.19 = (bf16[2,2,128,128]{3,2,1,0:T(8,128)(2,1)S(1)}, bf16[2,2,128,128]{3,2,1,0:T(8,128)(2,1)S(1)}, u32[]{:S(2)}, u32[]{:S(2)}) collective-permute-start(bf16[2,2,128,128]{3,2,1,0:T(8,128)(2,1)S(1)} %get-tuple-element.45), channel_id=1, source_target_pairs={{0,8},{8,0},{16,24},{24,16},{1,9},{9,1},{17,25},{25,17},{2,10},{10... | collective-permute-start | bytes 393224 | tf_op jit(solution)/shard_map/ppermute | solution.py:48
  135.6 5.0 %collective-permute-start.25 = (bf16[2,2,128,128]{3,2,1,0:T(8,128)(2,1)S(1)}, bf16[2,2,128,128]{3,2,1,0:T(8,128)(2,1)S(1)}, u32[]{:S(2)}, u32[]{:S(2)}) collective-permute-start(bf16[2,2,128,128]{3,2,1,0:T(8,128)(2,1)S(1)} %get-tuple-element.45), channel_id=1, source_target_pairs={{0,16},{8,24},{16,0},{24,8},{1,17},{9,25},{17,1},{25,9},{2,18},{10... | collective-permute-start | bytes 393224 | tf_op jit(solution)/shard_map/ppermute | solution.py:48
  136.4 7.0 %collective-permute-start.20 = (bf16[2,2,128,128]{3,2,1,0:T(8,128)(2,1)S(1)}, bf16[2,2,128,128]{3,2,1,0:T(8,128)(2,1)S(1)}, u32[]{:S(2)}, u32[]{:S(2)}) collective-permute-start(bf16[2,2,128,128]{3,2,1,0:T(8,128)(2,1)S(1)} %collective-permute-done.19.refs_0_), channel_id=1, source_target_pairs={{0,16},{8,24},{16,0},{24,8},{1,17},{9,25},{17,1},{25,9},{2,18},{10... | collective-permute-start | bytes 393224 | tf_op jit(solution)/shard_map/ppermute | solution.py:48

commit v6 on v5

--- a/solution.py
+++ b/solution.py
@@ -471,8 +471,10 @@
             half_ref[k, held] = volume_ref[k, held] - step_size * plane
     if final:
         low_ref, high_ref, part_ref, fresh_ref = refs[2 * groups + 2 :]
-        low_ref[...] = half_ref[:, :1].astype(BF16)
-        high_ref[...] = half_ref[:, share - 1 :].astype(BF16)
+        low, high = half_ref[:, :1].astype(F32), half_ref[:, share - 1 :].astype(F32)
+        odd = share_at(0, lax.axis_size("view")) & 1
+        low_ref[...] = jnp.where(odd == 1, low, high).astype(BF16)
+        high_ref[...] = jnp.where(odd == 1, high, low).astype(BF16)
         inner_columns(half_ref, part_ref, fresh_ref, inner_runs(share)[0][0])
 
 
@@ -513,7 +515,7 @@
     )(*near(half))
 
 
-def third_kernel(half_ref, before_ref, after_ref, first_ref, second_ref, part_ref, whole_ref, *rest):
+def third_kernel(half_ref, inside_ref, across_ref, first_ref, second_ref, part_ref, whole_ref, *rest):
     edges, sems = rest
     share = half_ref.shape[1]
     start = share_at(0, whole_ref.shape[1] // share) * share
@@ -529,11 +531,13 @@
 
     for ref, run in zip((first_ref, second_ref), inner_runs(share)):
         put(ref, *run)
+    odd = share_at(0, whole_ref.shape[1] // share) & 1
     for k in range(2):
+        inside, across = inside_ref[k, 0].astype(F32), across_ref[k, 0].astype(F32)
         for n, (c, before, after) in enumerate(
             (
-                (0, before_ref[k, 0].astype(F32), half_ref[k, 1]),
-                (share - 1, half_ref[k, share - 2], after_ref[k, 0].astype(F32)),
+                (0, jnp.where(odd == 1, inside, across), half_ref[k, 1]),
+                (share - 1, half_ref[k, share - 2], jnp.where(odd == 1, across, inside)),
             )
         ):
             here = half_ref[k, c]
@@ -546,7 +550,7 @@
         move.wait()
 
 
-def third_part(half, before, after, first, second, vcols):
+def third_part(half, inside, across, first, second, vcols):
     _, _, depth, rows = half.shape
     vmem = pl.BlockSpec(memory_space=VMEM)
     return pl.pallas_call(
@@ -560,7 +564,7 @@
         scratch_shapes=[VMEM((2, 2, depth, rows), F32), pltpu.SemaphoreType.DMA((4,))],
         compiler_params=limit(16),
         name="third_part",
-    )(*near(half, before, after, first, second))
+    )(*near(half, inside, across, first, second))
 
 
 def place_kernel(kinds, groups, *refs):
@@ -676,17 +680,18 @@
 
     middle = groups // 2
     (half,) = half_step_of(weight_pieces[:middle], all_windows[:middle], volume_own, False)
-    half, low_edge, high_edge, part_a, fresh_a = half_step_of(
+    half, inner_edge, outer_edge, part_a, fresh_a = half_step_of(
         weight_pieces[middle:], all_windows[middle:], half, True
     )
     order = []
     for t in range(tiles):
         order += [gray(r) * tiles + t for r in range(groups)][:: -1 if t % 2 else 1]
-    up = list(zip(order[:-1], order[1:]))
-    before = lax.ppermute(high_edge, ("view", "tile"), up)
-    after = lax.ppermute(low_edge, ("view", "tile"), [(b, a) for a, b in up])
+    links = list(zip(order[:-1], order[1:]))
+    links = [links[start::2] + [(b, a) for a, b in links[start::2]] for start in range(2)]
+    inside = lax.ppermute(inner_edge, ("view", "tile"), links[0])
+    across = lax.ppermute(outer_edge, ("view", "tile"), links[1])
     part_b, fresh_b = second_part(half)
-    part_c, volume_new = third_part(half, before, after, fresh_a, fresh_b, volume.shape[1])
+    part_c, volume_new = third_part(half, inside, across, fresh_a, fresh_b, volume.shape[1])
     held = {(0, 0): part_a, (1, 0): part_b, (2, 0): part_c}
     for masks in zip(view_masks, view_masks[::-1], view_masks):
         arrived = {}

time: 147 us -> 148 us (level)
  waiting for transfers between devices: 77 us -> 84.1 us
  starting transfers between devices: 41.2 us -> 34.9 us
    ppermute x2, waiting for transfers between devices: 12.4 us -> 20 us  [the longest x1 19.5 us: per_device(): inside = lax.ppermute(inner_edge, ('view', 'tile'), links[0])]
    ppermute x2, starting transfers between devices: 10.2 us -> 6.79 us  [the longest x1 5.61 us: per_device(): across = lax.ppermute(outer_edge, ('view', 'tile'), links[1])]
    ppermute x22, starting transfers between devices: 17.6 us -> 14.6 us  [swapped(): return lax.ppermute(value, axis, [(i, i ^ mask) for i in range(count)])]
where the time goes in v6:
time: 148 us; the launch traced here: 145 us
  waiting for transfers between devices  84.1 us (57%)
  starting transfers between devices  34.9 us (24%)
  Pallas kernels  23.9 us (16%)
    ppermute x22, waiting for transfers between devices, swapped(): return lax.ppermute(value, axis, [(i, i ^ mask) for i in range(count)])  58.9 us
    ppermute x1, waiting for transfers between devices, per_device(): inside = lax.ppermute(inner_edge, ('view', 'tile'), links[0])  19.5 us
    ppermute x22, starting transfers between devices, swapped(): return lax.ppermute(value, axis, [(i, i ^ mask) for i in range(count)])  14.6 us
    ppermute x4, starting transfers between devices, passed_along(): lax.ppermute(value, axis, [(source, source + steps) for source in range(i...  13.5 us
    ppermute x1, starting transfers between devices, per_device(): across = lax.ppermute(outer_edge, ('view', 'tile'), links[1])  5.61 us
    pallas_call x5, Pallas kernels, place(): pl.pallas_call(functools.partial(place_kernel, kinds, groups), out_shape=...  5.59 us
    pallas_call x1, Pallas kernels, patches(): pl.pallas_call(patch_kernel, out_shape=(VMEM((views, 3, width, rows), F32...  5.53 us
    ppermute x4, waiting for transfers between devices, passed_along(): lax.ppermute(value, axis, [(source, source + steps) for source in range(i...  5.29 us
  transfers between devices with their start and end apart: 28, of which 15 were waited for; matrix products, arithmetic and copies ran while one was open for 1% of the time, Pallas kernels for 5%

profile of v6, /device:TPU:1, one launch (start us, length us, event | category | flops | bytes accessed | tf_op | source)
XLA Modules:
  0.0 145.3 jit_solution(9999988506101035961)
XLA Ops:
  0.6 1.7 %deal.2 = (bf16[2,128,2048]{2,1,0:T(8,128)(2,1)S(1)}, bf16[2,128,2048]{2,1,0:T(8,128)(2,1)S(1)}) custom-call(bf16[2,128,8192]{2,1,0:T(8,128)(2,1)} %weights_ref.3), custom_call_target="tpu_custom_call" | custom-call | tf_op jit(solution)/shard_map/deal/pallas_call | solution.py:94
  2.4 0.0 copy-start.3
  2.4 0.0 copy-start.4
  2.4 0.0 copy-start.7
  2.4 0.0 copy-start.8
  2.5 2.3 %deal.3 = (bf16[2,128,2048]{2,1,0:T(8,128)(2,1)S(1)}, bf16[2,128,2048]{2,1,0:T(8,128)(2,1)S(1)}) custom-call(bf16[2,128,8192]{2,1,0:T(8,128)(2,1)} %weights_ref.3), custom_call_target="tpu_custom_call" | custom-call | tf_op jit(solution)/shard_map/deal/pallas_call | solution.py:94
  4.8 0.5 copy-done
  5.3 1.8 %project.1 = (bf16[4,2,2,64,128]{4,3,2,1,0:T(8,128)(2,1)S(1)}, bf16[4,2,2,64,128]{4,3,2,1,0:T(8,128)(2,1)S(1)}, f32[2,16,128,128]{3,2,1,0:T(8,128)S(1)}) custom-call(s32[2]{0:T(128)} %bitcast.33, f32[2,64,128,128]{3,2,1,0:T(8,128)S(1)} %copy-done, bf16[2,128,2048]{2,1,0:T(8,128)(2,1)S(1)} %get-tuple-element.26.refs_0_, ...), custom_call_target="tpu_custom_call" | custom-call | tf_op jit(solution)/shard_map/project/pallas_call | solution.py:175
  7.1 0.1 collective-permute-start.2
  7.3 2.4 %collective-permute-start = (bf16[2,2,64,128]{3,2,1,0:T(8,128)(2,1)S(1)}, bf16[2,2,64,128]{3,2,1,0:T(8,128)(2,1)S(1)}, u32[]{:S(2)}, u32[]{:S(2)}) collective-permute-start(bf16[2,2,64,128]{3,2,1,0:T(8,128)(2,1)S(1)} %convert_element_type.22), channel_id=1, source_target_pairs={{1,0},{2,1},{3,2},{4,3},{5,4},{6,5},{7,6},{9,8},{10,9},{11,10},{12... | collective-permute-start | bytes 196616 | tf_op jit(solution)/shard_map/ppermute | solution.py:26
  9.7 1.3 collective-permute-start.1
  11.0 0.1 fold.2
  11.0 2.7 %collective-permute-done.one_ref = bf16[2,2,64,128]{3,2,1,0:T(8,128)(2,1)S(1)} collective-permute-done((bf16[2,2,64,128]{3,2,1,0:T(8,128)(2,1)S(1)}, bf16[2,2,64,128]{3,2,1,0:T(8,128)(2,1)S(1)}, u32[]{:S(2)}, u32[]{:S(2)}) %collective-permute-start) | collective-permute-done | bytes 65568 | tf_op jit(solution)/shard_map/ppermute | solution.py:26
  13.8 2.5 %collective-permute-done.1.two_ref = bf16[2,2,64,128]{3,2,1,0:T(8,128)(2,1)S(1)} collective-permute-done((bf16[2,2,64,128]{3,2,1,0:T(8,128)(2,1)S(1)}, bf16[2,2,64,128]{3,2,1,0:T(8,128)(2,1)S(1)}, u32[]{:S(2)}, u32[]{:S(2)}) %collective-permute-start.1) | collective-permute-done | bytes 65568 | tf_op jit(solution)/shard_map/ppermute | solution.py:26
  16.4 5.5 %patches.1 = (f32[2,3,64,128]{3,2,1,0:T(8,128)S(1)}, bf16[2,3,64,128]{3,2,1,0:T(8,128)(2,1)S(1)}, bf16[2,3,64,128]{3,2,1,0:T(8,128)(2,1)S(1)}) custom-call(s32[2,32]{1,0:T(2,128)S(1)} %copy-done.5, s32[2]{0:T(128)S(1)} %bitcast.35, f32[2,2,64,128]{3,2,1,0:T(8,128)S(1)} %copy-done.1, bf16[2,2,64,128]{3,2,1,0:T(8,128)(2,1)S(1)} %collective-permute-done.one_ref, ...), custom_call_target="tpu_custom_call" | custom-call | flops 2147483648 | bytes 4194304 | tf_op jit(solution)/shard_map/patches/pallas_call | solution.py:341
  21.9 1.9 %collective-permute-start.3 = (bf16[2,3,64,128]{3,2,1,0:T(8,128)(2,1)S(1)}, bf16[2,3,64,128]{3,2,1,0:T(8,128)(2,1)S(1)}, u32[]{:S(2)}, u32[]{:S(2)}) collective-permute-start(bf16[2,3,64,128]{3,2,1,0:T(8,128)(2,1)S(1)} %get-tuple-element.34), channel_id=1, source_target_pairs={{0,1},{1,2},{2,3},{3,4},{4,5},{5,6},{6,7},{8,9},{9,10},{10,11},{11... | collective-permute-start | bytes 294920 | tf_op jit(solution)/shard_map/ppermute | solution.py:26
  23.8 7.9 %collective-permute-start.4 = (bf16[2,3,64,128]{3,2,1,0:T(8,128)(2,1)S(1)}, bf16[2,3,64,128]{3,2,1,0:T(8,128)(2,1)S(1)}, u32[]{:S(2)}, u32[]{:S(2)}) collective-permute-start(bf16[2,3,64,128]{3,2,1,0:T(8,128)(2,1)S(1)} %get-tuple-element.35), channel_id=1, source_target_pairs={{0,2},{1,3},{2,4},{3,5},{4,6},{5,7},{8,10},{9,11},{10,12},{11,13},... | collective-permute-start | bytes 294920 | tf_op jit(solution)/shard_map/ppermute | solution.py:26
  31.7 0.1 collective-permute-start.15
  31.8 0.1 collective-permute-start.7
  31.9 2.6 %collective-permute-start.8 = (bf16[2,128,2048]{2,1,0:T(8,128)(2,1)S(1)}, bf16[2,128,2048]{2,1,0:T(8,128)(2,1)S(1)}, u32[]{:S(2)}, u32[]{:S(2)}) collective-permute-start(bf16[2,128,2048]{2,1,0:T(8,128)(2,1)S(1)} %get-tuple-element.27.refs_1_), channel_id=1, source_target_pairs={{0,8},{8,0},{16,24},{24,16},{1,9},{9,1},{17,25},{25,17},{2,10},{10... | collective-permute-start | bytes 3145736 | tf_op jit(solution)/shard_map/ppermute | solution.py:48
  34.5 8.5 %collective-permute-done.5.arrived_ref = bf16[2,2,2,64,128]{4,3,2,1,0:T(8,128)(2,1)S(1)} collective-permute-done((bf16[2,2,2,64,128]{4,3,2,1,0:T(8,128)(2,1)S(1)}, bf16[2,2,2,64,128]{4,3,2,1,0:T(8,128)(2,1)S(1)}, u32[]{:S(2)}, u32[]{:S(2)}) %collective-permute-start.5) | collective-permute-done | bytes 131104 | tf_op jit(solution)/shard_map/ppermute | solution.py:48
  43.0 0.1 collective-permute-start.6
  43.1 3.4 %collective-permute-done.6 = bf16[1,2,2,64,128]{4,3,2,1,0:T(8,128)(2,1)S(1)} collective-permute-done((bf16[1,2,2,64,128]{4,3,2,1,0:T(8,128)(2,1)S(1)}, bf16[1,2,2,64,128]{4,3,2,1,0:T(8,128)(2,1)S(1)}, u32[]{:S(2)}, u32[]{:S(2)}) %collective-permute-start.6) | collective-permute-done | bytes 65568 | tf_op jit(solution)/shard_map/ppermute | solution.py:48
  46.5 0.1 fusion.6
  46.5 0.0 copy-start.10
  46.6 0.1 collective-permute-start.9
  46.6 0.1 collective-permute-start.10
  46.7 3.3 %collective-permute-done.9 = bf16[2,2,64,128]{3,2,1,0:T(8,128)(2,1)S(1)} collective-permute-done((bf16[2,2,64,128]{3,2,1,0:T(8,128)(2,1)S(1)}, bf16[2,2,64,128]{3,2,1,0:T(8,128)(2,1)S(1)}, u32[]{:S(2)}, u32[]{:S(2)}) %collective-permute-start.9) | collective-permute-done | bytes 65568 | tf_op jit(solution)/shard_map/ppermute | solution.py:48
  50.0 0.1 collective-permute-start.11
  50.2 0.8 collective-permute-done.10
  51.0 3.9 %collective-permute-done.11 = bf16[2,2,64,128]{3,2,1,0:T(8,128)(2,1)S(1)} collective-permute-done((bf16[2,2,64,128]{3,2,1,0:T(8,128)(2,1)S(1)}, bf16[2,2,64,128]{3,2,1,0:T(8,128)(2,1)S(1)}, u32[]{:S(2)}, u32[]{:S(2)}) %collective-permute-start.11) | collective-permute-done | bytes 65568 | tf_op jit(solution)/shard_map/ppermute | solution.py:48
  55.0 3.7 %collective-permute-start.12 = (bf16[4,2,2,64,128]{4,3,2,1,0:T(8,128)(2,1)S(1)}, bf16[4,2,2,64,128]{4,3,2,1,0:T(8,128)(2,1)S(1)}, u32[]{:S(2)}, u32[]{:S(2)}) collective-permute-start(bf16[4,2,2,64,128]{4,3,2,1,0:T(8,128)(2,1)S(1)} %pad_maximum_fusion), channel_id=1, source_target_pairs={{0,1},{1,0},{2,3},{3,2},{4,5},{5,4},{6,7},{7,6},{8,9},{9,8},{10,11... | collective-permute-start | bytes 786440 | tf_op jit(solution)/shard_map/ppermute | solution.py:48
  58.7 1.2 collective-permute-done.12.refs_4_
  59.9 0.7 cut.1.refs_2_
  60.5 0.4 collective-permute-start.16
  61.0 1.1 collective-permute-start.13
  62.1 21.9 %collective-permute-done.16.refs_3_ = bf16[2,2,128,128]{3,2,1,0:T(8,128)(2,1)S(1)} collective-permute-done((bf16[2,2,128,128]{3,2,1,0:T(8,128)(2,1)S(1)}, bf16[2,2,128,128]{3,2,1,0:T(8,128)(2,1)S(1)}, u32[]{:S(2)}, u32[]{:S(2)}) %collective-permute-start.16) | collective-permute-done | bytes 131104 | tf_op jit(solution)/shard_map/ppermute | solution.py:48
  84.0 0.8 half_step.2.refs_4_
  84.7 3.0 %collective-permute-done.14.refs_3_ = bf16[2,2,128,128]{3,2,1,0:T(8,128)(2,1)S(1)} collective-permute-done((bf16[2,2,128,128]{3,2,1,0:T(8,128)(2,1)S(1)}, bf16[2,2,128,128]{3,2,1,0:T(8,128)(2,1)S(1)}, u32[]{:S(2)}, u32[]{:S(2)}) %collective-permute-start.14) | collective-permute-done | bytes 131104 | tf_op jit(solution)/shard_map/ppermute | solution.py:48
  87.8 2.1 %half_step.3 = (f32[2,16,128,128]{3,2,1,0:T(8,128)S(1)}, bf16[2,1,128,128]{3,2,1,0:T(8,128)(2,1)S(1)}, bf16[2,1,128,128]{3,2,1,0:T(8,128)(2,1)S(1)}, bf16[2,6,12...) custom-call(bf16[2,128,2048]{2,1,0:T(8,128)(2,1)S(1)} %collective-permute-done.7.refs_0_, ...), custom_call_target="tpu_custom_call" | custom-call | tf_op jit(solution)/shard_map/half_step/pallas_call | solution.py:490
  89.8 1.7 %second_part.1 = (bf16[2,8,128,128]{3,2,1,0:T(8,128)(2,1)S(1)}, f32[2,8,128,128]{3,2,1,0:T(8,128)S(1)}) custom-call(f32[2,16,128,128]{3,2,1,0:T(8,128)S(1)} %get-tuple-element.40.half_ref), custom_call_target="tpu_custom_call" | custom-call | tf_op jit(solution)/shard_map/second_part/pallas_call | solution.py:508
  91.6 0.1 collective-permute-start.21
  91.6 0.1 collective-permute-start.23
  91.7 1.4 collective-permute-start.27
  93.1 1.5 %collective-permute-start.26 = (bf16[2,8,128,128]{3,2,1,0:T(8,128)(2,1)S(1)}, bf16[2,8,128,128]{3,2,1,0:T(8,128)(2,1)S(1)}, u32[]{:S(2)}, u32[]{:S(2)}) collective-permute-start(bf16[2,8,128,128]{3,2,1,0:T(8,128)(2,1)S(1)} %get-tuple-element.46), channel_id=1, source_target_pairs={{0,8},{8,0},{16,24},{24,16},{1,9},{9,1},{17,25},{25,17},{2,10},{10... | collective-permute-start | bytes 1572872 | tf_op jit(solution)/shard_map/ppermute | solution.py:48
  94.6 7.9 %collective-permute-done.21.refs_1_ = bf16[2,8,128,128]{3,2,1,0:T(8,128)(2,1)S(1)} collective-permute-done((bf16[2,8,128,128]{3,2,1,0:T(8,128)(2,1)S(1)}, bf16[2,8,128,128]{3,2,1,0:T(8,128)(2,1)S(1)}, u32[]{:S(2)}, u32[]{:S(2)}) %collective-permute-start.21) | collective-permute-done | bytes 524320 | tf_op jit(solution)/shard_map/ppermute | solution.py:48
  102.5 0.3 collective-permute-start.22
  102.8 1.2 collective-permute-start.17
  104.0 19.5 %collective-permute-done.17.inside_ref = bf16[2,1,128,128]{3,2,1,0:T(8,128)(2,1)S(1)} collective-permute-done((bf16[2,1,128,128]{3,2,1,0:T(8,128)(2,1)S(1)}, bf16[2,1,128,128]{3,2,1,0:T(8,128)(2,1)S(1)}, u32[]{:S(2)}, u32[]{:S(2)}) %collective-permute-start.17) | collective-permute-done | bytes 65568 | tf_op jit(solution)/shard_map/ppermute | solution.py:691
  123.4 5.6 %collective-permute-start.18 = (bf16[2,1,128,128]{3,2,1,0:T(8,128)(2,1)S(1)}, bf16[2,1,128,128]{3,2,1,0:T(8,128)(2,1)S(1)}, u32[]{:S(2)}, u32[]{:S(2)}) collective-permute-start(bf16[2,1,128,128]{3,2,1,0:T(8,128)(2,1)S(1)} %get-tuple-element.42), channel_id=1, source_target_pairs={{8,24},{16,17},{25,9},{1,2},{10,26},{18,19},{27,11},{3,4},{12,28},... | collective-permute-start | bytes 196616 | tf_op jit(solution)/shard_map/ppermute | solution.py:692
  129.0 1.4 collective-permute-start.24
  130.5 0.5 collective-permute-done.18.across_ref
  131.0 1.5 %third_part.1 = (bf16[2,2,128,128]{3,2,1,0:T(8,128)(2,1)S(1)}, f32[2,64,128,128]{3,2,1,0:T(8,128)}) custom-call(f32[2,16,128,128]{3,2,1,0:T(8,128)S(1)} %get-tuple-element.40.half_ref, bf16[2,1,128,128]{3,2,1,0:T(8,128)(2,1)S(1)} %collective-permute-done.17.inside_ref, bf16[2,1,128,128]{3,2,1,0:T(8,128)(2,1)S(1)} %collective-permute-done.18.across_ref, ...), custom_call_target="tpu_custom_call" | custom-call | tf_op jit(solution)/shard_map/third_part/pallas_call | solution.py:556
  132.5 0.1 collective-permute-start.19
  132.6 4.1 %collective-permute-done.19.refs_0_ = bf16[2,2,128,128]{3,2,1,0:T(8,128)(2,1)S(1)} collective-permute-done((bf16[2,2,128,128]{3,2,1,0:T(8,128)(2,1)S(1)}, bf16[2,2,128,128]{3,2,1,0:T(8,128)(2,1)S(1)}, u32[]{:S(2)}, u32[]{:S(2)}) %collective-permute-start.19) | collective-permute-done | bytes 131104 | tf_op jit(solution)/shard_map/ppermute | solution.py:48
  136.7 0.3 collective-permute-start.25
  137.0 1.2 collective-permute-start.20
  138.2 0.7 fusion.4
  138.8 1.2 place.5.refs_2_
  140.1 1.4 place.6.refs_2_
  141.5 0.9 place.7.refs_1_
  142.4 0.9 place.8.refs_2_
  143.4 0.8 collective-permute-done.20.refs_0_
  144.2 1.1 place.9
  (36 shorter events, 0.2 us)
Async XLA Ops:
  0.6 4.7 %copy-start = (f32[2,64,128,128]{3,2,1,0:T(8,128)S(1)}, f32[2,64,128,128]{3,2,1,0:T(8,128)}, u32[]{:S(2)}) copy-start(f32[2,64,128,128]{3,2,1,0:T(8,128)} %volume_ref.1) | copy-start | bytes 25165828
  2.4 4.9 %copy-start.1 = (f32[2,2,64,128]{3,2,1,0:T(8,128)S(1)}, f32[2,2,64,128]{3,2,1,0:T(8,128)}, u32[]{:S(2)}) copy-start(f32[2,2,64,128]{3,2,1,0:T(8,128)} %own_ref.1) | copy-start | bytes 393220
  2.4 13.9 %copy-start.3 = (s32[2,32,128,128]{3,2,1,0:T(8,128)S(1)}, s32[2,32,128,128]{3,2,1,0:T(8,128)}, u32[]{:S(2)}) copy-start(s32[2,32,128,128]{3,2,1,0:T(8,128)} %counts_ref.1) | copy-start | bytes 12582916
  2.4 13.9 %copy-start.4 = (f32[2,128,128]{2,1,0:T(8,128)S(1)}, f32[2,128,128]{2,1,0:T(8,128)}, u32[]{:S(2)}) copy-start(f32[2,128,128]{2,1,0:T(8,128)} %probe_ref.1) | copy-start | bytes 393220
  2.4 13.9 %copy-start.5 = (s32[2,32]{1,0:T(2,128)S(1)}, s32[2,32]{1,0:T(2,128)}, u32[]{:S(2)}) copy-start(s32[2,32]{1,0:T(2,128)} %positions.1) | copy-start | bytes 772
  2.4 13.9 %copy-start.6 = (s32[2,1]{0,1:T(1,128)S(1)}, s32[2,1]{0,1:T(1,128)}, u32[]{:S(2)}) copy-start(s32[2,1]{0,1:T(1,128)} %param.15) | copy-start | bytes 28
  2.4 13.9 %copy-start.7 = (bf16[256,256]{1,0:T(8,128)(2,1)S(1)}, bf16[256,256]{1,0:T(8,128)(2,1)}, u32[]{:S(2)}) copy-start(bf16[256,256]{1,0:T(8,128)(2,1)} %constant.17.forward_ref) | copy-start | bytes 393220
  2.4 13.9 %copy-start.8 = (bf16[256,256]{1,0:T(8,128)(2,1)S(1)}, bf16[256,256]{1,0:T(8,128)(2,1)}, u32[]{:S(2)}) copy-start(bf16[256,256]{1,0:T(8,128)(2,1)} %constant.18.inverse_ref) | copy-start | bytes 393220
  5.3 41.2 %copy-start.9 = (f32[2,2,64,128]{3,2,1,0:T(8,128)S(1)}, f32[2,2,64,128]{3,2,1,0:T(8,128)}, u32[]{:S(2)}) copy-start(f32[2,2,64,128]{3,2,1,0:T(8,128)} %param.12) | copy-start | bytes 393220
  7.1 52.7 %copy-start.2 = (s32[2,1]{0,1:T(1,128)S(1)}, s32[2,1]{0,1:T(1,128)}, u32[]{:S(2)}) copy-start(s32[2,1]{0,1:T(1,128)} %param.17) | copy-start | bytes 28
  7.1 3.8 %collective-permute-start.2 = (bf16[4,2,2,64,128]{4,3,2,1,0:T(8,128)(2,1)S(1)}, bf16[4,2,2,64,128]{4,3,2,1,0:T(8,128)(2,1)S(1)}, u32[]{:S(2)}, u32[]{:S(2)}) collective-permute-start(bf16[4,2,2,64,128]{4,3,2,1,0:T(8,128)(2,1)S(1)} %get-tuple-element.31), channel_id=1, source_target_pairs={{0,1},{1,0},{2,3},{3,2},{4,5},{5,4},{6,7},{7,6},{8,9},{9,8},{10,11... | collective-permute-start | bytes 786440 | tf_op jit(solution)/shard_map/ppermute | solution.py:48
  7.3 6.5 %collective-permute-start = (bf16[2,2,64,128]{3,2,1,0:T(8,128)(2,1)S(1)}, bf16[2,2,64,128]{3,2,1,0:T(8,128)(2,1)S(1)}, u32[]{:S(2)}, u32[]{:S(2)}) collective-permute-start(bf16[2,2,64,128]{3,2,1,0:T(8,128)(2,1)S(1)} %convert_element_type.22), channel_id=1, source_target_pairs={{1,0},{2,1},{3,2},{4,3},{5,4},{6,5},{7,6},{9,8},{10,9},{11,10},{12... | collective-permute-start | bytes 196616 | tf_op jit(solution)/shard_map/ppermute | solution.py:26
  9.7 6.7 %collective-permute-start.1 = (bf16[2,2,64,128]{3,2,1,0:T(8,128)(2,1)S(1)}, bf16[2,2,64,128]{3,2,1,0:T(8,128)(2,1)S(1)}, u32[]{:S(2)}, u32[]{:S(2)}) collective-permute-start(bf16[2,2,64,128]{3,2,1,0:T(8,128)(2,1)S(1)} %convert_element_type.22), channel_id=1, source_target_pairs={{2,0},{3,1},{4,2},{5,3},{6,4},{7,5},{10,8},{11,9},{12,10},{13,11},... | collective-permute-start | bytes 196616 | tf_op jit(solution)/shard_map/ppermute | solution.py:26
  21.9 12.5 %collective-permute-start.3 = (bf16[2,3,64,128]{3,2,1,0:T(8,128)(2,1)S(1)}, bf16[2,3,64,128]{3,2,1,0:T(8,128)(2,1)S(1)}, u32[]{:S(2)}, u32[]{:S(2)}) collective-permute-start(bf16[2,3,64,128]{3,2,1,0:T(8,128)(2,1)S(1)} %get-tuple-element.34), channel_id=1, source_target_pairs={{0,1},{1,2},{2,3},{3,4},{4,5},{5,6},{6,7},{8,9},{9,10},{10,11},{11... | collective-permute-start | bytes 294920 | tf_op jit(solution)/shard_map/ppermute | solution.py:26
  23.8 10.6 %collective-permute-start.4 = (bf16[2,3,64,128]{3,2,1,0:T(8,128)(2,1)S(1)}, bf16[2,3,64,128]{3,2,1,0:T(8,128)(2,1)S(1)}, u32[]{:S(2)}, u32[]{:S(2)}) collective-permute-start(bf16[2,3,64,128]{3,2,1,0:T(8,128)(2,1)S(1)} %get-tuple-element.35), channel_id=1, source_target_pairs={{0,2},{1,3},{2,4},{3,5},{4,6},{5,7},{8,10},{9,11},{10,12},{11,13},... | collective-permute-start | bytes 294920 | tf_op jit(solution)/shard_map/ppermute | solution.py:26
  31.7 52.3 %collective-permute-start.15 = (bf16[2,128,2048]{2,1,0:T(8,128)(2,1)S(1)}, bf16[2,128,2048]{2,1,0:T(8,128)(2,1)S(1)}, u32[]{:S(2)}, u32[]{:S(2)}) collective-permute-start(bf16[2,128,2048]{2,1,0:T(8,128)(2,1)S(1)} %get-tuple-element.28.refs_2_), channel_id=1, source_target_pairs={{0,16},{8,24},{16,0},{24,8},{1,17},{9,25},{17,1},{25,9},{2,18},{10... | collective-permute-start | bytes 3145736 | tf_op jit(solution)/shard_map/ppermute | solution.py:48
  31.8 56.0 %collective-permute-start.7 = (bf16[2,128,2048]{2,1,0:T(8,128)(2,1)S(1)}, bf16[2,128,2048]{2,1,0:T(8,128)(2,1)S(1)}, u32[]{:S(2)}, u32[]{:S(2)}) collective-permute-start(bf16[2,128,2048]{2,1,0:T(8,128)(2,1)S(1)} %get-tuple-element.29.refs_3_), channel_id=1, source_target_pairs={{0,24},{8,16},{16,8},{24,0},{1,25},{9,17},{17,9},{25,1},{2,26},{10... | collective-permute-start | bytes 3145736 | tf_op jit(solution)/shard_map/ppermute | solution.py:48
  31.9 55.9 %collective-permute-start.8 = (bf16[2,128,2048]{2,1,0:T(8,128)(2,1)S(1)}, bf16[2,128,2048]{2,1,0:T(8,128)(2,1)S(1)}, u32[]{:S(2)}, u32[]{:S(2)}) collective-permute-start(bf16[2,128,2048]{2,1,0:T(8,128)(2,1)S(1)} %get-tuple-element.27.refs_1_), channel_id=1, source_target_pairs={{0,8},{8,0},{16,24},{24,16},{1,9},{9,1},{17,25},{25,17},{2,10},{10... | collective-permute-start | bytes 3145736 | tf_op jit(solution)/shard_map/ppermute | solution.py:48
  34.4 8.6 %collective-permute-start.5 = (bf16[2,2,2,64,128]{4,3,2,1,0:T(8,128)(2,1)S(1)}, bf16[2,2,2,64,128]{4,3,2,1,0:T(8,128)(2,1)S(1)}, u32[]{:S(2)}, u32[]{:S(2)}) collective-permute-start(bf16[2,2,2,64,128]{4,3,2,1,0:T(8,128)(2,1)S(1)} %get-tuple-element.32.token_ref), channel_id=1, source_target_pairs={{0,4},{1,5},{2,6},{3,7},{4,0},{5,1},{6,2},{7,3},{8,12},{9,13},{10,... | collective-permute-start | bytes 393224 | tf_op jit(solution)/shard_map/ppermute | solution.py:48
  43.0 3.5 %collective-permute-start.6 = (bf16[1,2,2,64,128]{4,3,2,1,0:T(8,128)(2,1)S(1)}, bf16[1,2,2,64,128]{4,3,2,1,0:T(8,128)(2,1)S(1)}, u32[]{:S(2)}, u32[]{:S(2)}) collective-permute-start(bf16[1,2,2,64,128]{4,3,2,1,0:T(8,128)(2,1)S(1)} %get-tuple-element.38), channel_id=1, source_target_pairs={{0,2},{1,3},{2,0},{3,1},{4,6},{5,7},{6,4},{7,5},{8,10},{9,11},{10,... | collective-permute-start | bytes 196616 | tf_op jit(solution)/shard_map/ppermute | solution.py:48
  46.5 91.6 %copy-start.10 = (f32[2,2,64,128]{3,2,1,0:T(8,128)}, f32[2,2,64,128]{3,2,1,0:T(8,128)S(1)}, u32[]{:S(2)}) copy-start(f32[2,2,64,128]{3,2,1,0:T(8,128)S(1)} %get-tuple-element.50) | copy-start | bytes 393220
  46.6 3.5 %collective-permute-start.9 = (bf16[2,2,64,128]{3,2,1,0:T(8,128)(2,1)S(1)}, bf16[2,2,64,128]{3,2,1,0:T(8,128)(2,1)S(1)}, u32[]{:S(2)}, u32[]{:S(2)}) collective-permute-start(bf16[2,2,64,128]{3,2,1,0:T(8,128)(2,1)S(1)} %get-tuple-element.49), channel_id=1, source_target_pairs={{0,2},{1,3},{2,0},{3,1},{4,6},{5,7},{6,4},{7,5},{8,10},{9,11},{10,... | collective-permute-start | bytes 196616 | tf_op jit(solution)/shard_map/ppermute | solution.py:48
  46.6 4.4 %collective-permute-start.10 = (bf16[2,2,64,128]{3,2,1,0:T(8,128)(2,1)S(1)}, bf16[2,2,64,128]{3,2,1,0:T(8,128)(2,1)S(1)}, u32[]{:S(2)}, u32[]{:S(2)}) collective-permute-start(bf16[2,2,64,128]{3,2,1,0:T(8,128)(2,1)S(1)} %get-tuple-element.49), channel_id=1, source_target_pairs={{0,4},{1,5},{2,6},{3,7},{4,0},{5,1},{6,2},{7,3},{8,12},{9,13},{10,... | collective-permute-start | bytes 196616 | tf_op jit(solution)/shard_map/ppermute | solution.py:48
  50.0 4.9 %collective-permute-start.11 = (bf16[2,2,64,128]{3,2,1,0:T(8,128)(2,1)S(1)}, bf16[2,2,64,128]{3,2,1,0:T(8,128)(2,1)S(1)}, u32[]{:S(2)}, u32[]{:S(2)}) collective-permute-start(bf16[2,2,64,128]{3,2,1,0:T(8,128)(2,1)S(1)} %get-tuple-element.49), channel_id=1, source_target_pairs={{0,6},{1,7},{2,4},{3,5},{4,2},{5,3},{6,0},{7,1},{8,14},{9,15},{10,... | collective-permute-start | bytes 196616 | tf_op jit(solution)/shard_map/ppermute | solution.py:48
  55.0 4.9 %collective-permute-start.12 = (bf16[4,2,2,64,128]{4,3,2,1,0:T(8,128)(2,1)S(1)}, bf16[4,2,2,64,128]{4,3,2,1,0:T(8,128)(2,1)S(1)}, u32[]{:S(2)}, u32[]{:S(2)}) collective-permute-start(bf16[4,2,2,64,128]{4,3,2,1,0:T(8,128)(2,1)S(1)} %pad_maximum_fusion), channel_id=1, source_target_pairs={{0,1},{1,0},{2,3},{3,2},{4,5},{5,4},{6,7},{7,6},{8,9},{9,8},{10,11... | collective-permute-start | bytes 786440 | tf_op jit(solution)/shard_map/ppermute | solution.py:48
  60.5 23.4 %collective-permute-start.16 = (bf16[2,2,128,128]{3,2,1,0:T(8,128)(2,1)S(1)}, bf16[2,2,128,128]{3,2,1,0:T(8,128)(2,1)S(1)}, u32[]{:S(2)}, u32[]{:S(2)}) collective-permute-start(bf16[2,2,128,128]{3,2,1,0:T(8,128)(2,1)S(1)} %cut.1.refs_2_), channel_id=1, source_target_pairs={{0,16},{8,24},{16,0},{24,8},{1,17},{9,25},{17,1},{25,9},{2,18},{10... | collective-permute-start | bytes 393224 | tf_op jit(solution)/shard_map/ppermute | solution.py:48
  61.0 23.8 %collective-permute-start.13 = (bf16[2,2,128,128]{3,2,1,0:T(8,128)(2,1)S(1)}, bf16[2,2,128,128]{3,2,1,0:T(8,128)(2,1)S(1)}, u32[]{:S(2)}, u32[]{:S(2)}) collective-permute-start(bf16[2,2,128,128]{3,2,1,0:T(8,128)(2,1)S(1)} %cut.1.refs_2_), channel_id=1, source_target_pairs={{0,24},{8,16},{16,8},{24,0},{1,25},{9,17},{17,9},{25,1},{2,26},{10... | collective-permute-start | bytes 393224 | tf_op jit(solution)/shard_map/ppermute | solution.py:48
  83.9 3.8 %collective-permute-start.14 = (bf16[2,2,128,128]{3,2,1,0:T(8,128)(2,1)S(1)}, bf16[2,2,128,128]{3,2,1,0:T(8,128)(2,1)S(1)}, u32[]{:S(2)}, u32[]{:S(2)}) collective-permute-start(bf16[2,2,128,128]{3,2,1,0:T(8,128)(2,1)S(1)} %cut.1.refs_2_), channel_id=1, source_target_pairs={{0,8},{8,0},{16,24},{24,16},{1,9},{9,1},{17,25},{25,17},{2,10},{10... | collective-permute-start | bytes 393224 | tf_op jit(solution)/shard_map/ppermute | solution.py:48
  91.6 10.9 %collective-permute-start.21 = (bf16[2,8,128,128]{3,2,1,0:T(8,128)(2,1)S(1)}, bf16[2,8,128,128]{3,2,1,0:T(8,128)(2,1)S(1)}, u32[]{:S(2)}, u32[]{:S(2)}) collective-permute-start(bf16[2,8,128,128]{3,2,1,0:T(8,128)(2,1)S(1)} %get-tuple-element.46), channel_id=1, source_target_pairs={{0,16},{8,24},{16,0},{24,8},{1,17},{9,25},{17,1},{25,9},{2,18},{10... | collective-permute-start | bytes 1572872 | tf_op jit(solution)/shard_map/ppermute | solution.py:48
  91.6 37.4 %collective-permute-start.23 = (bf16[2,6,128,128]{3,2,1,0:T(8,128)(2,1)S(1)}, bf16[2,6,128,128]{3,2,1,0:T(8,128)(2,1)S(1)}, u32[]{:S(2)}, u32[]{:S(2)}) collective-permute-start(bf16[2,6,128,128]{3,2,1,0:T(8,128)(2,1)S(1)} %get-tuple-element.47), channel_id=1, source_target_pairs={{0,8},{8,0},{16,24},{24,16},{1,9},{9,1},{17,25},{25,17},{2,10},{10... | collective-permute-start | bytes 1179656 | tf_op jit(solution)/shard_map/ppermute | solution.py:48
  91.7 45.3 %collective-permute-start.27 = (bf16[2,6,128,128]{3,2,1,0:T(8,128)(2,1)S(1)}, bf16[2,6,128,128]{3,2,1,0:T(8,128)(2,1)S(1)}, u32[]{:S(2)}, u32[]{:S(2)}) collective-permute-start(bf16[2,6,128,128]{3,2,1,0:T(8,128)(2,1)S(1)} %get-tuple-element.47), channel_id=1, source_target_pairs={{0,16},{8,24},{16,0},{24,8},{1,17},{9,25},{17,1},{25,9},{2,18},{10... | collective-permute-start | bytes 1179656 | tf_op jit(solution)/shard_map/ppermute | solution.py:48
  93.1 47.0 %collective-permute-start.26 = (bf16[2,8,128,128]{3,2,1,0:T(8,128)(2,1)S(1)}, bf16[2,8,128,128]{3,2,1,0:T(8,128)(2,1)S(1)}, u32[]{:S(2)}, u32[]{:S(2)}) collective-permute-start(bf16[2,8,128,128]{3,2,1,0:T(8,128)(2,1)S(1)} %get-tuple-element.46), channel_id=1, source_target_pairs={{0,8},{8,0},{16,24},{24,16},{1,9},{9,1},{17,25},{25,17},{2,10},{10... | collective-permute-start | bytes 1572872 | tf_op jit(solution)/shard_map/ppermute | solution.py:48
  102.5 41.7 %collective-permute-start.22 = (bf16[2,8,128,128]{3,2,1,0:T(8,128)(2,1)S(1)}, bf16[2,8,128,128]{3,2,1,0:T(8,128)(2,1)S(1)}, u32[]{:S(2)}, u32[]{:S(2)}) collective-permute-start(bf16[2,8,128,128]{3,2,1,0:T(8,128)(2,1)S(1)} %collective-permute-done.21.refs_1_), channel_id=1, source_target_pairs={{0,8},{8,0},{16,24},{24,16},{1,9},{9,1},{17,25},{25,17},{2,10},{10... | collective-permute-start | bytes 1572872 | tf_op jit(solution)/shard_map/ppermute | solution.py:48
  102.8 20.7 %collective-permute-start.17 = (bf16[2,1,128,128]{3,2,1,0:T(8,128)(2,1)S(1)}, bf16[2,1,128,128]{3,2,1,0:T(8,128)(2,1)S(1)}, u32[]{:S(2)}, u32[]{:S(2)}) collective-permute-start(bf16[2,1,128,128]{3,2,1,0:T(8,128)(2,1)S(1)} %get-tuple-element.41), channel_id=1, source_target_pairs={{0,8},{24,16},{17,25},{9,1},{2,10},{26,18},{19,27},{11,3},{4,12},{... | collective-permute-start | bytes 196616 | tf_op jit(solution)/shard_map/ppermute | solution.py:691
  123.4 7.5 %collective-permute-start.18 = (bf16[2,1,128,128]{3,2,1,0:T(8,128)(2,1)S(1)}, bf16[2,1,128,128]{3,2,1,0:T(8,128)(2,1)S(1)}, u32[]{:S(2)}, u32[]{:S(2)}) collective-permute-start(bf16[2,1,128,128]{3,2,1,0:T(8,128)(2,1)S(1)} %get-tuple-element.42), channel_id=1, source_target_pairs={{8,24},{16,17},{25,9},{1,2},{10,26},{18,19},{27,11},{3,4},{12,28},... | collective-permute-start | bytes 196616 | tf_op jit(solution)/shard_map/ppermute | solution.py:692
  129.0 13.3 %collective-permute-start.24 = (bf16[2,6,128,128]{3,2,1,0:T(8,128)(2,1)S(1)}, bf16[2,6,128,128]{3,2,1,0:T(8,128)(2,1)S(1)}, u32[]{:S(2)}, u32[]{:S(2)}) collective-permute-start(bf16[2,6,128,128]{3,2,1,0:T(8,128)(2,1)S(1)} %collective-permute-done.23.refs_0_), channel_id=1, source_target_pairs={{0,16},{8,24},{16,0},{24,8},{1,17},{9,25},{17,1},{25,9},{2,18},{10... | collective-permute-start | bytes 1179656 | tf_op jit(solution)/shard_map/ppermute | solution.py:48
  132.5 4.2 %collective-permute-start.19 = (bf16[2,2,128,128]{3,2,1,0:T(8,128)(2,1)S(1)}, bf16[2,2,128,128]{3,2,1,0:T(8,128)(2,1)S(1)}, u32[]{:S(2)}, u32[]{:S(2)}) collective-permute-start(bf16[2,2,128,128]{3,2,1,0:T(8,128)(2,1)S(1)} %get-tuple-element.45), channel_id=1, source_target_pairs={{0,8},{8,0},{16,24},{24,16},{1,9},{9,1},{17,25},{25,17},{2,10},{10... | collective-permute-start | bytes 393224 | tf_op jit(solution)/shard_map/ppermute | solution.py:48
  136.7 4.8 %collective-permute-start.25 = (bf16[2,2,128,128]{3,2,1,0:T(8,128)(2,1)S(1)}, bf16[2,2,128,128]{3,2,1,0:T(8,128)(2,1)S(1)}, u32[]{:S(2)}, u32[]{:S(2)}) collective-permute-start(bf16[2,2,128,128]{3,2,1,0:T(8,128)(2,1)S(1)} %get-tuple-element.45), channel_id=1, source_target_pairs={{0,16},{8,24},{16,0},{24,8},{1,17},{9,25},{17,1},{25,9},{2,18},{10... | collective-permute-start | bytes 393224 | tf_op jit(solution)/shard_map/ppermute | solution.py:48
  137.0 7.2 %collective-permute-start.20 = (bf16[2,2,128,128]{3,2,1,0:T(8,128)(2,1)S(1)}, bf16[2,2,128,128]{3,2,1,0:T(8,128)(2,1)S(1)}, u32[]{:S(2)}, u32[]{:S(2)}) collective-permute-start(bf16[2,2,128,128]{3,2,1,0:T(8,128)(2,1)S(1)} %collective-permute-done.19.refs_0_), channel_id=1, source_target_pairs={{0,16},{8,24},{16,0},{24,8},{1,17},{9,25},{17,1},{25,9},{2,18},{10... | collective-permute-start | bytes 393224 | tf_op jit(solution)/shard_map/ppermute | solution.py:48
